TPU v7x, 32 devices: a whole 2x2x4 slice. The times are simulated.
32 devices in a mesh: grp: 2 (over y), train: 4 (over z), test: 2 (over x), proj: 2 (over core).
Axes of the slice: x: 2, y: 2, z: 4, core: 2. Of those that a mesh axis runs over, the one named last changes fastest.
Arguments:
- train_windows: bfloat16 [1024, 64, 512], P(('grp', 'test', 'train')), parts along dimension 0, may hold values from -6 to 6
- test_windows: bfloat16 [256, 64, 512], P(('grp', 'train', 'test')), parts along dimension 0, may hold values from -6 to 6
- train_labels: int32 [1024], P(('grp', 'test', 'train')), parts along dimension 0, may hold values from 0 to 7
- test_labels: int32 [256], P(('grp', 'train', 'test')), parts along dimension 0, may hold values from 0 to 7
- dilated_weight: bfloat16 [3, 512, 512], P(None, None, 'proj'), may hold values from -0.15625 to 0.15625
- branch_gain: float32 [512], P('proj'), may hold values from 0.25 to 1.75
- cls_weight: float32 [512, 8], P('proj'), may hold values from -0.75 to 0.75
- sign_seeds: int32 [4096], P('proj'), may hold values from 0 to 1073741823
- precond: float32 [2048], replicated, may hold values from 0.25 to 4
Outputs:
- scores: float32 [256, 512], P(('grp', 'train'), ('test', 'proj')), parts along dimension 0
There are 2 independent parts, one for each index of `grp`. A program takes and returns all parts, laid end to end along the dimension named above; an argument that names none is the same for every part. Nothing has to cross between parts.
All inputs are finite; a program needn't handle non-finite values.
Results may differ from a plain program's by a relative error of at most 0.00038.
Values may be sent and summed in bfloat16 or wider, within the bound.
No kernel may reach another device: no remote copies, remote signals or barrier semaphores. Data moves between devices by JAX's collectives and lax.ppermute only.
A program may use at most 64 MiB of HBM per device.

v0:
```python
import math

import jax
import jax.numpy as jnp
from jax import lax
from jax.sharding import PartitionSpec as P

C = 512
NCLS = 8
K = 2048
DILATION_STEP = 4


def sign_block(seed_rows, first_col, count):
    columns = jnp.arange(count, dtype=jnp.int32) + first_col
    mixed = seed_rows[:, None] ^ columns[None, :] * 668265261
    mixed = mixed * 625341585
    mixed = mixed ^ mixed >> 13
    mixed = mixed * 1274126177
    picked = mixed >> 16 & 1
    return (1 - 2 * picked).astype(jnp.bfloat16)


def pooled_rows(window_batch, dilated_weight, branch_gain, proj_index):
    sequence_length = window_batch.shape[1]
    half_width = dilated_weight.shape[2]
    zero_padded_input = jnp.pad(window_batch, ((0, 0), (DILATION_STEP, DILATION_STEP), (0, 0)))
    convolved_output = jnp.zeros((window_batch.shape[0], sequence_length, half_width), jnp.float32)
    for filter_tap_index in range(3):
        convolved_output = convolved_output + jnp.einsum(
            "rua,al->rul",
            zero_padded_input[
                :,
                filter_tap_index * DILATION_STEP : filter_tap_index * DILATION_STEP
                + sequence_length,
            ],
            dilated_weight[filter_tap_index],
            preferred_element_type=jnp.float32,
        )
    own_cols = lax.dynamic_slice_in_dim(
        window_batch, proj_index * half_width, half_width, 2
    ).astype(jnp.float32)
    return jnp.mean(own_cols + branch_gain * jax.nn.relu(convolved_output), axis=1)


def project_rows(pooled, logits, labels, seed_rows, first_col, count):
    chance = 1.0 / (1.0 + jnp.exp(-logits))
    target = (jnp.arange(NCLS, dtype=jnp.int32)[None, :] == labels[:, None]).astype(jnp.float32)
    residue = chance - target
    retain_weight = 1.0 - jnp.sum(chance * target, axis=1)
    window_count = pooled.shape[0]
    width = pooled.shape[1]
    gradient = (
        (pooled[:, :, None] * residue[:, None, :])
        .reshape(window_count, width * NCLS)
        .astype(jnp.bfloat16)
    )
    col_block = min(count, 1024)

    def project_block(block_index):
        return jnp.dot(
            gradient,
            sign_block(seed_rows, first_col + block_index * col_block, col_block),
            preferred_element_type=jnp.float32,
        )

    stacked = lax.map(project_block, jnp.arange(count // col_block, dtype=jnp.int32))
    return (jnp.moveaxis(stacked, 0, 1).reshape(window_count, count), retain_weight)


def shards(
    train_windows,
    test_windows,
    train_labels,
    test_labels,
    dilated_weight,
    branch_gain,
    cls_weight,
    sign_seeds,
    precond,
):
    proj_index = lax.axis_index("proj")
    train_count = train_windows.shape[0]
    pooled = jnp.concatenate(
        [
            pooled_rows(train_windows, dilated_weight, branch_gain, proj_index),
            pooled_rows(test_windows, dilated_weight, branch_gain, proj_index),
        ],
        axis=0,
    )
    labels = jnp.concatenate([train_labels, test_labels])
    score_scale = 1.0 / (K * math.sqrt(C))
    partial_value = jnp.dot(pooled, cls_weight, precision=lax.Precision.HIGHEST)
    logits = lax.psum(partial_value, "proj")
    proj_term, retain_weight = project_rows(pooled, logits, labels, sign_seeds, 0, K)
    features = lax.psum(proj_term, "proj")
    train_feat = (features[:train_count] * retain_weight[:train_count, None]).astype(jnp.bfloat16)
    test_feat = (features[train_count:] * precond[None, :]).astype(jnp.bfloat16)
    test_block = lax.all_gather(test_feat, "test", axis=0, tiled=True)
    all_cols = jnp.einsum(
        "ik,jk->ij",
        test_block,
        lax.all_gather(train_feat, "train", axis=0, tiled=True),
        preferred_element_type=jnp.float32,
    )
    out_width = all_cols.shape[1] // lax.axis_size("proj")
    scores = lax.dynamic_slice_in_dim(all_cols, proj_index * out_width, out_width, 1) * score_scale
    return scores


def solution(mesh):
    return jax.shard_map(
        shards,
        mesh=mesh,
        in_specs=(
            P(("grp", "test", "train"), None, None),
            P(("grp", "train", "test"), None, None),
            P(("grp", "test", "train")),
            P(("grp", "train", "test")),
            P(None, None, "proj"),
            P("proj"),
            P("proj", None),
            P("proj"),
            P(),
        ),
        out_specs=P(("grp", "train"), ("test", "proj")),
        check_vma=False,
    )
```

profile of v0, /device:TPU:0, one launch (start us, length us, event | category | flops | bytes accessed | tf_op | source)
XLA Modules:
  0.0 99.4 jit_solution(15685932726811911622)
XLA Ops:
  6.5 0.0 copy-start
  6.5 0.0 all-reduce.4.cloned.1.call-start
  6.5 0.0 copy-start.1
  6.5 0.0 copy-start.3
  6.5 5.6 %fusion.26 = f32[64,64,256]{2,1,0:T(8,128)} fusion(bf16[64,64,512]{2,1,0:T(8,128)(2,1)} %param.11, bf16[3,512,256]{2,1,0:T(8,128)(2,1)} %param.15), kind=kOutput, calls=%fused_computation.24 | convolution fusion | flops 1073741824 | bytes 8650752 | tf_op jit(solution)/shard_map/rua,al->rul/dot_general | solution.py:30
  12.1 0.0 copy-done.1
  12.1 0.0 copy-done.3
  12.1 0.0 copy-start.6
  12.1 3.2 %fusion.37 = f32[64,64,256]{2,1,0:T(8,128)} fusion(bf16[64,64,512]{2,1,0:T(8,128)(2,1)S(1)} %copy-done.1, bf16[3,512,256]{2,1,0:T(8,128)(2,1)S(1)} %copy-done.3), kind=kOutput, calls=%fused_computation.41 | convolution fusion | flops 1073741824 | bytes 8650752 | tf_op jit(solution)/shard_map/rua,al->rul/dot_general | solution.py:30
  15.4 0.0 copy-done.6
  15.4 0.0 copy-start.2
  15.4 7.6 %add_reduce_fusion = f32[64,256]{1,0:T(8,128)S(1)} fusion(f32[64,64,256]{2,1,0:T(8,128)} %fusion.26, f32[64,64,256]{2,1,0:T(8,128)} %fusion.37, bf16[64,64,512]{2,1,0:T(8,128)(2,1)} %param.11, f32[256]{0:T(256)S(1)} %copy-done.6, s32[]{:T(128)S(6)} %select_n.7, bf16[3,512,256]{2,1,0:T(8,128)(2,1)S(1)} %copy-done.3), kind=kOutput, calls=%fused_computation.26 | convolution fusion | flops 1081065472 | bytes 15008772 | tf_op jit(solution)/shard_map/rua,al->rul/dot_general | solution.py:30
  23.0 0.0 copy-done.2
  23.0 0.4 fusion.32
  23.5 0.0 copy-start.7
  23.5 0.0 copy-start.8
  23.5 0.0 copy-start.5
  23.5 0.4 convolution_add_fusion.1
  23.9 0.6 fusion.31
  24.6 0.0 copy-done
  24.6 0.2 fusion.52
  24.7 2.6 %psum.14 = f32[80,8]{0,1:T(8,128)S(1)} all-reduce(f32[80,8]{0,1:T(8,128)S(1)} %fusion.52), channel_id=1, replica_groups=mesh['grp'=2,'train'=4,'test'=2,'proj'=2] {'proj'}, use_global_device_ids=true, to_apply=%region_2.3 | all-reduce | flops 640 | bytes 5120 | tf_op jit(solution)/shard_map/psum | solution.py:94
  27.3 0.1 copy.12
  27.4 0.0 copy-done.7
  27.4 0.0 copy-done.8
  27.4 0.1 pad_add_fusion
  27.6 0.0 copy-done.5
  27.6 0.0 copy-start.4
  27.6 9.0 %while.11 = (s32[]{:T(128)}, f32[2,80,1024]{2,1,0:T(8,128)S(1)}, s32[2048]{0:T(1024)S(1)}, s32[2]{0:T(128)S(1)}, f32[80,8]{0,1:T(8,128)S(1)}, /*index=5*/f32[80,256]{0,1:T(8,128)S(1)}, s32[]{:T(128)}, s32[1]{0:T(128)}) while((s32[]{:T(128)}, f32[2,80,1024]{2,1,0:T(8,128)S(1)}, s32[2048]{0:T(1024)S(1)}, s32[2]{0:T(128)S(1)}, ...), condition=%wide.region_4.5_spmd.clone, body=%wide.region_3.4_spmd.clone.sunk | while | flops 356845568 | bytes 479349 | solution.py:67
  27.6 0.7 dynamic_slice.21
  28.9 3.2 %fusion.64 = f32[2,80,1024]{2,1,0:T(8,128)S(1)} fusion(f32[2,80,1024]{2,1,0:T(8,128)S(1)} %get-tuple-element.115, s32[]{:T(128)} %get-tuple-element.114, s32[1024]{0:T(1024)S(1)} %add_multiply_fusion.2, s32[2048]{0:T(1024)S(1)} %get-tuple-element.124, f32[80,8]{0,1:T(8,128)S(1)} %get-tuple-element.126, f32[80,256]{0,1:T(8,128)S(1)} %get-tuple-element.127), kind=kOutput, calls=%fused_computation.10.clone.1 | convolution fusion | flops 356843520 | bytes 475140 | tf_op jit(solution)/shard_map/while/body/eval_jaxpr/dot_general | solution.py:61
  32.1 0.7 dynamic_slice.21
  33.4 3.2 %fusion.64 = f32[2,80,1024]{2,1,0:T(8,128)S(1)} fusion(f32[2,80,1024]{2,1,0:T(8,128)S(1)} %get-tuple-element.115, s32[]{:T(128)} %get-tuple-element.114, s32[1024]{0:T(1024)S(1)} %add_multiply_fusion.2, s32[2048]{0:T(1024)S(1)} %get-tuple-element.124, f32[80,8]{0,1:T(8,128)S(1)} %get-tuple-element.126, f32[80,256]{0,1:T(8,128)S(1)} %get-tuple-element.127), kind=kOutput, calls=%fused_computation.10.clone.1 | convolution fusion | flops 356843520 | bytes 475140 | tf_op jit(solution)/shard_map/while/body/eval_jaxpr/dot_general | solution.py:61
  36.6 0.9 copy.14
  37.5 0.0 all-reduce.4.cloned.1.call-update
  37.5 0.0 all-gather.2.cloned.1.call-start
  37.6 21.6 %all-reduce.4.cloned.1.call-done = f32[80,2048]{1,0:T(8,128)} async-done(((f32[80,2048]{1,0:T(8,128)}), f32[80,2048]{1,0:T(8,128)}) %all-reduce.4.cloned.1.call-update) | async-done | bytes 655376 | tf_op jit(solution)/shard_map/psum | solution.py:96
  59.2 1.8 %fusion.33 = bf16[64,2048]{1,0:T(8,128)(2,1)} fusion(f32[80,2048]{1,0:T(8,128)} %all-reduce.4.cloned.1.call-done, f32[64]{0:T(128)S(1)} %bitcast.45), kind=kLoop, calls=%fused_computation.37 | loop fusion | flops 262144 | bytes 786688 | tf_op jit(solution)/shard_map/convert_element_type | solution.py:97
  61.0 0.0 all-gather.2.cloned.1.call-update
  61.1 0.0 copy-done.4
  61.1 0.9 fusion.47
  62.0 4.9 %all_gather.6 = bf16[32,2048]{1,0:T(8,128)(2,1)S(1)} all-gather(bf16[16,2048]{1,0:T(8,128)(2,1)S(1)} %fusion.47), channel_id=1, replica_groups=mesh['grp'=2,'train'=4,'test'=2,'proj'=2] {'test'}, dimensions={0}, use_global_device_ids=true | all-gather | bytes 196608 | tf_op jit(solution)/shard_map/all_gather | solution.py:99
  66.9 23.4 %all-gather.2.cloned.1.call-done = bf16[256,2048]{1,0:T(8,128)(2,1)} async-done(((bf16[64,2048]{1,0:T(8,128)(2,1)}), bf16[256,2048]{1,0:T(8,128)(2,1)}) %all-gather.2.cloned.1.call-update) | async-done | bytes 1048592 | tf_op jit(solution)/shard_map/all_gather | solution.py:103
  90.3 1.6 %fusion.53 = f32[32,256]{1,0:T(8,128)S(1)} fusion(bf16[32,2048]{1,0:T(8,128)(2,1)S(1)} %all_gather.6, bf16[256,2048]{1,0:T(8,128)(2,1)} %all-gather.2.cloned.1.call-done), kind=kOutput, calls=%fused_computation.68 | convolution fusion | flops 33554432 | bytes 1212416 | tf_op jit(solution)/shard_map/ik,jk->ij/dot_general | solution.py:100
  92.0 0.6 dynamic-slice_multiply_fusion
  (9 shorter events, 0.1 us)
Async XLA Ops:
  6.5 18.0 %copy-start = (f32[256,8]{0,1:T(8,128)S(1)}, f32[256,8]{0,1:T(8,128)}, u32[]{:S(2)}) copy-start(f32[256,8]{0,1:T(8,128)} %param.17) | copy-start | bytes 24580
  6.5 52.7 %all-reduce.4.cloned.1.call-start = ((), (), s32[]{:S(2)}) async-start(), calls=%async_computation | async-start | bytes 1310720 | tf_op jit(solution)/shard_map/psum | solution.py:96
  6.5 5.6 %copy-start.1 = (bf16[64,64,512]{2,1,0:T(8,128)(2,1)S(1)}, bf16[64,64,512]{2,1,0:T(8,128)(2,1)}, u32[]{:S(2)}) copy-start(bf16[64,64,512]{2,1,0:T(8,128)(2,1)} %param.11) | copy-start | bytes 12582916
  6.5 5.6 %copy-start.3 = (bf16[3,512,256]{2,1,0:T(8,128)(2,1)S(1)}, bf16[3,512,256]{2,1,0:T(8,128)(2,1)}, u32[]{:S(2)}) copy-start(bf16[3,512,256]{2,1,0:T(8,128)(2,1)} %param.15) | copy-start | bytes 2359300
  12.1 3.2 %copy-start.6 = (f32[256]{0:T(256)S(1)}, f32[256]{0:T(256)}, u32[]{:S(2)}) copy-start(f32[256]{0:T(256)} %param.16) | copy-start | bytes 3076
  15.4 7.6 %copy-start.2 = (bf16[16,64,512]{2,1,0:T(8,128)(2,1)S(1)}, bf16[16,64,512]{2,1,0:T(8,128)(2,1)}, u32[]{:S(2)}) copy-start(bf16[16,64,512]{2,1,0:T(8,128)(2,1)} %param.12) | copy-start | bytes 3145732
  23.5 4.0 %copy-start.7 = (s32[16]{0:T(128)S(1)}, s32[16]{0:T(128)}, u32[]{:S(2)}) copy-start(s32[16]{0:T(128)} %param.14) | copy-start | bytes 196
  23.5 4.0 %copy-start.8 = (s32[64]{0:T(128)S(1)}, s32[64]{0:T(128)}, u32[]{:S(2)}) copy-start(s32[64]{0:T(128)} %param.13) | copy-start | bytes 772
  23.5 4.1 %copy-start.5 = (s32[2048]{0:T(1024)S(1)}, s32[2048]{0:T(1024)}, u32[]{:S(2)}) copy-start(s32[2048]{0:T(1024)} %param.18) | copy-start | bytes 24580
  27.6 33.5 %copy-start.4 = (f32[2048]{0:T(1024)S(1)}, f32[2048]{0:T(1024)}, u32[]{:S(2)}) copy-start(f32[2048]{0:T(1024)} %param.19) | copy-start | bytes 24580
  37.5 52.8 %all-gather.2.cloned.1.call-start = ((), (), s32[]{:S(2)}) async-start(), calls=%async_computation.1 | async-start | bytes 1310720 | tf_op jit(solution)/shard_map/all_gather | solution.py:103
Sparse Core Ops, SparseCore 0:
  37.6 21.5 all-reduce.3
  61.2 29.1 all-gather.1
where the time goes:
time: 99.7 us; the launch traced here: 99.4 us
  waiting for transfers between devices  45 us (45%)
  matrix products  26.1 us (26%)
  between operations  13.6 us (14%)
  blocking collectives  7.54 us (8%)
  other arithmetic  3.51 us (4%)
  local copies, waits for them, and re-layouts  2.32 us (2%)
  loops' own time  1.31 us (1%)
    all_gather x1, waiting for transfers between devices, shards(): lax.all_gather(train_feat, 'train', axis=0, tiled=True)  23.4 us
    psum x1, waiting for transfers between devices, shards(): features = lax.psum(proj_term, 'proj')  21.6 us
    dot_general x6, matrix products, pooled_rows(): jnp.einsum('rua,al->rul', zero_padded_input[:, filter_tap_index * DILATIO...  17.9 us
    dot_general x2, matrix products, project_block(): jnp.dot(gradient, sign_block(seed_rows, first_col + block_index * col_blo...  6.41 us
    all_gather x1, blocking collectives, shards(): test_block = lax.all_gather(test_feat, 'test', axis=0, tiled=True)  4.94 us
    psum x1, blocking collectives, shards(): logits = lax.psum(partial_value, 'proj')  2.6 us
  transfers between devices with their start and end apart: 2, of which 2 were waited for; matrix products, arithmetic and copies ran while one was open for 1% of the time, Pallas kernels for 0%

commit v1 on v0

v1 whole, which is shorter than its diff:
```python
import functools
import math

import jax
import jax.numpy as jnp
from jax import lax
from jax.experimental import pallas as pl
from jax.experimental.pallas import tpu as pltpu
from jax.sharding import PartitionSpec as P

C = 512
NCLS = 8
K = 2048
DILATION_STEP = 4
MIX_COLUMN = 668265261
MIX_FIRST = 625341585
MIX_LAST = (1274126177 << 15) & 0xFFFFFFFF
MIX_LAST = MIX_LAST - (1 << 32) if MIX_LAST >= 1 << 31 else MIX_LAST
MIB = 2**20

VMEM = pl.BlockSpec(memory_space=pltpu.VMEM)
HBM = pl.BlockSpec(memory_space=pltpu.HBM)


def pool_kernel(
    block,
    train_hbm,
    test_hbm,
    weight_hbm,
    gain_ref,
    cls_ref,
    train_label_ref,
    test_label_ref,
    train_packet,
    test_packet,
    rows,
    weight,
    pooled,
    row_sem,
    weight_sem,
):
    proj_index = lax.axis_index("proj")
    train_count, length, width = train_hbm.shape
    test_count = test_hbm.shape[0]
    half = weight.shape[2]
    blocks = (train_count + test_count) // block
    weight_copy = pltpu.make_async_copy(weight_hbm, weight, weight_sem)
    weight_copy.start()
    for b in range(blocks):
        source = train_hbm if b < train_count // block else test_hbm
        offset = b * block if b < train_count // block else b * block - train_count
        pltpu.make_async_copy(
            source.at[pl.ds(offset, block)], rows.at[pl.ds(b * block, block)], row_sem.at[b]
        ).start()
    weight_copy.wait()
    gain = gain_ref[...]
    own_start = pl.multiple_of(proj_index * half, half)

    def one_block(b, carry):
        start = b * block
        pltpu.make_async_copy(
            test_hbm.at[pl.ds(0, block)], rows.at[pl.ds(start, block)], row_sem.at[b]
        ).wait()
        x = rows[pl.ds(start, block)]
        zeros = jnp.zeros((block, DILATION_STEP, width), x.dtype)
        before = jnp.concatenate([zeros, x[:, : length - DILATION_STEP]], axis=1)
        after = jnp.concatenate([x[:, DILATION_STEP:], zeros], axis=1)
        taps = jnp.concatenate([before, x, after], axis=2).reshape(block * length, 3 * width)
        conv = jnp.dot(
            taps, weight[...].reshape(3 * width, half), preferred_element_type=jnp.float32
        ).reshape(block, length, half)
        own = rows[pl.ds(start, block), :, pl.ds(own_start, half)].astype(jnp.float32)
        total = jnp.sum(own, axis=1) + gain * jnp.sum(jnp.maximum(conv, 0.0), axis=1)
        pooled[pl.ds(pl.multiple_of(start, block), block), :] = total * (1.0 / length)
        return carry

    lax.fori_loop(0, blocks, one_block, 0)
    for packet, label_ref, start, count in (
        (train_packet, train_label_ref, 0, train_count),
        (test_packet, test_label_ref, train_count, test_count),
    ):
        own = pooled[pl.ds(start, count), :]
        packet[pl.ds(0, count), :] = own
        packet[pl.ds(count, NCLS), pl.ds(0, count)] = lax.dot_general(
            cls_ref[...],
            own,
            (((1,), (1,)), ((), ())),
            precision=lax.Precision.HIGHEST,
            preferred_element_type=jnp.float32,
        )
        packet[pl.ds(count, NCLS), pl.ds(128, count)] = jnp.broadcast_to(
            label_ref[...].astype(jnp.float32), (NCLS, count)
        )


def pool(train_windows, test_windows, weight, gain, cls_t, train_labels, test_labels):
    block = 8
    train_count, length, width = train_windows.shape
    test_count = test_windows.shape[0]
    half = weight.shape[2]
    total = train_count + test_count
    return pl.pallas_call(
        functools.partial(pool_kernel, block),
        out_shape=(
            jax.ShapeDtypeStruct((train_count + NCLS, half), jnp.float32),
            jax.ShapeDtypeStruct((test_count + NCLS, half), jnp.float32),
        ),
        in_specs=[HBM, HBM, HBM, VMEM, VMEM, VMEM, VMEM],
        out_specs=(VMEM, VMEM),
        scratch_shapes=[
            pltpu.VMEM((total, length, width), jnp.bfloat16),
            pltpu.VMEM(weight.shape, jnp.bfloat16),
            pltpu.VMEM((total, half), jnp.float32),
            pltpu.SemaphoreType.DMA((total // block,)),
            pltpu.SemaphoreType.DMA,
        ],
        compiler_params=pltpu.CompilerParams(vmem_limit_bytes=24 * MIB),
        name="pool",
    )(train_windows, test_windows, weight, gain, cls_t, train_labels, test_labels)


def sign_kernel(seed_ref, sign_ref, turned):
    proj_index = lax.axis_index("proj")
    parts, rows, part_width = sign_ref.shape
    count = parts * part_width
    chunks = rows // 128
    per_chunk = 128 // NCLS
    turned[:, pl.ds(0, chunks)] = seed_ref[...].T
    columns = (
        lax.broadcasted_iota(jnp.int32, (per_chunk, count), 1) + proj_index * count
    ) * MIX_COLUMN
    for k in range(NCLS):
        seeds = turned[pl.ds(k, per_chunk, stride=NCLS), :]
        for h in range(chunks):
            mixed = (seeds[:, h : h + 1] ^ columns) * MIX_FIRST
            mixed = (mixed ^ (mixed >> 13)) * MIX_LAST
            signs = jnp.where(mixed < 0, -1.0, 1.0).astype(jnp.bfloat16)
            at = (k * chunks + h) * per_chunk
            for n in range(parts):
                sign_ref[n, pl.ds(at, per_chunk), :] = signs[:, n * part_width : (n + 1) * part_width]


def sign_block(seeds, count):
    rows = seeds.shape[0]
    parts = count // 256
    return pl.pallas_call(
        sign_kernel,
        out_shape=jax.ShapeDtypeStruct((parts, rows, 256), jnp.bfloat16),
        in_specs=[VMEM],
        out_specs=VMEM,
        scratch_shapes=[pltpu.VMEM((128, 128), jnp.int32)],
        compiler_params=pltpu.CompilerParams(vmem_limit_bytes=16 * MIB),
        cost_estimate=pl.CostEstimate(flops=8 * rows * count, bytes_accessed=2 * rows * count, transcendentals=0),
        name="signs",
    )(seeds.reshape(rows // 128, 128))


def score_kernel(train_blocks, test_blocks, train_count, test_count, *refs):
    packets = refs[: 2 * (train_blocks + test_blocks)]
    own_signs, other_signs, precond_ref, keep_ref, send_ref, grad, row_weight, total = refs[
        2 * (train_blocks + test_blocks) :
    ]
    step = pl.program_id(0)
    proj_index = lax.axis_index("proj")
    half = packets[0].shape[1]
    part_width = own_signs.shape[2]
    train_rows = train_blocks * train_count
    half_rows = NCLS * half

    @pl.when(step == 0)
    def _():
        total[...] = jnp.zeros_like(total)
        for i in range(train_blocks + test_blocks):
            mine, theirs = packets[2 * i], packets[2 * i + 1]
            if i < train_blocks:
                count = train_count
                at = _source(lax.axis_index("train"), i, train_blocks) * count
            else:
                count = test_count
                at = train_rows + _source(
                    lax.axis_index("test"), i - train_blocks, test_blocks
                ) * count
            at = pl.multiple_of(at, count)
            logits = mine[pl.ds(count, NCLS), pl.ds(0, 128)] + theirs[pl.ds(count, NCLS), pl.ds(0, 128)]
            label = mine[pl.ds(count, NCLS), pl.ds(128, 128)]
            chance = 1.0 / (1.0 + jnp.exp(-logits))
            classes = lax.broadcasted_iota(jnp.int32, (NCLS, 128), 0).astype(jnp.float32)
            target = jnp.where(label == classes, 1.0, 0.0)
            retain = 1.0 - jnp.sum(chance * target, axis=0, keepdims=True)
            stacked = jnp.concatenate(
                [chance - target, jnp.broadcast_to(retain, (NCLS, 128))], axis=0
            )
            turned = stacked.T[:count]
            if i < train_blocks:
                row_weight[pl.ds(at, count), :] = jnp.broadcast_to(turned[:, NCLS : NCLS + 1], (count, 128))
            for side, packet in enumerate((mine, theirs)):
                value = packet[pl.ds(0, count), :]
                for k in range(NCLS):
                    grad[pl.ds(at, count), pl.ds(side * half_rows + k * half, half)] = (
                        value * turned[:, k : k + 1]
                    ).astype(jnp.bfloat16)

    projected = jnp.dot(
        grad[:, pl.ds(0, half_rows)], own_signs[0], preferred_element_type=jnp.float32
    ) + jnp.dot(
        grad[:, pl.ds(half_rows, half_rows)], other_signs[0], preferred_element_type=jnp.float32
    )
    weight = row_weight[...]
    train_feat = (
        projected[:train_rows] * jnp.concatenate([weight] * (part_width // 128), axis=1)
    ).astype(jnp.bfloat16)
    test_feat = (projected[train_rows:] * precond_ref[...]).astype(jnp.bfloat16)
    total[...] += lax.dot_general(
        test_feat,
        train_feat,
        (((1,), (1,)), ((), ())),
        preferred_element_type=jnp.float32,
    )

    @pl.when(step == pl.num_programs(0) - 1)
    def _():
        out_width = keep_ref.shape[1]
        keep_ref[...] = total[:, pl.ds(pl.multiple_of(proj_index * out_width, 128), out_width)]
        send_ref[...] = total[:, pl.ds(pl.multiple_of((1 - proj_index) * out_width, 128), out_width)]


def _source(index, shift, count):
    if count & (count - 1) == 0:
        return index ^ shift
    return lax.rem(index + count - shift, count)


def _pairs(shift, count):
    if count & (count - 1) == 0:
        return [(i, i ^ shift) for i in range(count)]
    return [(i, (i + shift) % count) for i in range(count)]


def partial_scores(packets, own_signs, other_signs, precond, train_blocks, test_blocks, train_count, test_count):
    parts, rows, part_width = own_signs.shape
    total_rows = train_blocks * train_count + test_blocks * test_count
    out_rows = test_blocks * test_count
    out_cols = train_blocks * train_count
    sign_spec = pl.BlockSpec((1, rows, part_width), lambda n: (n, 0, 0))
    packet_specs = [pl.BlockSpec(v.shape, lambda n: (0, 0)) for v in packets]
    out_spec = pl.BlockSpec((out_rows, out_cols // 2), lambda n: (0, 0))
    return pl.pallas_call(
        functools.partial(score_kernel, train_blocks, test_blocks, train_count, test_count),
        grid=(parts,),
        out_shape=(jax.ShapeDtypeStruct((out_rows, out_cols // 2), jnp.float32),) * 2,
        in_specs=packet_specs
        + [
            sign_spec,
            sign_spec,
            pl.BlockSpec(
                (1, part_width), lambda n: (0, lax.axis_index("proj") * parts + n)
            ),
        ],
        out_specs=(out_spec, out_spec),
        scratch_shapes=[
            pltpu.VMEM((total_rows, 2 * rows), jnp.bfloat16),
            pltpu.VMEM((out_cols, 128), jnp.float32),
            pltpu.VMEM((out_rows, out_cols), jnp.float32),
        ],
        compiler_params=pltpu.CompilerParams(vmem_limit_bytes=40 * MIB),
        name="partial_scores",
    )(*packets, own_signs, other_signs, precond)


def shards(
    train_windows,
    test_windows,
    train_labels,
    test_labels,
    dilated_weight,
    branch_gain,
    cls_weight,
    sign_seeds,
    precond,
):
    train_count = train_windows.shape[0]
    test_count = test_windows.shape[0]
    train_blocks = lax.axis_size("train")
    test_blocks = lax.axis_size("test")
    count = K // lax.axis_size("proj")
    swap = [(0, 1), (1, 0)]
    other_seeds = lax.ppermute(sign_seeds, "proj", swap)
    train_packet, test_packet = pool(
        train_windows,
        test_windows,
        dilated_weight,
        branch_gain.reshape(1, -1),
        cls_weight.T,
        train_labels.reshape(1, -1),
        test_labels.reshape(1, -1),
    )
    mine = [train_packet]
    for shift in range(1, train_blocks):
        mine.append(lax.ppermute(train_packet, "train", _pairs(shift, train_blocks)))
    mine.append(test_packet)
    for shift in range(1, test_blocks):
        mine.append(lax.ppermute(test_packet, "test", _pairs(shift, test_blocks)))
    own_signs = sign_block(sign_seeds, count)
    other_signs = sign_block(other_seeds, count)
    packets = []
    for value in mine:
        packets += [value, lax.ppermute(value, "proj", swap)]
    keep, send = partial_scores(
        packets,
        own_signs,
        other_signs,
        precond.reshape(1, -1),
        train_blocks,
        test_blocks,
        train_count,
        test_count,
    )
    received = lax.ppermute(send, "proj", swap)
    return (keep + received) * (1.0 / (K * math.sqrt(C)))


def solution(mesh):
    return jax.shard_map(
        shards,
        mesh=mesh,
        in_specs=(
            P(("grp", "test", "train"), None, None),
            P(("grp", "train", "test"), None, None),
            P(("grp", "test", "train")),
            P(("grp", "train", "test")),
            P(None, None, "proj"),
            P("proj"),
            P("proj", None),
            P("proj"),
            P(),
        ),
        out_specs=P(("grp", "train"), ("test", "proj")),
        check_vma=False,
    )
```

time: 99.7 us -> 39.2 us (0.39)
  waiting for transfers between devices: 45 us -> 5.64 us
  matrix products: 26.1 us -> 0 us
  Pallas kernels: 0 us -> 16.4 us
  between operations: 13.6 us -> 0.1 us
  starting transfers between devices: 0.04 us -> 8.82 us
  blocking collectives: 7.54 us -> 0 us
  local copies, waits for them, and re-layouts: 2.32 us -> 7.24 us
  other arithmetic: 3.51 us -> 0.61 us
  loops' own time: 1.31 us -> 0 us
    dot_general x10 -> x0, matrix products: 26.1 us -> none  [the longest x6 17.9 us: pooled_rows(): jnp.einsum('rua,al->rul', zero_padded_input[:, filter_tap_index * DILATIO...]
    all_gather x1 -> x0, waiting for transfers between devices: 23.4 us -> none  [shards(): lax.all_gather(train_feat, 'train', axis=0, tiled=True)]
    psum x1 -> x0, waiting for transfers between devices: 21.6 us -> none  [shards(): features = lax.psum(proj_term, 'proj')]
    pallas_call x0 -> x4, Pallas kernels: none -> 16.4 us  [the longest x1 6.6 us: pool(): pl.pallas_call(functools.partial(pool_kernel, block), out_shape=(jax.Shap...]
    ppermute x0 -> x12, starting transfers between devices: none -> 8.82 us  [the longest x3 5.75 us: shards(): lax.ppermute(train_packet, 'train', _pairs(shift, train_blocks))]
    unnamed x19 -> x18, local copies, waits for them, and re-layouts: 0.13 us -> 7.24 us
    ppermute x0 -> x12, waiting for transfers between devices: none -> 5.64 us  [the longest x3 3.65 us: shards(): lax.ppermute(train_packet, 'train', _pairs(shift, train_blocks))]
    all_gather x1 -> x0, blocking collectives: 4.94 us -> none  [shards(): test_block = lax.all_gather(test_feat, 'test', axis=0, tiled=True)]
  transfers between devices with their start and end apart: 2 -> 12, of which waited for: 2 -> 4; matrix products, arithmetic and copies ran while one was open for 1% -> 0% of each run, Pallas kernels for 0% -> 13%
where the time goes in v1:
time: 39.2 us; the launch traced here: 38.9 us
  Pallas kernels  16.4 us (42%)
  starting transfers between devices  8.82 us (22%)
  local copies, waits for them, and re-layouts  7.24 us (18%)
  waiting for transfers between devices  5.64 us (14%)
  other arithmetic  0.61 us (2%)
    unnamed x18, local copies, waits for them, and re-layouts  7.24 us
    pallas_call x1, Pallas kernels, pool(): pl.pallas_call(functools.partial(pool_kernel, block), out_shape=(jax.Shap...  6.6 us
    ppermute x3, starting transfers between devices, shards(): lax.ppermute(train_packet, 'train', _pairs(shift, train_blocks))  5.75 us
    pallas_call x2, Pallas kernels, sign_block(): pl.pallas_call(sign_kernel, out_shape=jax.ShapeDtypeStruct((parts, rows,...  5.17 us
    pallas_call x1, Pallas kernels, partial_scores(): pl.pallas_call(functools.partial(score_kernel, train_blocks, test_blocks,...  4.69 us
    ppermute x3, waiting for transfers between devices, shards(): lax.ppermute(train_packet, 'train', _pairs(shift, train_blocks))  3.65 us
    ppermute x1, starting transfers between devices, shards(): mine.append(lax.ppermute(test_packet, 'test', _pairs(shift, test_blocks)))  1.64 us
    ppermute x6, waiting for transfers between devices, shards(): packets += [value, lax.ppermute(value, 'proj', swap)]  1.14 us
  transfers between devices with their start and end apart: 12, of which 4 were waited for; matrix products, arithmetic and copies ran while one was open for 0% of the time, Pallas kernels for 13%

profile of v1, /device:TPU:0, one launch (start us, length us, event | category | flops | bytes accessed | tf_op | source)
XLA Modules:
  0.0 38.9 jit_solution(9452608935014816696)
XLA Ops:
  0.0 0.0 copy-start
  0.0 2.2 %copy-done = bf16[64,64,512]{2,1,0:T(8,128)(2,1)S(1)} copy-done((bf16[64,64,512]{2,1,0:T(8,128)(2,1)S(1)}, bf16[64,64,512]{2,1,0:T(8,128)(2,1)}, u32[]{:S(2)}) %copy-start) | copy-done | bytes 4194328
  2.2 0.0 copy-start.1
  2.2 1.2 %copy-done.1 = bf16[16,64,512]{2,1,0:T(8,128)(2,1)S(1)} copy-done((bf16[16,64,512]{2,1,0:T(8,128)(2,1)S(1)}, bf16[16,64,512]{2,1,0:T(8,128)(2,1)}, u32[]{:S(2)}) %copy-start.1) | copy-done | bytes 1048600
  3.4 0.0 copy-start.2
  3.4 1.1 %copy-done.2 = bf16[3,512,256]{2,1,0:T(8,128)(2,1)S(1)} copy-done((bf16[3,512,256]{2,1,0:T(8,128)(2,1)S(1)}, bf16[3,512,256]{2,1,0:T(8,128)(2,1)}, u32[]{:S(2)}) %copy-start.2) | copy-done | bytes 786456
  4.5 0.0 copy-start.3
  4.5 0.7 %copy-done.3 = f32[256,8]{0,1:T(8,128)S(1)} copy-done((f32[256,8]{0,1:T(8,128)S(1)}, f32[256,8]{0,1:T(8,128)}, u32[]{:S(2)}) %copy-start.3) | copy-done | bytes 8216
  5.2 0.0 copy-start.6
  5.2 0.7 %copy-done.6 = f32[256]{0:T(256)S(1)} copy-done((f32[256]{0:T(256)S(1)}, f32[256]{0:T(256)}, u32[]{:S(2)}) %copy-start.6) | copy-done | bytes 1048
  5.9 0.0 copy-start.7
  5.9 0.7 %copy-done.7 = s32[64]{0:T(128)S(1)} copy-done((s32[64]{0:T(128)S(1)}, s32[64]{0:T(128)}, u32[]{:S(2)}) %copy-start.7) | copy-done | bytes 280
  6.6 0.0 copy-start.8
  6.6 0.7 %copy-done.8 = s32[16]{0:T(128)S(1)} copy-done((s32[16]{0:T(128)S(1)}, s32[16]{0:T(128)}, u32[]{:S(2)}) %copy-start.8) | copy-done | bytes 88
  7.2 0.0 copy-start.4
  7.2 6.6 %pool.1 = (f32[72,256]{1,0:T(8,128)S(1)}, f32[24,256]{1,0:T(8,128)S(1)}) custom-call(bf16[64,64,512]{2,1,0:T(8,128)(2,1)S(1)} %copy-done, bf16[16,64,512]{2,1,0:T(8,128)(2,1)S(1)} %copy-done.1, bf16[3,512,256]{2,1,0:T(8,128)(2,1)S(1)} %copy-done.2, f32[1,256]{1,0:T(1,128)S(1)} %bitcast.11, f32[8,256]{1,0:T(8,128)S(1)} %bitcast.7, s32[1,64]{1,0:T(1,128)S(1)} %bitcast.12, ...), custom_call_target="tpu_custom_call" | custom-call | tf_op jit(solution)/shard_map/pool/pallas_call | solution.py:102
  13.8 5.1 %collective-permute-start.5 = (f32[72,256]{1,0:T(8,128)S(1)}, f32[72,256]{1,0:T(8,128)S(1)}, u32[]{:S(2)}, u32[]{:S(2)}) collective-permute-start(f32[72,256]{1,0:T(8,128)S(1)} %get-tuple-element.9.refs_0_), channel_id=1, source_target_pairs={{0,12},{4,8},{8,4},{12,0},{1,13},{5,9},{9,5},{13,1},{2,14},{6,10},... | collective-permute-start | bytes 221192 | tf_op jit(solution)/shard_map/ppermute | solution.py:299
  19.0 0.0 collective-permute-start.3
  19.0 0.6 %collective-permute-start.1 = (f32[72,256]{1,0:T(8,128)S(1)}, f32[72,256]{1,0:T(8,128)S(1)}, u32[]{:S(2)}, u32[]{:S(2)}) collective-permute-start(f32[72,256]{1,0:T(8,128)S(1)} %get-tuple-element.9.refs_0_), channel_id=1, source_target_pairs={{0,4},{4,0},{8,12},{12,8},{1,5},{5,1},{9,13},{13,9},{2,6},{6,2},{1... | collective-permute-start | bytes 221192 | tf_op jit(solution)/shard_map/ppermute | solution.py:299
  19.6 0.0 copy-done.4
  19.6 0.0 collective-permute-start.10
  19.6 1.6 %collective-permute-start.8 = (f32[24,256]{1,0:T(8,128)S(1)}, f32[24,256]{1,0:T(8,128)S(1)}, u32[]{:S(2)}, u32[]{:S(2)}) collective-permute-start(f32[24,256]{1,0:T(8,128)S(1)} %get-tuple-element.10.refs_8_), channel_id=1, source_target_pairs={{0,2},{2,0},{1,3},{3,1},{4,6},{6,4},{5,7},{7,5},{8,10},{10,8},{9,1... | collective-permute-start | bytes 73736 | tf_op jit(solution)/shard_map/ppermute | solution.py:302
  21.2 0.0 collective-permute-done.10
  21.2 0.2 collective-permute-start
  21.5 0.2 collective-permute-done.5.refs_6_
  21.7 0.0 collective-permute-start.6
  21.8 3.4 %collective-permute-done.3.refs_4_ = f32[72,256]{1,0:T(8,128)S(1)} collective-permute-done((f32[72,256]{1,0:T(8,128)S(1)}, f32[72,256]{1,0:T(8,128)S(1)}, u32[]{:S(2)}, u32[]{:S(2)}) %collective-permute-start.3) | collective-permute-done | bytes 73760 | tf_op jit(solution)/shard_map/ppermute | solution.py:299
  25.2 0.0 collective-permute-start.4
  25.2 0.0 collective-permute-done.1.refs_2_
  25.2 0.5 %collective-permute-start.2 = (f32[72,256]{1,0:T(8,128)S(1)}, f32[72,256]{1,0:T(8,128)S(1)}, u32[]{:S(2)}, u32[]{:S(2)}) collective-permute-start(f32[72,256]{1,0:T(8,128)S(1)} %collective-permute-done.1.refs_2_), channel_id=1, source_target_pairs={{0,1},{1,0},{2,3},{3,2},{4,5},{5,4},{6,7},{7,6},{8,9},{9,8},{10,11... | collective-permute-start | bytes 221192 | tf_op jit(solution)/shard_map/ppermute | solution.py:307
  25.7 0.0 collective-permute-done.8.refs_10_
  25.7 0.1 collective-permute-start.7
  25.8 1.1 %collective-permute-done.7.refs_9_ = f32[24,256]{1,0:T(8,128)S(1)} collective-permute-done((f32[24,256]{1,0:T(8,128)S(1)}, f32[24,256]{1,0:T(8,128)S(1)}, u32[]{:S(2)}, u32[]{:S(2)}) %collective-permute-start.7) | collective-permute-done | bytes 24608 | tf_op jit(solution)/shard_map/ppermute | solution.py:307
  26.9 0.2 collective-permute-start.9
  27.1 0.0 copy-start.5
  27.1 2.6 %signs.2.refs_12_ = bf16[4,2048,256]{2,1,0:T(8,128)(2,1)S(1)} custom-call(s32[16,128]{1,0:T(8,128)S(1)} %bitcast.8), custom_call_target="tpu_custom_call" | custom-call | flops 16777216 | bytes 4194304 | tf_op jit(solution)/shard_map/signs/pallas_call | solution.py:146
  29.6 2.6 %signs.3.refs_13_ = bf16[4,2048,256]{2,1,0:T(8,128)(2,1)S(1)} custom-call(s32[16,128]{1,0:T(8,128)S(1)} %bitcast.9), custom_call_target="tpu_custom_call" | custom-call | flops 16777216 | bytes 4194304 | tf_op jit(solution)/shard_map/signs/pallas_call | solution.py:146
  32.2 0.0 collective-permute-done.9.refs_11_
  32.2 0.0 collective-permute-done.refs_1_
  32.3 0.0 collective-permute-done.6.refs_7_
  32.3 0.0 collective-permute-done.4.refs_5_
  32.3 0.0 collective-permute-done.2.refs_3_
  32.3 0.0 copy-done.5
  32.3 4.7 %partial_scores.1 = (f32[32,128]{1,0:T(8,128)S(1)}, f32[32,128]{1,0:T(8,128)S(1)}) custom-call(f32[72,256]{1,0:T(8,128)S(1)} %get-tuple-element.9.refs_0_, f32[72,256]{1,0:T(8,128)S(1)} %collective-permute-done.refs_1_, f32[72,256]{1,0:T(8,128)S(1)} %collective-permute-done.1.refs_2_, f32[72,256]{1,0:T(8,128)S(1)} %collective-permute-done.2.refs_3_, ...), custom_call_target="tpu_custom_call" | custom-call | tf_op jit(solution)/shard_map/partial_scores/pallas_call | solution.py:247
  37.0 0.4 %collective-permute-start.11 = (f32[32,128]{1,0:T(8,128)S(1)}, f32[32,128]{1,0:T(8,128)S(1)}, u32[]{:S(2)}, u32[]{:S(2)}) collective-permute-start(f32[32,128]{1,0:T(8,128)S(1)} %get-tuple-element.12), channel_id=1, source_target_pairs={{0,1},{1,0},{2,3},{3,2},{4,5},{5,4},{6,7},{7,6},{8,9},{9,8},{10,11... | collective-permute-start | bytes 49160 | tf_op jit(solution)/shard_map/ppermute | solution.py:318
  37.4 0.8 %collective-permute-done.11 = f32[32,128]{1,0:T(8,128)S(1)} collective-permute-done((f32[32,128]{1,0:T(8,128)S(1)}, f32[32,128]{1,0:T(8,128)S(1)}, u32[]{:S(2)}, u32[]{:S(2)}) %collective-permute-start.11) | collective-permute-done | bytes 16416 | tf_op jit(solution)/shard_map/ppermute | solution.py:318
  38.2 0.6 %add_multiply_fusion = f32[32,128]{1,0:T(8,128)} fusion(f32[32,128]{1,0:T(8,128)S(1)} %get-tuple-element.11, f32[32,128]{1,0:T(8,128)S(1)} %collective-permute-done.11), kind=kLoop, calls=%fused_computation | loop fusion | flops 8192 | bytes 49152 | tf_op jit(solution)/shard_map/mul | solution.py:319
Async XLA Ops:
  0.0 2.2 %copy-start = (bf16[64,64,512]{2,1,0:T(8,128)(2,1)S(1)}, bf16[64,64,512]{2,1,0:T(8,128)(2,1)}, u32[]{:S(2)}) copy-start(bf16[64,64,512]{2,1,0:T(8,128)(2,1)} %train_hbm.1) | copy-start | bytes 12582916
  2.2 1.2 %copy-start.1 = (bf16[16,64,512]{2,1,0:T(8,128)(2,1)S(1)}, bf16[16,64,512]{2,1,0:T(8,128)(2,1)}, u32[]{:S(2)}) copy-start(bf16[16,64,512]{2,1,0:T(8,128)(2,1)} %test_hbm.1) | copy-start | bytes 3145732
  3.4 1.1 %copy-start.2 = (bf16[3,512,256]{2,1,0:T(8,128)(2,1)S(1)}, bf16[3,512,256]{2,1,0:T(8,128)(2,1)}, u32[]{:S(2)}) copy-start(bf16[3,512,256]{2,1,0:T(8,128)(2,1)} %weight_hbm.1) | copy-start | bytes 2359300
  4.5 0.7 %copy-start.3 = (f32[256,8]{0,1:T(8,128)S(1)}, f32[256,8]{0,1:T(8,128)}, u32[]{:S(2)}) copy-start(f32[256,8]{0,1:T(8,128)} %param.15) | copy-start | bytes 24580
  5.2 0.7 %copy-start.6 = (f32[256]{0:T(256)S(1)}, f32[256]{0:T(256)}, u32[]{:S(2)}) copy-start(f32[256]{0:T(256)} %param.14) | copy-start | bytes 3076
  5.9 0.7 %copy-start.7 = (s32[64]{0:T(128)S(1)}, s32[64]{0:T(128)}, u32[]{:S(2)}) copy-start(s32[64]{0:T(128)} %param.11) | copy-start | bytes 772
  6.6 0.7 %copy-start.8 = (s32[16]{0:T(128)S(1)}, s32[16]{0:T(128)}, u32[]{:S(2)}) copy-start(s32[16]{0:T(128)} %param.12) | copy-start | bytes 196
  7.2 12.4 %copy-start.4 = (s32[2048]{0:T(1024)S(1)}, s32[2048]{0:T(1024)}, u32[]{:S(2)}) copy-start(s32[2048]{0:T(1024)} %param.16) | copy-start | bytes 24580
  13.8 7.9 %collective-permute-start.5 = (f32[72,256]{1,0:T(8,128)S(1)}, f32[72,256]{1,0:T(8,128)S(1)}, u32[]{:S(2)}, u32[]{:S(2)}) collective-permute-start(f32[72,256]{1,0:T(8,128)S(1)} %get-tuple-element.9.refs_0_), channel_id=1, source_target_pairs={{0,12},{4,8},{8,4},{12,0},{1,13},{5,9},{9,5},{13,1},{2,14},{6,10},... | collective-permute-start | bytes 221192 | tf_op jit(solution)/shard_map/ppermute | solution.py:299
  19.0 6.2 %collective-permute-start.3 = (f32[72,256]{1,0:T(8,128)S(1)}, f32[72,256]{1,0:T(8,128)S(1)}, u32[]{:S(2)}, u32[]{:S(2)}) collective-permute-start(f32[72,256]{1,0:T(8,128)S(1)} %get-tuple-element.9.refs_0_), channel_id=1, source_target_pairs={{0,8},{4,12},{8,0},{12,4},{1,9},{5,13},{9,1},{13,5},{2,10},{6,14},... | collective-permute-start | bytes 221192 | tf_op jit(solution)/shard_map/ppermute | solution.py:299
  19.0 6.2 %collective-permute-start.1 = (f32[72,256]{1,0:T(8,128)S(1)}, f32[72,256]{1,0:T(8,128)S(1)}, u32[]{:S(2)}, u32[]{:S(2)}) collective-permute-start(f32[72,256]{1,0:T(8,128)S(1)} %get-tuple-element.9.refs_0_), channel_id=1, source_target_pairs={{0,4},{4,0},{8,12},{12,8},{1,5},{5,1},{9,13},{13,9},{2,6},{6,2},{1... | collective-permute-start | bytes 221192 | tf_op jit(solution)/shard_map/ppermute | solution.py:299
  19.6 1.6 %collective-permute-start.10 = (s32[2048]{0:T(1024)S(1)}, s32[2048]{0:T(1024)S(1)}, u32[]{:S(2)}, u32[]{:S(2)}) collective-permute-start(s32[2048]{0:T(1024)S(1)} %copy-done.4), channel_id=1, source_target_pairs={{0,1},{1,0},{2,3},{3,2},{4,5},{5,4},{6,7},{7,6},{8,9},{9,8},{10,11... | collective-permute-start | bytes 24584 | tf_op jit(solution)/shard_map/ppermute | solution.py:287
  19.6 6.1 %collective-permute-start.8 = (f32[24,256]{1,0:T(8,128)S(1)}, f32[24,256]{1,0:T(8,128)S(1)}, u32[]{:S(2)}, u32[]{:S(2)}) collective-permute-start(f32[24,256]{1,0:T(8,128)S(1)} %get-tuple-element.10.refs_8_), channel_id=1, source_target_pairs={{0,2},{2,0},{1,3},{3,1},{4,6},{6,4},{5,7},{7,5},{8,10},{10,8},{9,1... | collective-permute-start | bytes 73736 | tf_op jit(solution)/shard_map/ppermute | solution.py:302
  21.2 11.0 %collective-permute-start = (f32[72,256]{1,0:T(8,128)S(1)}, f32[72,256]{1,0:T(8,128)S(1)}, u32[]{:S(2)}, u32[]{:S(2)}) collective-permute-start(f32[72,256]{1,0:T(8,128)S(1)} %get-tuple-element.9.refs_0_), channel_id=1, source_target_pairs={{0,1},{1,0},{2,3},{3,2},{4,5},{5,4},{6,7},{7,6},{8,9},{9,8},{10,11... | collective-permute-start | bytes 221192 | tf_op jit(solution)/shard_map/ppermute | solution.py:307
  21.7 10.5 %collective-permute-start.6 = (f32[72,256]{1,0:T(8,128)S(1)}, f32[72,256]{1,0:T(8,128)S(1)}, u32[]{:S(2)}, u32[]{:S(2)}) collective-permute-start(f32[72,256]{1,0:T(8,128)S(1)} %collective-permute-done.5.refs_6_), channel_id=1, source_target_pairs={{0,1},{1,0},{2,3},{3,2},{4,5},{5,4},{6,7},{7,6},{8,9},{9,8},{10,11... | collective-permute-start | bytes 221192 | tf_op jit(solution)/shard_map/ppermute | solution.py:307
  25.2 7.1 %collective-permute-start.4 = (f32[72,256]{1,0:T(8,128)S(1)}, f32[72,256]{1,0:T(8,128)S(1)}, u32[]{:S(2)}, u32[]{:S(2)}) collective-permute-start(f32[72,256]{1,0:T(8,128)S(1)} %collective-permute-done.3.refs_4_), channel_id=1, source_target_pairs={{0,1},{1,0},{2,3},{3,2},{4,5},{5,4},{6,7},{7,6},{8,9},{9,8},{10,11... | collective-permute-start | bytes 221192 | tf_op jit(solution)/shard_map/ppermute | solution.py:307
  25.2 7.1 %collective-permute-start.2 = (f32[72,256]{1,0:T(8,128)S(1)}, f32[72,256]{1,0:T(8,128)S(1)}, u32[]{:S(2)}, u32[]{:S(2)}) collective-permute-start(f32[72,256]{1,0:T(8,128)S(1)} %collective-permute-done.1.refs_2_), channel_id=1, source_target_pairs={{0,1},{1,0},{2,3},{3,2},{4,5},{5,4},{6,7},{7,6},{8,9},{9,8},{10,11... | collective-permute-start | bytes 221192 | tf_op jit(solution)/shard_map/ppermute | solution.py:307
  25.7 1.2 %collective-permute-start.7 = (f32[24,256]{1,0:T(8,128)S(1)}, f32[24,256]{1,0:T(8,128)S(1)}, u32[]{:S(2)}, u32[]{:S(2)}) collective-permute-start(f32[24,256]{1,0:T(8,128)S(1)} %get-tuple-element.10.refs_8_), channel_id=1, source_target_pairs={{0,1},{1,0},{2,3},{3,2},{4,5},{5,4},{6,7},{7,6},{8,9},{9,8},{10,11... | collective-permute-start | bytes 73736 | tf_op jit(solution)/shard_map/ppermute | solution.py:307
  26.9 5.4 %collective-permute-start.9 = (f32[24,256]{1,0:T(8,128)S(1)}, f32[24,256]{1,0:T(8,128)S(1)}, u32[]{:S(2)}, u32[]{:S(2)}) collective-permute-start(f32[24,256]{1,0:T(8,128)S(1)} %collective-permute-done.8.refs_10_), channel_id=1, source_target_pairs={{0,1},{1,0},{2,3},{3,2},{4,5},{5,4},{6,7},{7,6},{8,9},{9,8},{10,11... | collective-permute-start | bytes 73736 | tf_op jit(solution)/shard_map/ppermute | solution.py:307
  27.1 5.2 %copy-start.5 = (f32[2048]{0:T(1024)S(1)}, f32[2048]{0:T(1024)}, u32[]{:S(2)}) copy-start(f32[2048]{0:T(1024)} %param.17) | copy-start | bytes 24580
  37.0 1.2 %collective-permute-start.11 = (f32[32,128]{1,0:T(8,128)S(1)}, f32[32,128]{1,0:T(8,128)S(1)}, u32[]{:S(2)}, u32[]{:S(2)}) collective-permute-start(f32[32,128]{1,0:T(8,128)S(1)} %get-tuple-element.12), channel_id=1, source_target_pairs={{0,1},{1,0},{2,3},{3,2},{4,5},{5,4},{6,7},{7,6},{8,9},{9,8},{10,11... | collective-permute-start | bytes 49160 | tf_op jit(solution)/shard_map/ppermute | solution.py:318

commit v2 on v1

--- a/solution.py
+++ b/solution.py
@@ -31,13 +31,21 @@
     cls_ref,
     train_label_ref,
     test_label_ref,
+    seed_ref,
     train_packet,
     test_packet,
+    own_packet,
     rows,
     weight,
     pooled,
+    gain_row,
+    cls_rows,
+    train_label,
+    test_label,
+    seeds,
     row_sem,
     weight_sem,
+    small_sem,
 ):
     proj_index = lax.axis_index("proj")
     train_count, length, width = train_hbm.shape
@@ -52,8 +60,24 @@
         pltpu.make_async_copy(
             source.at[pl.ds(offset, block)], rows.at[pl.ds(b * block, block)], row_sem.at[b]
         ).start()
+    small = [
+        pltpu.make_async_copy(source, target, small_sem.at[i])
+        for i, (source, target) in enumerate(
+            (
+                (gain_ref, gain_row),
+                (cls_ref, cls_rows),
+                (train_label_ref, train_label),
+                (test_label_ref, test_label),
+                (seed_ref, seeds),
+            )
+        )
+    ]
+    for copy in small:
+        copy.start()
     weight_copy.wait()
-    gain = gain_ref[...]
+    for copy in small:
+        copy.wait()
+    gain = gain_row[...]
     own_start = pl.multiple_of(proj_index * half, half)
 
     def one_block(b, carry):
@@ -75,25 +99,30 @@
         return carry
 
     lax.fori_loop(0, blocks, one_block, 0)
+    at = 0
     for packet, label_ref, start, count in (
-        (train_packet, train_label_ref, 0, train_count),
-        (test_packet, test_label_ref, train_count, test_count),
+        (train_packet, train_label, 0, train_count),
+        (test_packet, test_label, train_count, test_count),
     ):
         own = pooled[pl.ds(start, count), :]
-        packet[pl.ds(0, count), :] = own
-        packet[pl.ds(count, NCLS), pl.ds(0, count)] = lax.dot_general(
-            cls_ref[...],
+        logits = lax.dot_general(
+            cls_rows[...],
             own,
             (((1,), (1,)), ((), ())),
             precision=lax.Precision.HIGHEST,
             preferred_element_type=jnp.float32,
         )
-        packet[pl.ds(count, NCLS), pl.ds(128, count)] = jnp.broadcast_to(
-            label_ref[...].astype(jnp.float32), (NCLS, count)
-        )
-
-
-def pool(train_windows, test_windows, weight, gain, cls_t, train_labels, test_labels):
+        labels = jnp.broadcast_to(label_ref[...].astype(jnp.float32), (NCLS, count))
+        for target, first in ((packet, 0), (own_packet, at)):
+            target[pl.ds(first, count), :] = own
+            target[pl.ds(first + count, NCLS), pl.ds(0, count)] = logits
+            target[pl.ds(first + count, NCLS), pl.ds(128, count)] = labels
+        at += count + NCLS
+    own_packet[pl.ds(at, seeds.shape[0]), pl.ds(0, 128)] = (seeds[...] >> 15).astype(jnp.float32)
+    own_packet[pl.ds(at, seeds.shape[0]), pl.ds(128, 128)] = (seeds[...] & 32767).astype(jnp.float32)
+
+
+def pool(train_windows, test_windows, weight, gain, cls_t, train_labels, test_labels, seeds):
     block = 8
     train_count, length, width = train_windows.shape
     test_count = test_windows.shape[0]
@@ -104,28 +133,46 @@
         out_shape=(
             jax.ShapeDtypeStruct((train_count + NCLS, half), jnp.float32),
             jax.ShapeDtypeStruct((test_count + NCLS, half), jnp.float32),
+            jax.ShapeDtypeStruct((total + 2 * NCLS + seeds.shape[0], half), jnp.float32),
         ),
-        in_specs=[HBM, HBM, HBM, VMEM, VMEM, VMEM, VMEM],
-        out_specs=(VMEM, VMEM),
+        in_specs=[HBM] * 8,
+        out_specs=(VMEM, VMEM, VMEM),
         scratch_shapes=[
             pltpu.VMEM((total, length, width), jnp.bfloat16),
             pltpu.VMEM(weight.shape, jnp.bfloat16),
             pltpu.VMEM((total, half), jnp.float32),
+            pltpu.VMEM(gain.shape, jnp.float32),
+            pltpu.VMEM(cls_t.shape, jnp.float32),
+            pltpu.VMEM(train_labels.shape, jnp.int32),
+            pltpu.VMEM(test_labels.shape, jnp.int32),
+            pltpu.VMEM(seeds.shape, jnp.int32),
             pltpu.SemaphoreType.DMA((total // block,)),
             pltpu.SemaphoreType.DMA,
+            pltpu.SemaphoreType.DMA((5,)),
         ],
         compiler_params=pltpu.CompilerParams(vmem_limit_bytes=24 * MIB),
         name="pool",
-    )(train_windows, test_windows, weight, gain, cls_t, train_labels, test_labels)
-
-
-def sign_kernel(seed_ref, sign_ref, turned):
+    )(
+        *(
+            pltpu.with_memory_space_constraint(value, pltpu.HBM)
+            for value in (train_windows, test_windows, weight, gain, cls_t, train_labels, test_labels, seeds)
+        )
+    )
+
+
+def sign_kernel(packed, seed_ref, sign_ref, turned):
     proj_index = lax.axis_index("proj")
     parts, rows, part_width = sign_ref.shape
     count = parts * part_width
     chunks = rows // 128
     per_chunk = 128 // NCLS
-    turned[:, pl.ds(0, chunks)] = seed_ref[...].T
+    if packed:
+        first = seed_ref.shape[0] - chunks
+        high = seed_ref[pl.ds(first, chunks), pl.ds(0, 128)].astype(jnp.int32)
+        seeds = high * 32768 + seed_ref[pl.ds(first, chunks), pl.ds(128, 128)].astype(jnp.int32)
+    else:
+        seeds = seed_ref[...]
+    turned[:, pl.ds(0, chunks)] = seeds.T
     columns = (
         lax.broadcasted_iota(jnp.int32, (per_chunk, count), 1) + proj_index * count
     ) * MIX_COLUMN
@@ -140,26 +187,26 @@
                 sign_ref[n, pl.ds(at, per_chunk), :] = signs[:, n * part_width : (n + 1) * part_width]
 
 
-def sign_block(seeds, count):
-    rows = seeds.shape[0]
+def sign_block(seeds, rows, count):
     parts = count // 256
     return pl.pallas_call(
-        sign_kernel,
+        functools.partial(sign_kernel, seeds.dtype == jnp.float32),
         out_shape=jax.ShapeDtypeStruct((parts, rows, 256), jnp.bfloat16),
         in_specs=[VMEM],
         out_specs=VMEM,
         scratch_shapes=[pltpu.VMEM((128, 128), jnp.int32)],
         compiler_params=pltpu.CompilerParams(vmem_limit_bytes=16 * MIB),
-        cost_estimate=pl.CostEstimate(flops=8 * rows * count, bytes_accessed=2 * rows * count, transcendentals=0),
+        cost_estimate=pl.CostEstimate(
+            flops=8 * rows * count, bytes_accessed=2 * rows * count, transcendentals=0
+        ),
         name="signs",
-    )(seeds.reshape(rows // 128, 128))
+    )(seeds)
 
 
 def score_kernel(train_blocks, test_blocks, train_count, test_count, *refs):
-    packets = refs[: 2 * (train_blocks + test_blocks)]
-    own_signs, other_signs, precond_ref, keep_ref, send_ref, grad, row_weight, total = refs[
-        2 * (train_blocks + test_blocks) :
-    ]
+    far = train_blocks + test_blocks - 2
+    packets = refs[: 2 * far + 2]
+    own_signs, other_signs, precond_ref, keep_ref, send_ref, grad, row_weight, total = refs[2 * far + 2 :]
     step = pl.program_id(0)
     proj_index = lax.axis_index("proj")
     half = packets[0].shape[1]
@@ -171,7 +218,16 @@
     def _():
         total[...] = jnp.zeros_like(total)
         for i in range(train_blocks + test_blocks):
-            mine, theirs = packets[2 * i], packets[2 * i + 1]
+            first = 0
+            if i == 0:
+                mine, theirs = packets[0], packets[1]
+            elif i < train_blocks:
+                mine, theirs = packets[2 * i], packets[2 * i + 1]
+            elif i == train_blocks:
+                mine, theirs = packets[0], packets[1]
+                first = train_count + NCLS
+            else:
+                mine, theirs = packets[2 * (i - 1)], packets[2 * (i - 1) + 1]
             if i < train_blocks:
                 count = train_count
                 at = _source(lax.axis_index("train"), i, train_blocks) * count
@@ -181,8 +237,9 @@
                     lax.axis_index("test"), i - train_blocks, test_blocks
                 ) * count
             at = pl.multiple_of(at, count)
-            logits = mine[pl.ds(count, NCLS), pl.ds(0, 128)] + theirs[pl.ds(count, NCLS), pl.ds(0, 128)]
-            label = mine[pl.ds(count, NCLS), pl.ds(128, 128)]
+            class_rows = pl.ds(first + count, NCLS)
+            logits = mine[class_rows, pl.ds(0, 128)] + theirs[class_rows, pl.ds(0, 128)]
+            label = mine[class_rows, pl.ds(128, 128)]
             chance = 1.0 / (1.0 + jnp.exp(-logits))
             classes = lax.broadcasted_iota(jnp.int32, (NCLS, 128), 0).astype(jnp.float32)
             target = jnp.where(label == classes, 1.0, 0.0)
@@ -194,7 +251,7 @@
             if i < train_blocks:
                 row_weight[pl.ds(at, count), :] = jnp.broadcast_to(turned[:, NCLS : NCLS + 1], (count, 128))
             for side, packet in enumerate((mine, theirs)):
-                value = packet[pl.ds(0, count), :]
+                value = packet[pl.ds(first, count), :]
                 for k in range(NCLS):
                     grad[pl.ds(at, count), pl.ds(side * half_rows + k * half, half)] = (
                         value * turned[:, k : k + 1]
@@ -284,8 +341,8 @@
     test_blocks = lax.axis_size("test")
     count = K // lax.axis_size("proj")
     swap = [(0, 1), (1, 0)]
-    other_seeds = lax.ppermute(sign_seeds, "proj", swap)
-    train_packet, test_packet = pool(
+    seeds = sign_seeds.reshape(-1, 128)
+    train_packet, test_packet, own_packet = pool(
         train_windows,
         test_windows,
         dilated_weight,
@@ -293,17 +350,16 @@
         cls_weight.T,
         train_labels.reshape(1, -1),
         test_labels.reshape(1, -1),
-    )
-    mine = [train_packet]
-    for shift in range(1, train_blocks):
-        mine.append(lax.ppermute(train_packet, "train", _pairs(shift, train_blocks)))
-    mine.append(test_packet)
-    for shift in range(1, test_blocks):
-        mine.append(lax.ppermute(test_packet, "test", _pairs(shift, test_blocks)))
-    own_signs = sign_block(sign_seeds, count)
-    other_signs = sign_block(other_seeds, count)
-    packets = []
-    for value in mine:
+        seeds,
+    )
+    far = [lax.ppermute(train_packet, "train", _pairs(shift, train_blocks)) for shift in range(1, train_blocks)]
+    far += [lax.ppermute(test_packet, "test", _pairs(shift, test_blocks)) for shift in range(1, test_blocks)]
+    other_packet = lax.ppermute(own_packet, "proj", swap)
+    own_signs = sign_block(seeds, sign_seeds.shape[0], count)
+    *far, own_signs, other_packet = lax.optimization_barrier((*far, own_signs, other_packet))
+    other_signs = sign_block(other_packet, sign_seeds.shape[0], count)
+    packets = [own_packet, other_packet]
+    for value in far:
         packets += [value, lax.ppermute(value, "proj", swap)]
     keep, send = partial_scores(
         packets,

time: 39.2 us -> 31.2 us (0.80)
  local copies, waits for them, and re-layouts: 7.24 us -> 0.01 us
  waiting for transfers between devices: 5.64 us -> 3.01 us
  Pallas kernels: 16.4 us -> 18.7 us
    unnamed x18 -> x4, local copies, waits for them, and re-layouts: 7.24 us -> 0.01 us
    pallas_call x1, Pallas kernels: 6.6 us -> 8.82 us  [pool(): pl.pallas_call(functools.partial(pool_kernel, block), out_shape=(jax.Shap...]
    ppermute x3, waiting for transfers between devices: 3.65 us -> 1.88 us  [shards(): lax.ppermute(train_packet, 'train', _pairs(shift, train_blocks))]
    ppermute x6 -> x4, waiting for transfers between devices: 1.14 us -> 0.01 us  [shards(): packets += [value, lax.ppermute(value, 'proj', swap)]]
    ppermute x2, starting transfers between devices: 1.64 us -> 2.15 us  [the longest x1 1.63 us: shards(): lax.ppermute(test_packet, 'test', _pairs(shift, test_blocks))]
    ppermute x3, starting transfers between devices: 5.75 us -> 5.32 us  [shards(): lax.ppermute(train_packet, 'train', _pairs(shift, train_blocks))]
    ppermute x6 -> x4, starting transfers between devices: 1.02 us -> 1.02 us  [shards(): packets += [value, lax.ppermute(value, 'proj', swap)]]
  transfers between devices with their start and end apart: 12 -> 10, of which waited for: 4 -> 2; matrix products, arithmetic and copies ran while one was open for 0% -> 0% of each run, Pallas kernels for 13% -> 17%
where the time goes in v2:
time: 31.2 us; the launch traced here: 31 us
  Pallas kernels  18.7 us (60%)
  starting transfers between devices  8.62 us (28%)
  waiting for transfers between devices  3.01 us (10%)
  other arithmetic  0.61 us (2%)
    pallas_call x1, Pallas kernels, pool(): pl.pallas_call(functools.partial(pool_kernel, block), out_shape=(jax.Shap...  8.82 us
    ppermute x3, starting transfers between devices, shards(): lax.ppermute(train_packet, 'train', _pairs(shift, train_blocks))  5.32 us
    pallas_call x2, Pallas kernels, sign_block(): pl.pallas_call(functools.partial(sign_kernel, seeds.dtype == jnp.float32)...  5.17 us
    pallas_call x1, Pallas kernels, partial_scores(): pl.pallas_call(functools.partial(score_kernel, train_blocks, test_blocks,...  4.68 us
    ppermute x3, waiting for transfers between devices, shards(): lax.ppermute(train_packet, 'train', _pairs(shift, train_blocks))  1.88 us
    ppermute x1, starting transfers between devices, shards(): lax.ppermute(test_packet, 'test', _pairs(shift, test_blocks))  1.63 us
    ppermute x1, waiting for transfers between devices, shards(): received = lax.ppermute(send, 'proj', swap)  1.11 us
    ppermute x4, starting transfers between devices, shards(): packets += [value, lax.ppermute(value, 'proj', swap)]  1.02 us
  transfers between devices with their start and end apart: 10, of which 2 were waited for; matrix products, arithmetic and copies ran while one was open for 0% of the time, Pallas kernels for 17%

profile of v2, /device:TPU:0, one launch (start us, length us, event | category | flops | bytes accessed | tf_op | source)
XLA Modules:
  0.0 31.0 jit_solution(18085711647322672129)
XLA Ops:
  0.0 0.0 copy-start
  0.0 8.8 %pool.1 = (f32[72,256]{1,0:T(8,128)S(1)}, f32[24,256]{1,0:T(8,128)S(1)}, f32[112,256]{1,0:T(8,128)S(1)}) custom-call(bf16[64,64,512]{2,1,0:T(8,128)(2,1)} %train_hbm.1, bf16[16,64,512]{2,1,0:T(8,128)(2,1)} %test_hbm.1, bf16[3,512,256]{2,1,0:T(8,128)(2,1)} %weight_hbm.1, f32[1,256]{1,0:T(1,128)} %bitcast.10, f32[8,256]{1,0:T(8,128)} %bitcast.9, ...), custom_call_target="tpu_custom_call" | custom-call | tf_op jit(solution)/shard_map/pool/pallas_call | solution.py:131
  8.8 0.5 %collective-permute-start.4 = (f32[112,256]{1,0:T(8,128)S(1)}, f32[112,256]{1,0:T(8,128)S(1)}, u32[]{:S(2)}, u32[]{:S(2)}) collective-permute-start(f32[112,256]{1,0:T(8,128)S(1)} %get-tuple-element.16.refs_0_), channel_id=1, source_target_pairs={{0,1},{1,0},{2,3},{3,2},{4,5},{5,4},{6,7},{7,6},{8,9},{9,8},{10,11... | collective-permute-start | bytes 344072 | tf_op jit(solution)/shard_map/ppermute | solution.py:357
  9.4 4.7 %collective-permute-start.2 = (f32[72,256]{1,0:T(8,128)S(1)}, f32[72,256]{1,0:T(8,128)S(1)}, u32[]{:S(2)}, u32[]{:S(2)}) collective-permute-start(f32[72,256]{1,0:T(8,128)S(1)} %get-tuple-element.17), channel_id=1, source_target_pairs={{0,12},{4,8},{8,4},{12,0},{1,13},{5,9},{9,5},{13,1},{2,14},{6,10},... | collective-permute-start | bytes 221192 | tf_op jit(solution)/shard_map/ppermute | solution.py:355
  14.0 0.0 collective-permute-start.1
  14.0 0.6 %collective-permute-start = (f32[72,256]{1,0:T(8,128)S(1)}, f32[72,256]{1,0:T(8,128)S(1)}, u32[]{:S(2)}, u32[]{:S(2)}) collective-permute-start(f32[72,256]{1,0:T(8,128)S(1)} %get-tuple-element.17), channel_id=1, source_target_pairs={{0,4},{4,0},{8,12},{12,8},{1,5},{5,1},{9,13},{13,9},{2,6},{6,2},{1... | collective-permute-start | bytes 221192 | tf_op jit(solution)/shard_map/ppermute | solution.py:355
  14.7 0.0 copy-start.1
  14.7 1.6 %collective-permute-start.3 = (f32[24,256]{1,0:T(8,128)S(1)}, f32[24,256]{1,0:T(8,128)S(1)}, u32[]{:S(2)}, u32[]{:S(2)}) collective-permute-start(f32[24,256]{1,0:T(8,128)S(1)} %get-tuple-element.18), channel_id=1, source_target_pairs={{0,2},{2,0},{1,3},{3,1},{4,6},{6,4},{5,7},{7,5},{8,10},{10,8},{9,1... | collective-permute-start | bytes 73736 | tf_op jit(solution)/shard_map/ppermute | solution.py:356
  16.3 0.0 copy-done
  16.3 2.6 %signs.2.refs_10_ = bf16[4,2048,256]{2,1,0:T(8,128)(2,1)S(1)} custom-call(s32[16,128]{1,0:T(8,128)S(1)} %bitcast.7), custom_call_target="tpu_custom_call" | custom-call | flops 16777216 | bytes 4194304 | tf_op jit(solution)/shard_map/signs/pallas_call | solution.py:192
  18.9 0.0 collective-permute-done.3.refs_8_
  18.9 0.0 collective-permute-done.2.refs_6_
  18.9 1.9 %collective-permute-done.1.refs_4_ = f32[72,256]{1,0:T(8,128)S(1)} collective-permute-done((f32[72,256]{1,0:T(8,128)S(1)}, f32[72,256]{1,0:T(8,128)S(1)}, u32[]{:S(2)}, u32[]{:S(2)}) %collective-permute-start.1) | collective-permute-done | bytes 73760 | tf_op jit(solution)/shard_map/ppermute | solution.py:355
  20.8 0.0 collective-permute-done.refs_2_
  20.8 0.0 collective-permute-done.4.seed_ref.refs_1_
  20.8 0.0 collective-permute-start.5
  20.8 0.5 %collective-permute-start.6 = (f32[72,256]{1,0:T(8,128)S(1)}, f32[72,256]{1,0:T(8,128)S(1)}, u32[]{:S(2)}, u32[]{:S(2)}) collective-permute-start(f32[72,256]{1,0:T(8,128)S(1)} %collective-permute-done.1.refs_4_), channel_id=1, source_target_pairs={{0,1},{1,0},{2,3},{3,2},{4,5},{5,4},{6,7},{7,6},{8,9},{9,8},{10,11... | collective-permute-start | bytes 221192 | tf_op jit(solution)/shard_map/ppermute | solution.py:363
  21.3 0.1 collective-permute-start.7
  21.4 0.4 %collective-permute-start.8 = (f32[24,256]{1,0:T(8,128)S(1)}, f32[24,256]{1,0:T(8,128)S(1)}, u32[]{:S(2)}, u32[]{:S(2)}) collective-permute-start(f32[24,256]{1,0:T(8,128)S(1)} %collective-permute-done.3.refs_8_), channel_id=1, source_target_pairs={{0,1},{1,0},{2,3},{3,2},{4,5},{5,4},{6,7},{7,6},{8,9},{9,8},{10,11... | collective-permute-start | bytes 73736 | tf_op jit(solution)/shard_map/ppermute | solution.py:363
  21.8 2.6 %signs.3.refs_11_ = bf16[4,2048,256]{2,1,0:T(8,128)(2,1)S(1)} custom-call(f32[112,256]{1,0:T(8,128)S(1)} %collective-permute-done.4.seed_ref.refs_1_), custom_call_target="tpu_custom_call" | custom-call | flops 16777216 | bytes 4194304 | tf_op jit(solution)/shard_map/signs/pallas_call | solution.py:192
  24.4 0.0 collective-permute-done.8.refs_9_
  24.4 0.0 collective-permute-done.5.refs_3_
  24.4 0.0 collective-permute-done.6.refs_5_
  24.5 0.0 collective-permute-done.7.refs_7_
  24.5 0.0 copy-done.1
  24.5 4.7 %partial_scores.1 = (f32[32,128]{1,0:T(8,128)S(1)}, f32[32,128]{1,0:T(8,128)S(1)}) custom-call(f32[112,256]{1,0:T(8,128)S(1)} %get-tuple-element.16.refs_0_, f32[112,256]{1,0:T(8,128)S(1)} %collective-permute-done.4.seed_ref.refs_1_, f32[72,256]{1,0:T(8,128)S(1)} %collective-permute-done.refs_2_, f32[72,256]{1,0:T(8,128)S(1)} %collective-permute-done.5.refs_3_, ...), custom_call_target="tpu_custom_call" | custom-call | tf_op jit(solution)/shard_map/partial_scores/pallas_call | solution.py:304
  29.2 0.1 collective-permute-start.9
  29.3 1.1 %collective-permute-done.9 = f32[32,128]{1,0:T(8,128)S(1)} collective-permute-done((f32[32,128]{1,0:T(8,128)S(1)}, f32[32,128]{1,0:T(8,128)S(1)}, u32[]{:S(2)}, u32[]{:S(2)}) %collective-permute-start.9) | collective-permute-done | bytes 16416 | tf_op jit(solution)/shard_map/ppermute | solution.py:374
  30.4 0.6 %add_multiply_fusion = f32[32,128]{1,0:T(8,128)} fusion(f32[32,128]{1,0:T(8,128)S(1)} %get-tuple-element.25, f32[32,128]{1,0:T(8,128)S(1)} %collective-permute-done.9), kind=kLoop, calls=%fused_computation | loop fusion | flops 8192 | bytes 49152 | tf_op jit(solution)/shard_map/mul | solution.py:375
Async XLA Ops:
  0.0 16.3 %copy-start = (s32[2048]{0:T(1024)S(1)}, s32[2048]{0:T(1024)}, u32[]{:S(2)}) copy-start(s32[2048]{0:T(1024)} %param.16) | copy-start | bytes 24580
  8.8 12.0 %collective-permute-start.4 = (f32[112,256]{1,0:T(8,128)S(1)}, f32[112,256]{1,0:T(8,128)S(1)}, u32[]{:S(2)}, u32[]{:S(2)}) collective-permute-start(f32[112,256]{1,0:T(8,128)S(1)} %get-tuple-element.16.refs_0_), channel_id=1, source_target_pairs={{0,1},{1,0},{2,3},{3,2},{4,5},{5,4},{6,7},{7,6},{8,9},{9,8},{10,11... | collective-permute-start | bytes 344072 | tf_op jit(solution)/shard_map/ppermute | solution.py:357
  9.4 9.6 %collective-permute-start.2 = (f32[72,256]{1,0:T(8,128)S(1)}, f32[72,256]{1,0:T(8,128)S(1)}, u32[]{:S(2)}, u32[]{:S(2)}) collective-permute-start(f32[72,256]{1,0:T(8,128)S(1)} %get-tuple-element.17), channel_id=1, source_target_pairs={{0,12},{4,8},{8,4},{12,0},{1,13},{5,9},{9,5},{13,1},{2,14},{6,10},... | collective-permute-start | bytes 221192 | tf_op jit(solution)/shard_map/ppermute | solution.py:355
  14.0 6.8 %collective-permute-start.1 = (f32[72,256]{1,0:T(8,128)S(1)}, f32[72,256]{1,0:T(8,128)S(1)}, u32[]{:S(2)}, u32[]{:S(2)}) collective-permute-start(f32[72,256]{1,0:T(8,128)S(1)} %get-tuple-element.17), channel_id=1, source_target_pairs={{0,8},{4,12},{8,0},{12,4},{1,9},{5,13},{9,1},{13,5},{2,10},{6,14},... | collective-permute-start | bytes 221192 | tf_op jit(solution)/shard_map/ppermute | solution.py:355
  14.0 6.8 %collective-permute-start = (f32[72,256]{1,0:T(8,128)S(1)}, f32[72,256]{1,0:T(8,128)S(1)}, u32[]{:S(2)}, u32[]{:S(2)}) collective-permute-start(f32[72,256]{1,0:T(8,128)S(1)} %get-tuple-element.17), channel_id=1, source_target_pairs={{0,4},{4,0},{8,12},{12,8},{1,5},{5,1},{9,13},{13,9},{2,6},{6,2},{1... | collective-permute-start | bytes 221192 | tf_op jit(solution)/shard_map/ppermute | solution.py:355
  14.7 9.8 %copy-start.1 = (f32[2048]{0:T(1024)S(1)}, f32[2048]{0:T(1024)}, u32[]{:S(2)}) copy-start(f32[2048]{0:T(1024)} %param.17) | copy-start | bytes 24580
  14.7 4.2 %collective-permute-start.3 = (f32[24,256]{1,0:T(8,128)S(1)}, f32[24,256]{1,0:T(8,128)S(1)}, u32[]{:S(2)}, u32[]{:S(2)}) collective-permute-start(f32[24,256]{1,0:T(8,128)S(1)} %get-tuple-element.18), channel_id=1, source_target_pairs={{0,2},{2,0},{1,3},{3,1},{4,6},{6,4},{5,7},{7,5},{8,10},{10,8},{9,1... | collective-permute-start | bytes 73736 | tf_op jit(solution)/shard_map/ppermute | solution.py:356
  20.8 3.6 %collective-permute-start.5 = (f32[72,256]{1,0:T(8,128)S(1)}, f32[72,256]{1,0:T(8,128)S(1)}, u32[]{:S(2)}, u32[]{:S(2)}) collective-permute-start(f32[72,256]{1,0:T(8,128)S(1)} %collective-permute-done.refs_2_), channel_id=1, source_target_pairs={{0,1},{1,0},{2,3},{3,2},{4,5},{5,4},{6,7},{7,6},{8,9},{9,8},{10,11... | collective-permute-start | bytes 221192 | tf_op jit(solution)/shard_map/ppermute | solution.py:363
  20.8 3.6 %collective-permute-start.6 = (f32[72,256]{1,0:T(8,128)S(1)}, f32[72,256]{1,0:T(8,128)S(1)}, u32[]{:S(2)}, u32[]{:S(2)}) collective-permute-start(f32[72,256]{1,0:T(8,128)S(1)} %collective-permute-done.1.refs_4_), channel_id=1, source_target_pairs={{0,1},{1,0},{2,3},{3,2},{4,5},{5,4},{6,7},{7,6},{8,9},{9,8},{10,11... | collective-permute-start | bytes 221192 | tf_op jit(solution)/shard_map/ppermute | solution.py:363
  21.3 3.1 %collective-permute-start.7 = (f32[72,256]{1,0:T(8,128)S(1)}, f32[72,256]{1,0:T(8,128)S(1)}, u32[]{:S(2)}, u32[]{:S(2)}) collective-permute-start(f32[72,256]{1,0:T(8,128)S(1)} %collective-permute-done.2.refs_6_), channel_id=1, source_target_pairs={{0,1},{1,0},{2,3},{3,2},{4,5},{5,4},{6,7},{7,6},{8,9},{9,8},{10,11... | collective-permute-start | bytes 221192 | tf_op jit(solution)/shard_map/ppermute | solution.py:363
  21.4 3.0 %collective-permute-start.8 = (f32[24,256]{1,0:T(8,128)S(1)}, f32[24,256]{1,0:T(8,128)S(1)}, u32[]{:S(2)}, u32[]{:S(2)}) collective-permute-start(f32[24,256]{1,0:T(8,128)S(1)} %collective-permute-done.3.refs_8_), channel_id=1, source_target_pairs={{0,1},{1,0},{2,3},{3,2},{4,5},{5,4},{6,7},{7,6},{8,9},{9,8},{10,11... | collective-permute-start | bytes 73736 | tf_op jit(solution)/shard_map/ppermute | solution.py:363
  29.2 1.2 %collective-permute-start.9 = (f32[32,128]{1,0:T(8,128)S(1)}, f32[32,128]{1,0:T(8,128)S(1)}, u32[]{:S(2)}, u32[]{:S(2)}) collective-permute-start(f32[32,128]{1,0:T(8,128)S(1)} %get-tuple-element.26), channel_id=1, source_target_pairs={{0,1},{1,0},{2,3},{3,2},{4,5},{5,4},{6,7},{7,6},{8,9},{9,8},{10,11... | collective-permute-start | bytes 49160 | tf_op jit(solution)/shard_map/ppermute | solution.py:374

commit v3 on v2

--- a/solution.py
+++ b/solution.py
@@ -17,6 +17,7 @@
 MIX_LAST = (1274126177 << 15) & 0xFFFFFFFF
 MIX_LAST = MIX_LAST - (1 << 32) if MIX_LAST >= 1 << 31 else MIX_LAST
 MIB = 2**20
+AHEAD = 3
 
 VMEM = pl.BlockSpec(memory_space=pltpu.VMEM)
 HBM = pl.BlockSpec(memory_space=pltpu.HBM)
@@ -54,12 +55,16 @@
     blocks = (train_count + test_count) // block
     weight_copy = pltpu.make_async_copy(weight_hbm, weight, weight_sem)
     weight_copy.start()
-    for b in range(blocks):
+
+    def fetch(b):
         source = train_hbm if b < train_count // block else test_hbm
         offset = b * block if b < train_count // block else b * block - train_count
-        pltpu.make_async_copy(
+        return pltpu.make_async_copy(
             source.at[pl.ds(offset, block)], rows.at[pl.ds(b * block, block)], row_sem.at[b]
-        ).start()
+        )
+
+    for b in range(min(AHEAD, blocks)):
+        fetch(b).start()
     small = [
         pltpu.make_async_copy(source, target, small_sem.at[i])
         for i, (source, target) in enumerate(
@@ -82,6 +87,12 @@
 
     def one_block(b, carry):
         start = b * block
+        for late in range(AHEAD, blocks):
+
+            @pl.when(b == late - AHEAD)
+            def _():
+                fetch(late).start()
+
         pltpu.make_async_copy(
             test_hbm.at[pl.ds(0, block)], rows.at[pl.ds(start, block)], row_sem.at[b]
         ).wait()
@@ -123,7 +134,7 @@
 
 
 def pool(train_windows, test_windows, weight, gain, cls_t, train_labels, test_labels, seeds):
-    block = 8
+    block = 16
     train_count, length, width = train_windows.shape
     test_count = test_windows.shape[0]
     half = weight.shape[2]
@@ -160,7 +171,7 @@
     )
 
 
-def sign_kernel(packed, seed_ref, sign_ref, turned):
+def sign_kernel(packed, seed_ref, sign_ref, turned, column_ref):
     proj_index = lax.axis_index("proj")
     parts, rows, part_width = sign_ref.shape
     count = parts * part_width
@@ -173,13 +184,17 @@
     else:
         seeds = seed_ref[...]
     turned[:, pl.ds(0, chunks)] = seeds.T
-    columns = (
-        lax.broadcasted_iota(jnp.int32, (per_chunk, count), 1) + proj_index * count
-    ) * MIX_COLUMN
+
+    @pl.when(proj_index >= 0)
+    def _():
+        column_ref[...] = (
+            lax.broadcasted_iota(jnp.int32, column_ref.shape, 1) + proj_index * count
+        ) * MIX_COLUMN
+
     for k in range(NCLS):
         seeds = turned[pl.ds(k, per_chunk, stride=NCLS), :]
         for h in range(chunks):
-            mixed = (seeds[:, h : h + 1] ^ columns) * MIX_FIRST
+            mixed = (seeds[:, h : h + 1] ^ column_ref[...]) * MIX_FIRST
             mixed = (mixed ^ (mixed >> 13)) * MIX_LAST
             signs = jnp.where(mixed < 0, -1.0, 1.0).astype(jnp.bfloat16)
             at = (k * chunks + h) * per_chunk
@@ -194,7 +209,7 @@
         out_shape=jax.ShapeDtypeStruct((parts, rows, 256), jnp.bfloat16),
         in_specs=[VMEM],
         out_specs=VMEM,
-        scratch_shapes=[pltpu.VMEM((128, 128), jnp.int32)],
+        scratch_shapes=[pltpu.VMEM((128, 128), jnp.int32), pltpu.VMEM((128 // NCLS, count), jnp.int32)],
         compiler_params=pltpu.CompilerParams(vmem_limit_bytes=16 * MIB),
         cost_estimate=pl.CostEstimate(
             flops=8 * rows * count, bytes_accessed=2 * rows * count, transcendentals=0
@@ -206,79 +221,72 @@
 def score_kernel(train_blocks, test_blocks, train_count, test_count, *refs):
     far = train_blocks + test_blocks - 2
     packets = refs[: 2 * far + 2]
-    own_signs, other_signs, precond_ref, keep_ref, send_ref, grad, row_weight, total = refs[2 * far + 2 :]
-    step = pl.program_id(0)
+    own_signs, other_signs, precond_ref, keep_ref, send_ref, train_feat, test_feat = refs[2 * far + 2 :]
     proj_index = lax.axis_index("proj")
-    half = packets[0].shape[1]
-    part_width = own_signs.shape[2]
+    parts, half_rows, part_width = own_signs.shape
     train_rows = train_blocks * train_count
-    half_rows = NCLS * half
-
-    @pl.when(step == 0)
-    def _():
-        total[...] = jnp.zeros_like(total)
-        for i in range(train_blocks + test_blocks):
-            first = 0
-            if i == 0:
-                mine, theirs = packets[0], packets[1]
-            elif i < train_blocks:
-                mine, theirs = packets[2 * i], packets[2 * i + 1]
-            elif i == train_blocks:
-                mine, theirs = packets[0], packets[1]
-                first = train_count + NCLS
-            else:
-                mine, theirs = packets[2 * (i - 1)], packets[2 * (i - 1) + 1]
-            if i < train_blocks:
-                count = train_count
-                at = _source(lax.axis_index("train"), i, train_blocks) * count
-            else:
-                count = test_count
-                at = train_rows + _source(
-                    lax.axis_index("test"), i - train_blocks, test_blocks
-                ) * count
-            at = pl.multiple_of(at, count)
-            class_rows = pl.ds(first + count, NCLS)
-            logits = mine[class_rows, pl.ds(0, 128)] + theirs[class_rows, pl.ds(0, 128)]
-            label = mine[class_rows, pl.ds(128, 128)]
-            chance = 1.0 / (1.0 + jnp.exp(-logits))
-            classes = lax.broadcasted_iota(jnp.int32, (NCLS, 128), 0).astype(jnp.float32)
-            target = jnp.where(label == classes, 1.0, 0.0)
-            retain = 1.0 - jnp.sum(chance * target, axis=0, keepdims=True)
-            stacked = jnp.concatenate(
-                [chance - target, jnp.broadcast_to(retain, (NCLS, 128))], axis=0
-            )
-            turned = stacked.T[:count]
-            if i < train_blocks:
-                row_weight[pl.ds(at, count), :] = jnp.broadcast_to(turned[:, NCLS : NCLS + 1], (count, 128))
-            for side, packet in enumerate((mine, theirs)):
-                value = packet[pl.ds(first, count), :]
-                for k in range(NCLS):
-                    grad[pl.ds(at, count), pl.ds(side * half_rows + k * half, half)] = (
-                        value * turned[:, k : k + 1]
-                    ).astype(jnp.bfloat16)
-
-    projected = jnp.dot(
-        grad[:, pl.ds(0, half_rows)], own_signs[0], preferred_element_type=jnp.float32
-    ) + jnp.dot(
-        grad[:, pl.ds(half_rows, half_rows)], other_signs[0], preferred_element_type=jnp.float32
-    )
-    weight = row_weight[...]
-    train_feat = (
-        projected[:train_rows] * jnp.concatenate([weight] * (part_width // 128), axis=1)
-    ).astype(jnp.bfloat16)
-    test_feat = (projected[train_rows:] * precond_ref[...]).astype(jnp.bfloat16)
-    total[...] += lax.dot_general(
-        test_feat,
-        train_feat,
-        (((1,), (1,)), ((), ())),
-        preferred_element_type=jnp.float32,
-    )
-
-    @pl.when(step == pl.num_programs(0) - 1)
-    def _():
-        out_width = keep_ref.shape[1]
-        keep_ref[...] = total[:, pl.ds(pl.multiple_of(proj_index * out_width, 128), out_width)]
-        send_ref[...] = total[:, pl.ds(pl.multiple_of((1 - proj_index) * out_width, 128), out_width)]
+    gradients = []
+    row_weights = []
+    for i in range(train_blocks + test_blocks):
+        first = 0
+        if i == 0:
+            mine, theirs = packets[0], packets[1]
+        elif i < train_blocks:
+            mine, theirs = packets[2 * i], packets[2 * i + 1]
+        elif i == train_blocks:
+            mine, theirs = packets[0], packets[1]
+            first = train_count + NCLS
+        else:
+            mine, theirs = packets[2 * (i - 1)], packets[2 * (i - 1) + 1]
+        count = train_count if i < train_blocks else test_count
+        class_rows = pl.ds(first + count, NCLS)
+        logits = mine[class_rows, pl.ds(0, 128)] + theirs[class_rows, pl.ds(0, 128)]
+        label = mine[class_rows, pl.ds(128, 128)]
+        chance = 1.0 / (1.0 + jnp.exp(-logits))
+        classes = lax.broadcasted_iota(jnp.int32, (NCLS, 128), 0).astype(jnp.float32)
+        target = jnp.where(label == classes, 1.0, 0.0)
+        retain = 1.0 - jnp.sum(chance * target, axis=0, keepdims=True)
+        stacked = jnp.concatenate([chance - target, jnp.broadcast_to(retain, (NCLS, 128))], axis=0)
+        turned = stacked.T[:count]
+        if i < train_blocks:
+            row_weights.append(turned[:, NCLS : NCLS + 1])
+        pieces = []
+        for packet in (mine, theirs):
+            value = packet[pl.ds(first, count), :]
+            for k in range(NCLS):
+                pieces.append((value * turned[:, k : k + 1]).astype(jnp.bfloat16))
+        gradients.append(jnp.concatenate(pieces, axis=1))
+    gradient = jnp.concatenate(gradients, axis=0)
+    train_index, test_index = lax.axis_index("train"), lax.axis_index("test")
+    for n in range(parts):
+        projected = jnp.dot(
+            gradient,
+            jnp.concatenate([own_signs[n], other_signs[n]], axis=0),
+            preferred_element_type=jnp.float32,
+        )
+        columns = pl.ds(n * part_width, part_width)
+        for i in range(train_blocks):
+            part = projected[i * train_count : (i + 1) * train_count]
+            train_feat[_source(train_index, i, train_blocks), :, columns] = (
+                part * row_weights[i]
+            ).astype(jnp.bfloat16)
+        precond = precond_ref[
+            :, pl.ds(pl.multiple_of(proj_index * (parts * part_width) + n * part_width, 128), part_width)
+        ]
+        for i in range(test_blocks):
+            start = train_rows + i * test_count
+            test_feat[_source(test_index, i, test_blocks), :, columns] = (
+                projected[start : start + test_count] * precond
+            ).astype(jnp.bfloat16)
+    half_blocks = train_blocks // 2
+    test = test_feat[...].reshape(test_blocks * test_count, parts * part_width)
+    for target, side in ((send_ref, 1 - proj_index), (keep_ref, proj_index)):
+        train = train_feat[pl.ds(side * half_blocks, half_blocks)].reshape(
+            half_blocks * train_count, parts * part_width
+        )
+        target[...] = lax.dot_general(
+            test, train, (((1,), (1,)), ((), ())), preferred_element_type=jnp.float32
+        )
 
 
 def _source(index, shift, count):
@@ -295,31 +303,24 @@
 
 def partial_scores(packets, own_signs, other_signs, precond, train_blocks, test_blocks, train_count, test_count):
     parts, rows, part_width = own_signs.shape
-    total_rows = train_blocks * train_count + test_blocks * test_count
     out_rows = test_blocks * test_count
     out_cols = train_blocks * train_count
-    sign_spec = pl.BlockSpec((1, rows, part_width), lambda n: (n, 0, 0))
-    packet_specs = [pl.BlockSpec(v.shape, lambda n: (0, 0)) for v in packets]
-    out_spec = pl.BlockSpec((out_rows, out_cols // 2), lambda n: (0, 0))
+    total_rows = out_rows + out_cols
     return pl.pallas_call(
         functools.partial(score_kernel, train_blocks, test_blocks, train_count, test_count),
-        grid=(parts,),
         out_shape=(jax.ShapeDtypeStruct((out_rows, out_cols // 2), jnp.float32),) * 2,
-        in_specs=packet_specs
-        + [
-            sign_spec,
-            sign_spec,
-            pl.BlockSpec(
-                (1, part_width), lambda n: (0, lax.axis_index("proj") * parts + n)
-            ),
-        ],
-        out_specs=(out_spec, out_spec),
+        in_specs=[VMEM] * (len(packets) + 3),
+        out_specs=(VMEM, VMEM),
         scratch_shapes=[
-            pltpu.VMEM((total_rows, 2 * rows), jnp.bfloat16),
-            pltpu.VMEM((out_cols, 128), jnp.float32),
-            pltpu.VMEM((out_rows, out_cols), jnp.float32),
+            pltpu.VMEM((train_blocks, train_count, parts * part_width), jnp.bfloat16),
+            pltpu.VMEM((test_blocks, test_count, parts * part_width), jnp.bfloat16),
         ],
         compiler_params=pltpu.CompilerParams(vmem_limit_bytes=40 * MIB),
+        cost_estimate=pl.CostEstimate(
+            flops=4 * total_rows * rows * parts * part_width,
+            bytes_accessed=4 * rows * parts * part_width,
+            transcendentals=0,
+        ),
         name="partial_scores",
     )(*packets, own_signs, other_signs, precond)
 

time: 31.2 us -> 27.7 us (0.89)
  Pallas kernels: 18.7 us -> 14.8 us
  waiting for transfers between devices: 3.01 us -> 3.38 us
    pallas_call x1, Pallas kernels: 8.82 us -> 7.25 us  [pool(): pl.pallas_call(functools.partial(pool_kernel, block), out_shape=(jax.Shap...]
    pallas_call x1, Pallas kernels: 4.68 us -> 3.16 us  [partial_scores(): pl.pallas_call(functools.partial(score_kernel, train_blocks, test_blocks,...]
    pallas_call x2, Pallas kernels: 5.17 us -> 4.44 us  [sign_block(): pl.pallas_call(functools.partial(sign_kernel, seeds.dtype == jnp.float32)...]
    ppermute x3, waiting for transfers between devices: 1.88 us -> 2.25 us  [shards(): lax.ppermute(train_packet, 'train', _pairs(shift, train_blocks))]
  transfers between devices with their start and end apart: 10 -> 10, of which waited for: 2 -> 2; matrix products, arithmetic and copies ran while one was open for 0% -> 0% of each run, Pallas kernels for 17% -> 16%
where the time goes in v3:
time: 27.7 us; the launch traced here: 27.5 us
  Pallas kernels  14.8 us (53%)
  starting transfers between devices  8.58 us (31%)
  waiting for transfers between devices  3.38 us (12%)
  other arithmetic  0.61 us (2%)
    pallas_call x1, Pallas kernels, pool(): pl.pallas_call(functools.partial(pool_kernel, block), out_shape=(jax.Shap...  7.25 us
    ppermute x3, starting transfers between devices, shards(): lax.ppermute(train_packet, 'train', _pairs(shift, train_blocks))  5.3 us
    pallas_call x2, Pallas kernels, sign_block(): pl.pallas_call(functools.partial(sign_kernel, seeds.dtype == jnp.float32)...  4.44 us
    pallas_call x1, Pallas kernels, partial_scores(): pl.pallas_call(functools.partial(score_kernel, train_blocks, test_blocks,...  3.16 us
    ppermute x3, waiting for transfers between devices, shards(): lax.ppermute(train_packet, 'train', _pairs(shift, train_blocks))  2.25 us
    ppermute x1, starting transfers between devices, shards(): lax.ppermute(test_packet, 'test', _pairs(shift, test_blocks))  1.63 us
    ppermute x1, waiting for transfers between devices, shards(): received = lax.ppermute(send, 'proj', swap)  1.11 us
    ppermute x4, starting transfers between devices, shards(): packets += [value, lax.ppermute(value, 'proj', swap)]  1.02 us
  transfers between devices with their start and end apart: 10, of which 2 were waited for; matrix products, arithmetic and copies ran while one was open for 0% of the time, Pallas kernels for 16%

profile of v3, /device:TPU:0, one launch (start us, length us, event | category | flops | bytes accessed | tf_op | source)
XLA Modules:
  0.0 27.5 jit_solution(9716091536626894663)
XLA Ops:
  0.0 0.0 copy-start
  0.0 7.3 %pool.1 = (f32[72,256]{1,0:T(8,128)S(1)}, f32[24,256]{1,0:T(8,128)S(1)}, f32[112,256]{1,0:T(8,128)S(1)}) custom-call(bf16[64,64,512]{2,1,0:T(8,128)(2,1)} %train_hbm.1, bf16[16,64,512]{2,1,0:T(8,128)(2,1)} %test_hbm.1, bf16[3,512,256]{2,1,0:T(8,128)(2,1)} %weight_hbm.1, f32[1,256]{1,0:T(1,128)} %bitcast.10, f32[8,256]{1,0:T(8,128)} %bitcast.9, ...), custom_call_target="tpu_custom_call" | custom-call | tf_op jit(solution)/shard_map/pool/pallas_call | solution.py:142
  7.3 0.5 %collective-permute-start.4 = (f32[112,256]{1,0:T(8,128)S(1)}, f32[112,256]{1,0:T(8,128)S(1)}, u32[]{:S(2)}, u32[]{:S(2)}) collective-permute-start(f32[112,256]{1,0:T(8,128)S(1)} %get-tuple-element.16.refs_0_), channel_id=1, source_target_pairs={{0,1},{1,0},{2,3},{3,2},{4,5},{5,4},{6,7},{7,6},{8,9},{9,8},{10,11... | collective-permute-start | bytes 344072 | tf_op jit(solution)/shard_map/ppermute | solution.py:358
  7.8 4.7 %collective-permute-start.2 = (f32[72,256]{1,0:T(8,128)S(1)}, f32[72,256]{1,0:T(8,128)S(1)}, u32[]{:S(2)}, u32[]{:S(2)}) collective-permute-start(f32[72,256]{1,0:T(8,128)S(1)} %get-tuple-element.17), channel_id=1, source_target_pairs={{0,12},{4,8},{8,4},{12,0},{1,13},{5,9},{9,5},{13,1},{2,14},{6,10},... | collective-permute-start | bytes 221192 | tf_op jit(solution)/shard_map/ppermute | solution.py:356
  12.5 0.0 collective-permute-start.1
  12.5 0.6 %collective-permute-start = (f32[72,256]{1,0:T(8,128)S(1)}, f32[72,256]{1,0:T(8,128)S(1)}, u32[]{:S(2)}, u32[]{:S(2)}) collective-permute-start(f32[72,256]{1,0:T(8,128)S(1)} %get-tuple-element.17), channel_id=1, source_target_pairs={{0,4},{4,0},{8,12},{12,8},{1,5},{5,1},{9,13},{13,9},{2,6},{6,2},{1... | collective-permute-start | bytes 221192 | tf_op jit(solution)/shard_map/ppermute | solution.py:356
  13.1 0.0 copy-start.1
  13.1 1.6 %collective-permute-start.3 = (f32[24,256]{1,0:T(8,128)S(1)}, f32[24,256]{1,0:T(8,128)S(1)}, u32[]{:S(2)}, u32[]{:S(2)}) collective-permute-start(f32[24,256]{1,0:T(8,128)S(1)} %get-tuple-element.18), channel_id=1, source_target_pairs={{0,2},{2,0},{1,3},{3,1},{4,6},{6,4},{5,7},{7,5},{8,10},{10,8},{9,1... | collective-permute-start | bytes 73736 | tf_op jit(solution)/shard_map/ppermute | solution.py:357
  14.7 0.0 copy-done
  14.7 2.2 %signs.2.refs_10_ = bf16[4,2048,256]{2,1,0:T(8,128)(2,1)S(1)} custom-call(s32[16,128]{1,0:T(8,128)S(1)} %bitcast.7), custom_call_target="tpu_custom_call" | custom-call | flops 16777216 | bytes 4194304 | tf_op jit(solution)/shard_map/signs/pallas_call | solution.py:207
  17.0 0.0 collective-permute-done.3.refs_8_
  17.0 0.0 collective-permute-done.2.refs_6_
  17.0 2.2 %collective-permute-done.1.refs_4_ = f32[72,256]{1,0:T(8,128)S(1)} collective-permute-done((f32[72,256]{1,0:T(8,128)S(1)}, f32[72,256]{1,0:T(8,128)S(1)}, u32[]{:S(2)}, u32[]{:S(2)}) %collective-permute-start.1) | collective-permute-done | bytes 73760 | tf_op jit(solution)/shard_map/ppermute | solution.py:356
  19.2 0.0 collective-permute-done.refs_2_
  19.2 0.0 collective-permute-done.4.seed_ref.refs_1_
  19.2 0.0 collective-permute-start.5
  19.2 0.5 %collective-permute-start.6 = (f32[72,256]{1,0:T(8,128)S(1)}, f32[72,256]{1,0:T(8,128)S(1)}, u32[]{:S(2)}, u32[]{:S(2)}) collective-permute-start(f32[72,256]{1,0:T(8,128)S(1)} %collective-permute-done.1.refs_4_), channel_id=1, source_target_pairs={{0,1},{1,0},{2,3},{3,2},{4,5},{5,4},{6,7},{7,6},{8,9},{9,8},{10,11... | collective-permute-start | bytes 221192 | tf_op jit(solution)/shard_map/ppermute | solution.py:364
  19.7 0.1 collective-permute-start.7
  19.8 0.4 %collective-permute-start.8 = (f32[24,256]{1,0:T(8,128)S(1)}, f32[24,256]{1,0:T(8,128)S(1)}, u32[]{:S(2)}, u32[]{:S(2)}) collective-permute-start(f32[24,256]{1,0:T(8,128)S(1)} %collective-permute-done.3.refs_8_), channel_id=1, source_target_pairs={{0,1},{1,0},{2,3},{3,2},{4,5},{5,4},{6,7},{7,6},{8,9},{9,8},{10,11... | collective-permute-start | bytes 73736 | tf_op jit(solution)/shard_map/ppermute | solution.py:364
  20.3 2.2 %signs.3.refs_11_ = bf16[4,2048,256]{2,1,0:T(8,128)(2,1)S(1)} custom-call(f32[112,256]{1,0:T(8,128)S(1)} %collective-permute-done.4.seed_ref.refs_1_), custom_call_target="tpu_custom_call" | custom-call | flops 16777216 | bytes 4194304 | tf_op jit(solution)/shard_map/signs/pallas_call | solution.py:207
  22.5 0.0 collective-permute-done.8.refs_9_
  22.5 0.0 collective-permute-done.5.refs_3_
  22.5 0.0 collective-permute-done.6.refs_5_
  22.5 0.0 collective-permute-done.7.refs_7_
  22.5 0.0 copy-done.1
  22.5 3.2 %partial_scores.1 = (f32[32,128]{1,0:T(8,128)S(1)}, f32[32,128]{1,0:T(8,128)S(1)}) custom-call(f32[112,256]{1,0:T(8,128)S(1)} %get-tuple-element.16.refs_0_, f32[112,256]{1,0:T(8,128)S(1)} %collective-permute-done.4.seed_ref.refs_1_, f32[72,256]{1,0:T(8,128)S(1)} %collective-permute-done.refs_2_, f32[72,256]{1,0:T(8,128)S(1)} %collective-permute-done.5.refs_3_, ...), custom_call_target="tpu_custom_call" | custom-call | flops 2415919104 | bytes 8388608 | tf_op jit(solution)/shard_map/partial_scores/pallas_call | solution.py:309
  25.7 0.1 collective-permute-start.9
  25.8 1.1 %collective-permute-done.9 = f32[32,128]{1,0:T(8,128)S(1)} collective-permute-done((f32[32,128]{1,0:T(8,128)S(1)}, f32[32,128]{1,0:T(8,128)S(1)}, u32[]{:S(2)}, u32[]{:S(2)}) %collective-permute-start.9) | collective-permute-done | bytes 16416 | tf_op jit(solution)/shard_map/ppermute | solution.py:375
  26.9 0.6 %add_multiply_fusion = f32[32,128]{1,0:T(8,128)} fusion(f32[32,128]{1,0:T(8,128)S(1)} %get-tuple-element.25, f32[32,128]{1,0:T(8,128)S(1)} %collective-permute-done.9), kind=kLoop, calls=%fused_computation | loop fusion | flops 8192 | bytes 49152 | tf_op jit(solution)/shard_map/mul | solution.py:376
Async XLA Ops:
  0.0 14.7 %copy-start = (s32[2048]{0:T(1024)S(1)}, s32[2048]{0:T(1024)}, u32[]{:S(2)}) copy-start(s32[2048]{0:T(1024)} %param.16) | copy-start | bytes 24580
  7.3 12.0 %collective-permute-start.4 = (f32[112,256]{1,0:T(8,128)S(1)}, f32[112,256]{1,0:T(8,128)S(1)}, u32[]{:S(2)}, u32[]{:S(2)}) collective-permute-start(f32[112,256]{1,0:T(8,128)S(1)} %get-tuple-element.16.refs_0_), channel_id=1, source_target_pairs={{0,1},{1,0},{2,3},{3,2},{4,5},{5,4},{6,7},{7,6},{8,9},{9,8},{10,11... | collective-permute-start | bytes 344072 | tf_op jit(solution)/shard_map/ppermute | solution.py:358
  7.8 9.2 %collective-permute-start.2 = (f32[72,256]{1,0:T(8,128)S(1)}, f32[72,256]{1,0:T(8,128)S(1)}, u32[]{:S(2)}, u32[]{:S(2)}) collective-permute-start(f32[72,256]{1,0:T(8,128)S(1)} %get-tuple-element.17), channel_id=1, source_target_pairs={{0,12},{4,8},{8,4},{12,0},{1,13},{5,9},{9,5},{13,1},{2,14},{6,10},... | collective-permute-start | bytes 221192 | tf_op jit(solution)/shard_map/ppermute | solution.py:356
  12.5 6.8 %collective-permute-start.1 = (f32[72,256]{1,0:T(8,128)S(1)}, f32[72,256]{1,0:T(8,128)S(1)}, u32[]{:S(2)}, u32[]{:S(2)}) collective-permute-start(f32[72,256]{1,0:T(8,128)S(1)} %get-tuple-element.17), channel_id=1, source_target_pairs={{0,8},{4,12},{8,0},{12,4},{1,9},{5,13},{9,1},{13,5},{2,10},{6,14},... | collective-permute-start | bytes 221192 | tf_op jit(solution)/shard_map/ppermute | solution.py:356
  12.5 6.8 %collective-permute-start = (f32[72,256]{1,0:T(8,128)S(1)}, f32[72,256]{1,0:T(8,128)S(1)}, u32[]{:S(2)}, u32[]{:S(2)}) collective-permute-start(f32[72,256]{1,0:T(8,128)S(1)} %get-tuple-element.17), channel_id=1, source_target_pairs={{0,4},{4,0},{8,12},{12,8},{1,5},{5,1},{9,13},{13,9},{2,6},{6,2},{1... | collective-permute-start | bytes 221192 | tf_op jit(solution)/shard_map/ppermute | solution.py:356
  13.1 9.4 %copy-start.1 = (f32[2048]{0:T(1024)S(1)}, f32[2048]{0:T(1024)}, u32[]{:S(2)}) copy-start(f32[2048]{0:T(1024)} %param.17) | copy-start | bytes 24580
  13.1 3.9 %collective-permute-start.3 = (f32[24,256]{1,0:T(8,128)S(1)}, f32[24,256]{1,0:T(8,128)S(1)}, u32[]{:S(2)}, u32[]{:S(2)}) collective-permute-start(f32[24,256]{1,0:T(8,128)S(1)} %get-tuple-element.18), channel_id=1, source_target_pairs={{0,2},{2,0},{1,3},{3,1},{4,6},{6,4},{5,7},{7,5},{8,10},{10,8},{9,1... | collective-permute-start | bytes 73736 | tf_op jit(solution)/shard_map/ppermute | solution.py:357
  19.2 3.3 %collective-permute-start.5 = (f32[72,256]{1,0:T(8,128)S(1)}, f32[72,256]{1,0:T(8,128)S(1)}, u32[]{:S(2)}, u32[]{:S(2)}) collective-permute-start(f32[72,256]{1,0:T(8,128)S(1)} %collective-permute-done.refs_2_), channel_id=1, source_target_pairs={{0,1},{1,0},{2,3},{3,2},{4,5},{5,4},{6,7},{7,6},{8,9},{9,8},{10,11... | collective-permute-start | bytes 221192 | tf_op jit(solution)/shard_map/ppermute | solution.py:364
  19.2 3.3 %collective-permute-start.6 = (f32[72,256]{1,0:T(8,128)S(1)}, f32[72,256]{1,0:T(8,128)S(1)}, u32[]{:S(2)}, u32[]{:S(2)}) collective-permute-start(f32[72,256]{1,0:T(8,128)S(1)} %collective-permute-done.1.refs_4_), channel_id=1, source_target_pairs={{0,1},{1,0},{2,3},{3,2},{4,5},{5,4},{6,7},{7,6},{8,9},{9,8},{10,11... | collective-permute-start | bytes 221192 | tf_op jit(solution)/shard_map/ppermute | solution.py:364
  19.7 2.8 %collective-permute-start.7 = (f32[72,256]{1,0:T(8,128)S(1)}, f32[72,256]{1,0:T(8,128)S(1)}, u32[]{:S(2)}, u32[]{:S(2)}) collective-permute-start(f32[72,256]{1,0:T(8,128)S(1)} %collective-permute-done.2.refs_6_), channel_id=1, source_target_pairs={{0,1},{1,0},{2,3},{3,2},{4,5},{5,4},{6,7},{7,6},{8,9},{9,8},{10,11... | collective-permute-start | bytes 221192 | tf_op jit(solution)/shard_map/ppermute | solution.py:364
  19.8 2.7 %collective-permute-start.8 = (f32[24,256]{1,0:T(8,128)S(1)}, f32[24,256]{1,0:T(8,128)S(1)}, u32[]{:S(2)}, u32[]{:S(2)}) collective-permute-start(f32[24,256]{1,0:T(8,128)S(1)} %collective-permute-done.3.refs_8_), channel_id=1, source_target_pairs={{0,1},{1,0},{2,3},{3,2},{4,5},{5,4},{6,7},{7,6},{8,9},{9,8},{10,11... | collective-permute-start | bytes 73736 | tf_op jit(solution)/shard_map/ppermute | solution.py:364
  25.7 1.2 %collective-permute-start.9 = (f32[32,128]{1,0:T(8,128)S(1)}, f32[32,128]{1,0:T(8,128)S(1)}, u32[]{:S(2)}, u32[]{:S(2)}) collective-permute-start(f32[32,128]{1,0:T(8,128)S(1)} %get-tuple-element.26), channel_id=1, source_target_pairs={{0,1},{1,0},{2,3},{3,2},{4,5},{5,4},{6,7},{7,6},{8,9},{9,8},{10,11... | collective-permute-start | bytes 49160 | tf_op jit(solution)/shard_map/ppermute | solution.py:375

commit v4 on v3

--- a/solution.py
+++ b/solution.py
@@ -53,18 +53,6 @@
     test_count = test_hbm.shape[0]
     half = weight.shape[2]
     blocks = (train_count + test_count) // block
-    weight_copy = pltpu.make_async_copy(weight_hbm, weight, weight_sem)
-    weight_copy.start()
-
-    def fetch(b):
-        source = train_hbm if b < train_count // block else test_hbm
-        offset = b * block if b < train_count // block else b * block - train_count
-        return pltpu.make_async_copy(
-            source.at[pl.ds(offset, block)], rows.at[pl.ds(b * block, block)], row_sem.at[b]
-        )
-
-    for b in range(min(AHEAD, blocks)):
-        fetch(b).start()
     small = [
         pltpu.make_async_copy(source, target, small_sem.at[i])
         for i, (source, target) in enumerate(
@@ -79,6 +67,18 @@
     ]
     for copy in small:
         copy.start()
+    weight_copy = pltpu.make_async_copy(weight_hbm, weight, weight_sem)
+    weight_copy.start()
+
+    def fetch(b):
+        source = train_hbm if b < train_count // block else test_hbm
+        offset = b * block if b < train_count // block else b * block - train_count
+        return pltpu.make_async_copy(
+            source.at[pl.ds(offset, block)], rows.at[pl.ds(b * block, block)], row_sem.at[b]
+        )
+
+    for b in range(min(AHEAD, blocks)):
+        fetch(b).start()
     weight_copy.wait()
     for copy in small:
         copy.wait()
@@ -171,11 +171,11 @@
     )
 
 
-def sign_kernel(packed, seed_ref, sign_ref, turned, column_ref):
+def sign_kernel(packed, classes, seed_ref, sign_ref, turned, column_ref):
     proj_index = lax.axis_index("proj")
     parts, rows, part_width = sign_ref.shape
     count = parts * part_width
-    chunks = rows // 128
+    chunks = rows // ((128 // NCLS) * len(classes))
     per_chunk = 128 // NCLS
     if packed:
         first = seed_ref.shape[0] - chunks
@@ -191,21 +191,22 @@
             lax.broadcasted_iota(jnp.int32, column_ref.shape, 1) + proj_index * count
         ) * MIX_COLUMN
 
-    for k in range(NCLS):
+    for k in classes:
         seeds = turned[pl.ds(k, per_chunk, stride=NCLS), :]
         for h in range(chunks):
             mixed = (seeds[:, h : h + 1] ^ column_ref[...]) * MIX_FIRST
             mixed = (mixed ^ (mixed >> 13)) * MIX_LAST
             signs = jnp.where(mixed < 0, -1.0, 1.0).astype(jnp.bfloat16)
-            at = (k * chunks + h) * per_chunk
+            at = ((k - classes[0]) * chunks + h) * per_chunk
             for n in range(parts):
                 sign_ref[n, pl.ds(at, per_chunk), :] = signs[:, n * part_width : (n + 1) * part_width]
 
 
-def sign_block(seeds, rows, count):
+def sign_block(seeds, channels, count, classes):
+    rows = channels * len(classes)
     parts = count // 256
     return pl.pallas_call(
-        functools.partial(sign_kernel, seeds.dtype == jnp.float32),
+        functools.partial(sign_kernel, seeds.dtype == jnp.float32, classes),
         out_shape=jax.ShapeDtypeStruct((parts, rows, 256), jnp.bfloat16),
         in_specs=[VMEM],
         out_specs=VMEM,
@@ -221,9 +222,10 @@
 def score_kernel(train_blocks, test_blocks, train_count, test_count, *refs):
     far = train_blocks + test_blocks - 2
     packets = refs[: 2 * far + 2]
-    own_signs, other_signs, precond_ref, keep_ref, send_ref, train_feat, test_feat = refs[2 * far + 2 :]
+    signs = refs[2 * far + 2 : -5]
+    precond_ref, keep_ref, send_ref, train_feat, test_feat = refs[-5:]
     proj_index = lax.axis_index("proj")
-    parts, half_rows, part_width = own_signs.shape
+    parts, _, part_width = signs[0].shape
     train_rows = train_blocks * train_count
     gradients = []
     row_weights = []
@@ -261,7 +263,7 @@
     for n in range(parts):
         projected = jnp.dot(
             gradient,
-            jnp.concatenate([own_signs[n], other_signs[n]], axis=0),
+            jnp.concatenate([value[n] for value in signs], axis=0),
             preferred_element_type=jnp.float32,
         )
         columns = pl.ds(n * part_width, part_width)
@@ -301,15 +303,16 @@
     return [(i, (i + shift) % count) for i in range(count)]
 
 
-def partial_scores(packets, own_signs, other_signs, precond, train_blocks, test_blocks, train_count, test_count):
-    parts, rows, part_width = own_signs.shape
+def partial_scores(packets, signs, precond, train_blocks, test_blocks, train_count, test_count):
+    parts, _, part_width = signs[0].shape
+    rows = sum(value.shape[1] for value in signs)
     out_rows = test_blocks * test_count
     out_cols = train_blocks * train_count
     total_rows = out_rows + out_cols
     return pl.pallas_call(
         functools.partial(score_kernel, train_blocks, test_blocks, train_count, test_count),
         out_shape=(jax.ShapeDtypeStruct((out_rows, out_cols // 2), jnp.float32),) * 2,
-        in_specs=[VMEM] * (len(packets) + 3),
+        in_specs=[VMEM] * (len(packets) + len(signs) + 1),
         out_specs=(VMEM, VMEM),
         scratch_shapes=[
             pltpu.VMEM((train_blocks, train_count, parts * part_width), jnp.bfloat16),
@@ -317,12 +320,12 @@
         ],
         compiler_params=pltpu.CompilerParams(vmem_limit_bytes=40 * MIB),
         cost_estimate=pl.CostEstimate(
-            flops=4 * total_rows * rows * parts * part_width,
-            bytes_accessed=4 * rows * parts * part_width,
+            flops=2 * total_rows * rows * parts * part_width,
+            bytes_accessed=2 * rows * parts * part_width,
             transcendentals=0,
         ),
         name="partial_scores",
-    )(*packets, own_signs, other_signs, precond)
+    )(*packets, *signs, precond)
 
 
 def shards(
@@ -356,16 +359,28 @@
     far = [lax.ppermute(train_packet, "train", _pairs(shift, train_blocks)) for shift in range(1, train_blocks)]
     far += [lax.ppermute(test_packet, "test", _pairs(shift, test_blocks)) for shift in range(1, test_blocks)]
     other_packet = lax.ppermute(own_packet, "proj", swap)
-    own_signs = sign_block(seeds, sign_seeds.shape[0], count)
-    *far, own_signs, other_packet = lax.optimization_barrier((*far, own_signs, other_packet))
-    other_signs = sign_block(other_packet, sign_seeds.shape[0], count)
+    early = [i for i in range(len(far)) if i >= train_blocks - 1 or i == train_blocks - 2]
+    late = [i for i in range(len(far)) if i not in early]
+    channels = sign_seeds.shape[0] // NCLS
+    classes = tuple(range(NCLS))
+    own_signs = sign_block(seeds, channels, count, classes)
+    far_other = [None] * len(far)
+    *held, own_signs, other_packet = lax.optimization_barrier((*(far[i] for i in early), own_signs, other_packet))
+    for i, value in zip(early, held):
+        far[i] = value
+        far_other[i] = lax.ppermute(value, "proj", swap)
+    first_signs = sign_block(other_packet, channels, count, classes[: NCLS // 2])
+    *held, first_signs = lax.optimization_barrier((*(far[i] for i in late), first_signs))
+    for i, value in zip(late, held):
+        far[i] = value
+        far_other[i] = lax.ppermute(value, "proj", swap)
+    last_signs = sign_block(other_packet, channels, count, classes[NCLS // 2 :])
     packets = [own_packet, other_packet]
-    for value in far:
-        packets += [value, lax.ppermute(value, "proj", swap)]
+    for value, other in zip(far, far_other):
+        packets += [value, other]
     keep, send = partial_scores(
         packets,
-        own_signs,
-        other_signs,
+        [own_signs, first_signs, last_signs],
         precond.reshape(1, -1),
         train_blocks,
         test_blocks,

time: 27.7 us -> 26.2 us (0.946)
  waiting for transfers between devices: 3.38 us -> 1.81 us
    ppermute x3, waiting for transfers between devices: 2.25 us -> 0.96 us  [shards(): lax.ppermute(train_packet, 'train', _pairs(shift, train_blocks))]
    ppermute x1, starting transfers between devices: 0.09 us -> 0.53 us  [shards(): received = lax.ppermute(send, 'proj', swap)]
    ppermute x4, starting transfers between devices: 1.02 us -> 0.59 us  [shards(): far_other[i] = lax.ppermute(value, 'proj', swap)]
    pallas_call x2 -> x3, Pallas kernels: 4.44 us -> 4.6 us  [sign_block(): pl.pallas_call(functools.partial(sign_kernel, seeds.dtype == jnp.float32,...]
  transfers between devices with their start and end apart: 10 -> 10, of which waited for: 2 -> 2; matrix products, arithmetic and copies ran while one was open for 0% -> 0% of each run, Pallas kernels for 16% -> 18%
where the time goes in v4:
time: 26.2 us; the launch traced here: 26 us
  Pallas kernels  14.9 us (57%)
  starting transfers between devices  8.58 us (33%)
  waiting for transfers between devices  1.81 us (7%)
  other arithmetic  0.61 us (2%)
    pallas_call x1, Pallas kernels, pool(): pl.pallas_call(functools.partial(pool_kernel, block), out_shape=(jax.Shap...  7.17 us
    ppermute x3, starting transfers between devices, shards(): lax.ppermute(train_packet, 'train', _pairs(shift, train_blocks))  5.3 us
    pallas_call x3, Pallas kernels, sign_block(): pl.pallas_call(functools.partial(sign_kernel, seeds.dtype == jnp.float32,...  4.6 us
    pallas_call x1, Pallas kernels, partial_scores(): pl.pallas_call(functools.partial(score_kernel, train_blocks, test_blocks,...  3.16 us
    ppermute x1, starting transfers between devices, shards(): lax.ppermute(test_packet, 'test', _pairs(shift, test_blocks))  1.64 us
    ppermute x3, waiting for transfers between devices, shards(): lax.ppermute(train_packet, 'train', _pairs(shift, train_blocks))  0.96 us
    ppermute x1, waiting for transfers between devices, shards(): received = lax.ppermute(send, 'proj', swap)  0.84 us
    mul x1, other arithmetic, shards(): return (keep + received) * (1.0 / (K * math.sqrt(C)))  0.61 us
  transfers between devices with their start and end apart: 10, of which 2 were waited for; matrix products, arithmetic and copies ran while one was open for 0% of the time, Pallas kernels for 18%

profile of v4, /device:TPU:0, one launch (start us, length us, event | category | flops | bytes accessed | tf_op | source)
XLA Modules:
  0.0 26.0 jit_solution(16832824372996862549)
XLA Ops:
  0.0 0.0 copy-start
  0.0 7.2 %pool.1 = (f32[72,256]{1,0:T(8,128)S(1)}, f32[24,256]{1,0:T(8,128)S(1)}, f32[112,256]{1,0:T(8,128)S(1)}) custom-call(bf16[64,64,512]{2,1,0:T(8,128)(2,1)} %train_hbm.1, bf16[16,64,512]{2,1,0:T(8,128)(2,1)} %test_hbm.1, bf16[3,512,256]{2,1,0:T(8,128)(2,1)} %weight_hbm.1, f32[1,256]{1,0:T(1,128)} %bitcast.10, f32[8,256]{1,0:T(8,128)} %bitcast.9, ...), custom_call_target="tpu_custom_call" | custom-call | tf_op jit(solution)/shard_map/pool/pallas_call | solution.py:142
  7.2 0.5 %collective-permute-start.2 = (f32[112,256]{1,0:T(8,128)S(1)}, f32[112,256]{1,0:T(8,128)S(1)}, u32[]{:S(2)}, u32[]{:S(2)}) collective-permute-start(f32[112,256]{1,0:T(8,128)S(1)} %get-tuple-element.17.refs_0_), channel_id=1, source_target_pairs={{0,1},{1,0},{2,3},{3,2},{4,5},{5,4},{6,7},{7,6},{8,9},{9,8},{10,11... | collective-permute-start | bytes 344072 | tf_op jit(solution)/shard_map/ppermute | solution.py:361
  7.7 4.7 %collective-permute-start = (f32[72,256]{1,0:T(8,128)S(1)}, f32[72,256]{1,0:T(8,128)S(1)}, u32[]{:S(2)}, u32[]{:S(2)}) collective-permute-start(f32[72,256]{1,0:T(8,128)S(1)} %get-tuple-element.18), channel_id=1, source_target_pairs={{0,12},{4,8},{8,4},{12,0},{1,13},{5,9},{9,5},{13,1},{2,14},{6,10},... | collective-permute-start | bytes 221192 | tf_op jit(solution)/shard_map/ppermute | solution.py:359
  12.4 0.0 collective-permute-start.4
  12.4 0.6 %collective-permute-start.3 = (f32[72,256]{1,0:T(8,128)S(1)}, f32[72,256]{1,0:T(8,128)S(1)}, u32[]{:S(2)}, u32[]{:S(2)}) collective-permute-start(f32[72,256]{1,0:T(8,128)S(1)} %get-tuple-element.18), channel_id=1, source_target_pairs={{0,4},{4,0},{8,12},{12,8},{1,5},{5,1},{9,13},{13,9},{2,6},{6,2},{1... | collective-permute-start | bytes 221192 | tf_op jit(solution)/shard_map/ppermute | solution.py:359
  13.0 0.0 copy-start.1
  13.0 1.6 %collective-permute-start.1 = (f32[24,256]{1,0:T(8,128)S(1)}, f32[24,256]{1,0:T(8,128)S(1)}, u32[]{:S(2)}, u32[]{:S(2)}) collective-permute-start(f32[24,256]{1,0:T(8,128)S(1)} %get-tuple-element.19), channel_id=1, source_target_pairs={{0,2},{2,0},{1,3},{3,1},{4,6},{6,4},{5,7},{7,5},{8,10},{10,8},{9,1... | collective-permute-start | bytes 73736 | tf_op jit(solution)/shard_map/ppermute | solution.py:360
  14.7 0.0 copy-done
  14.7 2.2 %signs.3.refs_10_ = bf16[4,2048,256]{2,1,0:T(8,128)(2,1)S(1)} custom-call(s32[16,128]{1,0:T(8,128)S(1)} %bitcast.7), custom_call_target="tpu_custom_call" | custom-call | flops 16777216 | bytes 4194304 | tf_op jit(solution)/shard_map/signs/pallas_call | solution.py:208
  16.9 0.0 collective-permute-done.1.refs_8_
  16.9 0.0 collective-permute-done.refs_6_
  16.9 0.0 collective-permute-done.2.seed_ref.refs_1_
  16.9 0.1 collective-permute-start.7
  17.0 1.2 %signs.4.refs_11_ = bf16[4,1024,256]{2,1,0:T(8,128)(2,1)S(1)} custom-call(f32[112,256]{1,0:T(8,128)S(1)} %collective-permute-done.2.seed_ref.refs_1_), custom_call_target="tpu_custom_call" | custom-call | flops 8388608 | bytes 2097152 | tf_op jit(solution)/shard_map/signs/pallas_call | solution.py:208
  18.2 0.9 %collective-permute-done.4.refs_4_ = f32[72,256]{1,0:T(8,128)S(1)} collective-permute-done((f32[72,256]{1,0:T(8,128)S(1)}, f32[72,256]{1,0:T(8,128)S(1)}, u32[]{:S(2)}, u32[]{:S(2)}) %collective-permute-start.4) | collective-permute-done | bytes 73760 | tf_op jit(solution)/shard_map/ppermute | solution.py:359
  19.1 0.0 collective-permute-done.3.refs_2_
  19.1 0.0 collective-permute-start.5
  19.1 0.5 %collective-permute-start.6 = (f32[72,256]{1,0:T(8,128)S(1)}, f32[72,256]{1,0:T(8,128)S(1)}, u32[]{:S(2)}, u32[]{:S(2)}) collective-permute-start(f32[72,256]{1,0:T(8,128)S(1)} %collective-permute-done.4.refs_4_), channel_id=1, source_target_pairs={{0,1},{1,0},{2,3},{3,2},{4,5},{5,4},{6,7},{7,6},{8,9},{9,8},{10,11... | collective-permute-start | bytes 221192 | tf_op jit(solution)/shard_map/ppermute | solution.py:376
  19.7 0.0 collective-permute-start.8
  19.7 1.2 %signs.5.refs_12_ = bf16[4,1024,256]{2,1,0:T(8,128)(2,1)S(1)} custom-call(f32[112,256]{1,0:T(8,128)S(1)} %collective-permute-done.2.seed_ref.refs_1_), custom_call_target="tpu_custom_call" | custom-call | flops 8388608 | bytes 2097152 | tf_op jit(solution)/shard_map/signs/pallas_call | solution.py:208
  20.9 0.0 collective-permute-done.8.refs_9_
  20.9 0.0 collective-permute-done.7.refs_7_
  20.9 0.0 collective-permute-done.5.refs_3_
  20.9 0.0 collective-permute-done.6.refs_5_
  20.9 0.0 copy-done.1
  20.9 3.2 %partial_scores.1 = (f32[32,128]{1,0:T(8,128)S(1)}, f32[32,128]{1,0:T(8,128)S(1)}) custom-call(f32[112,256]{1,0:T(8,128)S(1)} %get-tuple-element.17.refs_0_, f32[112,256]{1,0:T(8,128)S(1)} %collective-permute-done.2.seed_ref.refs_1_, f32[72,256]{1,0:T(8,128)S(1)} %collective-permute-done.3.refs_2_, f32[72,256]{1,0:T(8,128)S(1)} %collective-permute-done.5.refs_3_, ...), custom_call_target="tpu_custom_call" | custom-call | flops 2415919104 | bytes 8388608 | tf_op jit(solution)/shard_map/partial_scores/pallas_call | solution.py:312
  24.1 0.5 %collective-permute-start.9 = (f32[32,128]{1,0:T(8,128)S(1)}, f32[32,128]{1,0:T(8,128)S(1)}, u32[]{:S(2)}, u32[]{:S(2)}) collective-permute-start(f32[32,128]{1,0:T(8,128)S(1)} %get-tuple-element.28), channel_id=1, source_target_pairs={{0,1},{1,0},{2,3},{3,2},{4,5},{5,4},{6,7},{7,6},{8,9},{9,8},{10,11... | collective-permute-start | bytes 49160 | tf_op jit(solution)/shard_map/ppermute | solution.py:390
  24.6 0.8 %collective-permute-done.9 = f32[32,128]{1,0:T(8,128)S(1)} collective-permute-done((f32[32,128]{1,0:T(8,128)S(1)}, f32[32,128]{1,0:T(8,128)S(1)}, u32[]{:S(2)}, u32[]{:S(2)}) %collective-permute-start.9) | collective-permute-done | bytes 16416 | tf_op jit(solution)/shard_map/ppermute | solution.py:390
  25.4 0.6 %add_multiply_fusion = f32[32,128]{1,0:T(8,128)} fusion(f32[32,128]{1,0:T(8,128)S(1)} %get-tuple-element.27, f32[32,128]{1,0:T(8,128)S(1)} %collective-permute-done.9), kind=kLoop, calls=%fused_computation | loop fusion | flops 8192 | bytes 49152 | tf_op jit(solution)/shard_map/mul | solution.py:391
Async XLA Ops:
  0.0 14.7 %copy-start = (s32[2048]{0:T(1024)S(1)}, s32[2048]{0:T(1024)}, u32[]{:S(2)}) copy-start(s32[2048]{0:T(1024)} %param.16) | copy-start | bytes 24580
  7.2 9.7 %collective-permute-start.2 = (f32[112,256]{1,0:T(8,128)S(1)}, f32[112,256]{1,0:T(8,128)S(1)}, u32[]{:S(2)}, u32[]{:S(2)}) collective-permute-start(f32[112,256]{1,0:T(8,128)S(1)} %get-tuple-element.17.refs_0_), channel_id=1, source_target_pairs={{0,1},{1,0},{2,3},{3,2},{4,5},{5,4},{6,7},{7,6},{8,9},{9,8},{10,11... | collective-permute-start | bytes 344072 | tf_op jit(solution)/shard_map/ppermute | solution.py:361
  7.7 9.2 %collective-permute-start = (f32[72,256]{1,0:T(8,128)S(1)}, f32[72,256]{1,0:T(8,128)S(1)}, u32[]{:S(2)}, u32[]{:S(2)}) collective-permute-start(f32[72,256]{1,0:T(8,128)S(1)} %get-tuple-element.18), channel_id=1, source_target_pairs={{0,12},{4,8},{8,4},{12,0},{1,13},{5,9},{9,5},{13,1},{2,14},{6,10},... | collective-permute-start | bytes 221192 | tf_op jit(solution)/shard_map/ppermute | solution.py:359
  12.4 6.8 %collective-permute-start.4 = (f32[72,256]{1,0:T(8,128)S(1)}, f32[72,256]{1,0:T(8,128)S(1)}, u32[]{:S(2)}, u32[]{:S(2)}) collective-permute-start(f32[72,256]{1,0:T(8,128)S(1)} %get-tuple-element.18), channel_id=1, source_target_pairs={{0,8},{4,12},{8,0},{12,4},{1,9},{5,13},{9,1},{13,5},{2,10},{6,14},... | collective-permute-start | bytes 221192 | tf_op jit(solution)/shard_map/ppermute | solution.py:359
  12.4 6.8 %collective-permute-start.3 = (f32[72,256]{1,0:T(8,128)S(1)}, f32[72,256]{1,0:T(8,128)S(1)}, u32[]{:S(2)}, u32[]{:S(2)}) collective-permute-start(f32[72,256]{1,0:T(8,128)S(1)} %get-tuple-element.18), channel_id=1, source_target_pairs={{0,4},{4,0},{8,12},{12,8},{1,5},{5,1},{9,13},{13,9},{2,6},{6,2},{1... | collective-permute-start | bytes 221192 | tf_op jit(solution)/shard_map/ppermute | solution.py:359
  13.0 7.9 %copy-start.1 = (f32[2048]{0:T(1024)S(1)}, f32[2048]{0:T(1024)}, u32[]{:S(2)}) copy-start(f32[2048]{0:T(1024)} %param.17) | copy-start | bytes 24580
  13.0 3.9 %collective-permute-start.1 = (f32[24,256]{1,0:T(8,128)S(1)}, f32[24,256]{1,0:T(8,128)S(1)}, u32[]{:S(2)}, u32[]{:S(2)}) collective-permute-start(f32[24,256]{1,0:T(8,128)S(1)} %get-tuple-element.19), channel_id=1, source_target_pairs={{0,2},{2,0},{1,3},{3,1},{4,6},{6,4},{5,7},{7,5},{8,10},{10,8},{9,1... | collective-permute-start | bytes 73736 | tf_op jit(solution)/shard_map/ppermute | solution.py:360
  16.9 4.0 %collective-permute-start.7 = (f32[72,256]{1,0:T(8,128)S(1)}, f32[72,256]{1,0:T(8,128)S(1)}, u32[]{:S(2)}, u32[]{:S(2)}) collective-permute-start(f32[72,256]{1,0:T(8,128)S(1)} %collective-permute-done.refs_6_), channel_id=1, source_target_pairs={{0,1},{1,0},{2,3},{3,2},{4,5},{5,4},{6,7},{7,6},{8,9},{9,8},{10,11... | collective-permute-start | bytes 221192 | tf_op jit(solution)/shard_map/ppermute | solution.py:371
  19.1 1.7 %collective-permute-start.5 = (f32[72,256]{1,0:T(8,128)S(1)}, f32[72,256]{1,0:T(8,128)S(1)}, u32[]{:S(2)}, u32[]{:S(2)}) collective-permute-start(f32[72,256]{1,0:T(8,128)S(1)} %collective-permute-done.3.refs_2_), channel_id=1, source_target_pairs={{0,1},{1,0},{2,3},{3,2},{4,5},{5,4},{6,7},{7,6},{8,9},{9,8},{10,11... | collective-permute-start | bytes 221192 | tf_op jit(solution)/shard_map/ppermute | solution.py:376
  19.1 1.7 %collective-permute-start.6 = (f32[72,256]{1,0:T(8,128)S(1)}, f32[72,256]{1,0:T(8,128)S(1)}, u32[]{:S(2)}, u32[]{:S(2)}) collective-permute-start(f32[72,256]{1,0:T(8,128)S(1)} %collective-permute-done.4.refs_4_), channel_id=1, source_target_pairs={{0,1},{1,0},{2,3},{3,2},{4,5},{5,4},{6,7},{7,6},{8,9},{9,8},{10,11... | collective-permute-start | bytes 221192 | tf_op jit(solution)/shard_map/ppermute | solution.py:376
  19.7 1.2 %collective-permute-start.8 = (f32[24,256]{1,0:T(8,128)S(1)}, f32[24,256]{1,0:T(8,128)S(1)}, u32[]{:S(2)}, u32[]{:S(2)}) collective-permute-start(f32[24,256]{1,0:T(8,128)S(1)} %collective-permute-done.1.refs_8_), channel_id=1, source_target_pairs={{0,1},{1,0},{2,3},{3,2},{4,5},{5,4},{6,7},{7,6},{8,9},{9,8},{10,11... | collective-permute-start | bytes 73736 | tf_op jit(solution)/shard_map/ppermute | solution.py:371
  24.1 1.4 %collective-permute-start.9 = (f32[32,128]{1,0:T(8,128)S(1)}, f32[32,128]{1,0:T(8,128)S(1)}, u32[]{:S(2)}, u32[]{:S(2)}) collective-permute-start(f32[32,128]{1,0:T(8,128)S(1)} %get-tuple-element.28), channel_id=1, source_target_pairs={{0,1},{1,0},{2,3},{3,2},{4,5},{5,4},{6,7},{7,6},{8,9},{9,8},{10,11... | collective-permute-start | bytes 49160 | tf_op jit(solution)/shard_map/ppermute | solution.py:390

commit v5 on v4

--- a/solution.py
+++ b/solution.py
@@ -18,9 +18,80 @@
 MIX_LAST = MIX_LAST - (1 << 32) if MIX_LAST >= 1 << 31 else MIX_LAST
 MIB = 2**20
 AHEAD = 3
+EARLY_CLASSES = tuple(range(1))
 
 VMEM = pl.BlockSpec(memory_space=pltpu.VMEM)
 HBM = pl.BlockSpec(memory_space=pltpu.HBM)
+
+
+def write_signs(classes, seeds, sign_ref, turned, column_ref):
+    proj_index = lax.axis_index("proj")
+    parts, rows, part_width = sign_ref.shape
+    count = parts * part_width
+    per_chunk = 128 // NCLS
+    chunks = rows // (per_chunk * len(classes))
+    turned[:, pl.ds(0, chunks)] = seeds.T
+
+    @pl.when(proj_index >= 0)
+    def _():
+        column_ref[...] = (
+            lax.broadcasted_iota(jnp.int32, column_ref.shape, 1) + proj_index * count
+        ) * MIX_COLUMN
+
+    for k in classes:
+        class_seeds = turned[pl.ds(k, per_chunk, stride=NCLS), :]
+        for h in range(chunks):
+            mixed = (class_seeds[:, h : h + 1] ^ column_ref[...]) * MIX_FIRST
+            mixed = (mixed ^ (mixed >> 13)) * MIX_LAST
+            signs = jnp.where(mixed < 0, -1.0, 1.0).astype(jnp.bfloat16)
+            at = ((k - classes[0]) * chunks + h) * per_chunk
+            for n in range(parts):
+                sign_ref[n, pl.ds(at, per_chunk), :] = signs[:, n * part_width : (n + 1) * part_width]
+
+
+def power_of_two(exponent):
+    return jnp.exp(exponent * math.log(2.0))
+
+
+def encode_packet(packet, pooled, logits, labels):
+    count = pooled.shape[0]
+    largest = jnp.maximum(jnp.max(jnp.abs(pooled), axis=1, keepdims=True), 1e-30)
+    exponent = jnp.floor(jnp.log(largest) * (1.0 / math.log(2.0)))
+    factor = jnp.ceil(largest * power_of_two(-exponent) * 8192.0)
+    step = factor * (power_of_two(exponent) * (1.0 / (8192.0 * 32767.0)))
+    steps = jnp.clip(jnp.round(pooled * (1.0 / step)), -32767.0, 32767.0)
+    packet[pl.ds(0, count), :] = steps.astype(jnp.int32).astype(jnp.int16)
+    lane = lax.broadcasted_iota(jnp.int32, (count, 128), 1)
+    turned = jnp.where(lane == 1, factor, jnp.where(lane == 2, exponent, 0.0)).T[:NCLS]
+    logit_exponent = jnp.ceil(
+        jnp.log(jnp.maximum(jnp.max(jnp.abs(logits), axis=0, keepdims=True), 1e-30)) * (1.0 / math.log(2.0))
+    )
+    scaled = logits * (power_of_two(-logit_exponent) * 8192.0)
+    high = jnp.round(scaled)
+    low = jnp.round((scaled - high) * 16384.0)
+    row = lax.broadcasted_iota(jnp.int32, (NCLS, count), 0)
+    facts = jnp.where(row == 0, labels, jnp.where(row == 3, logit_exponent, turned))
+    blank = jnp.zeros((NCLS, 128 - count), jnp.float32)
+    extra = jnp.concatenate(
+        [
+            jnp.concatenate([high, blank, facts, blank], axis=1),
+            jnp.concatenate([low, blank, jnp.zeros((NCLS, 128), jnp.float32)], axis=1),
+        ],
+        axis=0,
+    )
+    packet[pl.ds(count, 2 * NCLS), :] = extra.astype(jnp.int32).astype(jnp.int16)
+
+
+def decode_packet(packet):
+    count = packet.shape[0] - 2 * NCLS
+    steps = packet[pl.ds(0, count), :].astype(jnp.int32).astype(jnp.float32)
+    extra = packet[pl.ds(count, 2 * NCLS), :].astype(jnp.int32).astype(jnp.float32)
+    facts = extra[:NCLS, 128:]
+    step = facts[1:2] * (power_of_two(facts[2:3]) * (1.0 / (8192.0 * 32767.0)))
+    logits = (extra[:NCLS, :128] + extra[NCLS:, :128] * (1.0 / 16384.0)) * (
+        power_of_two(facts[3:4]) * (1.0 / 8192.0)
+    )
+    return steps, step, logits, facts[0:1]
 
 
 def pool_kernel(
@@ -36,6 +107,7 @@
     train_packet,
     test_packet,
     own_packet,
+    sign_ref,
     rows,
     weight,
     pooled,
@@ -44,6 +116,8 @@
     train_label,
     test_label,
     seeds,
+    turned,
+    column_ref,
     row_sem,
     weight_sem,
     small_sem,
@@ -79,9 +153,10 @@
 
     for b in range(min(AHEAD, blocks)):
         fetch(b).start()
-    weight_copy.wait()
     for copy in small:
         copy.wait()
+    write_signs(EARLY_CLASSES, seeds[...], sign_ref, turned, column_ref)
+    weight_copy.wait()
     gain = gain_row[...]
     own_start = pl.multiple_of(proj_index * half, half)
 
@@ -124,16 +199,16 @@
             preferred_element_type=jnp.float32,
         )
         labels = jnp.broadcast_to(label_ref[...].astype(jnp.float32), (NCLS, count))
-        for target, first in ((packet, 0), (own_packet, at)):
-            target[pl.ds(first, count), :] = own
-            target[pl.ds(first + count, NCLS), pl.ds(0, count)] = logits
-            target[pl.ds(first + count, NCLS), pl.ds(128, count)] = labels
+        own_packet[pl.ds(at, count), :] = own
+        own_packet[pl.ds(at + count, NCLS), pl.ds(0, count)] = logits
+        own_packet[pl.ds(at + count, NCLS), pl.ds(128, count)] = labels
+        encode_packet(packet, own, logits, labels)
         at += count + NCLS
     own_packet[pl.ds(at, seeds.shape[0]), pl.ds(0, 128)] = (seeds[...] >> 15).astype(jnp.float32)
     own_packet[pl.ds(at, seeds.shape[0]), pl.ds(128, 128)] = (seeds[...] & 32767).astype(jnp.float32)
 
 
-def pool(train_windows, test_windows, weight, gain, cls_t, train_labels, test_labels, seeds):
+def pool(train_windows, test_windows, weight, gain, cls_t, train_labels, test_labels, seeds, count):
     block = 16
     train_count, length, width = train_windows.shape
     test_count = test_windows.shape[0]
@@ -142,12 +217,13 @@
     return pl.pallas_call(
         functools.partial(pool_kernel, block),
         out_shape=(
-            jax.ShapeDtypeStruct((train_count + NCLS, half), jnp.float32),
-            jax.ShapeDtypeStruct((test_count + NCLS, half), jnp.float32),
+            jax.ShapeDtypeStruct((train_count + 2 * NCLS, half), jnp.int16),
+            jax.ShapeDtypeStruct((test_count + 2 * NCLS, half), jnp.int16),
             jax.ShapeDtypeStruct((total + 2 * NCLS + seeds.shape[0], half), jnp.float32),
+            jax.ShapeDtypeStruct((count // 256, seeds.size // NCLS * len(EARLY_CLASSES), 256), jnp.bfloat16),
         ),
         in_specs=[HBM] * 8,
-        out_specs=(VMEM, VMEM, VMEM),
+        out_specs=(VMEM, VMEM, VMEM, VMEM),
         scratch_shapes=[
             pltpu.VMEM((total, length, width), jnp.bfloat16),
             pltpu.VMEM(weight.shape, jnp.bfloat16),
@@ -157,6 +233,8 @@
             pltpu.VMEM(train_labels.shape, jnp.int32),
             pltpu.VMEM(test_labels.shape, jnp.int32),
             pltpu.VMEM(seeds.shape, jnp.int32),
+            pltpu.VMEM((128, 128), jnp.int32),
+            pltpu.VMEM((128 // NCLS, count), jnp.int32),
             pltpu.SemaphoreType.DMA((total // block,)),
             pltpu.SemaphoreType.DMA,
             pltpu.SemaphoreType.DMA((5,)),
@@ -172,34 +250,14 @@
 
 
 def sign_kernel(packed, classes, seed_ref, sign_ref, turned, column_ref):
-    proj_index = lax.axis_index("proj")
-    parts, rows, part_width = sign_ref.shape
-    count = parts * part_width
-    chunks = rows // ((128 // NCLS) * len(classes))
-    per_chunk = 128 // NCLS
     if packed:
+        chunks = sign_ref.shape[1] // ((128 // NCLS) * len(classes))
         first = seed_ref.shape[0] - chunks
         high = seed_ref[pl.ds(first, chunks), pl.ds(0, 128)].astype(jnp.int32)
         seeds = high * 32768 + seed_ref[pl.ds(first, chunks), pl.ds(128, 128)].astype(jnp.int32)
     else:
         seeds = seed_ref[...]
-    turned[:, pl.ds(0, chunks)] = seeds.T
-
-    @pl.when(proj_index >= 0)
-    def _():
-        column_ref[...] = (
-            lax.broadcasted_iota(jnp.int32, column_ref.shape, 1) + proj_index * count
-        ) * MIX_COLUMN
-
-    for k in classes:
-        seeds = turned[pl.ds(k, per_chunk, stride=NCLS), :]
-        for h in range(chunks):
-            mixed = (seeds[:, h : h + 1] ^ column_ref[...]) * MIX_FIRST
-            mixed = (mixed ^ (mixed >> 13)) * MIX_LAST
-            signs = jnp.where(mixed < 0, -1.0, 1.0).astype(jnp.bfloat16)
-            at = ((k - classes[0]) * chunks + h) * per_chunk
-            for n in range(parts):
-                sign_ref[n, pl.ds(at, per_chunk), :] = signs[:, n * part_width : (n + 1) * part_width]
+    write_signs(classes, seeds, sign_ref, turned, column_ref)
 
 
 def sign_block(seeds, channels, count, classes):
@@ -230,31 +288,34 @@
     gradients = []
     row_weights = []
     for i in range(train_blocks + test_blocks):
-        first = 0
-        if i == 0:
-            mine, theirs = packets[0], packets[1]
-        elif i < train_blocks:
-            mine, theirs = packets[2 * i], packets[2 * i + 1]
-        elif i == train_blocks:
-            mine, theirs = packets[0], packets[1]
-            first = train_count + NCLS
+        count = train_count if i < train_blocks else test_count
+        if i == 0 or i == train_blocks:
+            first = 0 if i == 0 else train_count + NCLS
+            values, logits, steps = [], 0.0, []
+            for packet in packets[:2]:
+                values.append(packet[pl.ds(first, count), :])
+                logits += packet[pl.ds(first + count, NCLS), pl.ds(0, 128)]
+            label = packets[0][pl.ds(first + count, 1), pl.ds(128, 128)]
         else:
-            mine, theirs = packets[2 * (i - 1)], packets[2 * (i - 1) + 1]
-        count = train_count if i < train_blocks else test_count
-        class_rows = pl.ds(first + count, NCLS)
-        logits = mine[class_rows, pl.ds(0, 128)] + theirs[class_rows, pl.ds(0, 128)]
-        label = mine[class_rows, pl.ds(128, 128)]
+            at = 2 * i if i < train_blocks else 2 * (i - 1)
+            decoded = [decode_packet(packet) for packet in packets[at : at + 2]]
+            values = [value for value, _, _, _ in decoded]
+            steps = [step for _, step, _, _ in decoded]
+            logits = decoded[0][2] + decoded[1][2]
+            label = decoded[0][3]
         chance = 1.0 / (1.0 + jnp.exp(-logits))
         classes = lax.broadcasted_iota(jnp.int32, (NCLS, 128), 0).astype(jnp.float32)
         target = jnp.where(label == classes, 1.0, 0.0)
         retain = 1.0 - jnp.sum(chance * target, axis=0, keepdims=True)
-        stacked = jnp.concatenate([chance - target, jnp.broadcast_to(retain, (NCLS, 128))], axis=0)
-        turned = stacked.T[:count]
+        rest = [retain, *steps]
+        rest += [jnp.zeros((NCLS - len(rest), 128), jnp.float32)]
+        turned = jnp.concatenate([chance - target, *rest], axis=0).T[:count]
         if i < train_blocks:
             row_weights.append(turned[:, NCLS : NCLS + 1])
         pieces = []
-        for packet in (mine, theirs):
-            value = packet[pl.ds(first, count), :]
+        for value_index, value in enumerate(values):
+            if steps:
+                value = value * turned[:, NCLS + 1 + value_index : NCLS + 2 + value_index]
             for k in range(NCLS):
                 pieces.append((value * turned[:, k : k + 1]).astype(jnp.bfloat16))
         gradients.append(jnp.concatenate(pieces, axis=1))
@@ -346,7 +407,7 @@
     count = K // lax.axis_size("proj")
     swap = [(0, 1), (1, 0)]
     seeds = sign_seeds.reshape(-1, 128)
-    train_packet, test_packet, own_packet = pool(
+    train_packet, test_packet, own_packet, early_signs = pool(
         train_windows,
         test_windows,
         dilated_weight,
@@ -355,32 +416,24 @@
         train_labels.reshape(1, -1),
         test_labels.reshape(1, -1),
         seeds,
+        count,
     )
     far = [lax.ppermute(train_packet, "train", _pairs(shift, train_blocks)) for shift in range(1, train_blocks)]
     far += [lax.ppermute(test_packet, "test", _pairs(shift, test_blocks)) for shift in range(1, test_blocks)]
     other_packet = lax.ppermute(own_packet, "proj", swap)
-    early = [i for i in range(len(far)) if i >= train_blocks - 1 or i == train_blocks - 2]
-    late = [i for i in range(len(far)) if i not in early]
     channels = sign_seeds.shape[0] // NCLS
     classes = tuple(range(NCLS))
-    own_signs = sign_block(seeds, channels, count, classes)
-    far_other = [None] * len(far)
-    *held, own_signs, other_packet = lax.optimization_barrier((*(far[i] for i in early), own_signs, other_packet))
-    for i, value in zip(early, held):
-        far[i] = value
-        far_other[i] = lax.ppermute(value, "proj", swap)
+    own_signs = sign_block(seeds, channels, count, classes[len(EARLY_CLASSES) :])
     first_signs = sign_block(other_packet, channels, count, classes[: NCLS // 2])
-    *held, first_signs = lax.optimization_barrier((*(far[i] for i in late), first_signs))
-    for i, value in zip(late, held):
-        far[i] = value
-        far_other[i] = lax.ppermute(value, "proj", swap)
+    *far, own_signs, first_signs = lax.optimization_barrier((*far, own_signs, first_signs))
+    far_other = [lax.ppermute(value, "proj", swap) for value in far]
     last_signs = sign_block(other_packet, channels, count, classes[NCLS // 2 :])
     packets = [own_packet, other_packet]
     for value, other in zip(far, far_other):
         packets += [value, other]
     keep, send = partial_scores(
         packets,
-        [own_signs, first_signs, last_signs],
+        [early_signs, own_signs, first_signs, last_signs],
         precond.reshape(1, -1),
         train_blocks,
         test_blocks,

time: 26.2 us -> 25.8 us (0.985)
  waiting for transfers between devices: 1.81 us -> 1.13 us
    ppermute x3, waiting for transfers between devices: 0.96 us -> 0.01 us  [shards(): lax.ppermute(train_packet, 'train', _pairs(shift, train_blocks))]
    ppermute x4, starting transfers between devices: 0.59 us -> 1.08 us  [shards(): far_other = [lax.ppermute(value, 'proj', swap) for value in far]]
    ppermute x1, starting transfers between devices: 0.53 us -> 0.1 us  [shards(): received = lax.ppermute(send, 'proj', swap)]
    pallas_call x1, Pallas kernels: 7.17 us -> 7.57 us  [pool(): pl.pallas_call(functools.partial(pool_kernel, block), out_shape=(jax.Shap...]
    ppermute x1, waiting for transfers between devices: 0.84 us -> 1.1 us  [shards(): received = lax.ppermute(send, 'proj', swap)]
  transfers between devices with their start and end apart: 10 -> 10, of which waited for: 2 -> 1; matrix products, arithmetic and copies ran while one was open for 0% -> 0% of each run, Pallas kernels for 18% -> 17%
where the time goes in v5:
time: 25.8 us; the launch traced here: 25.6 us
  Pallas kernels  15.1 us (59%)
  starting transfers between devices  8.65 us (34%)
  waiting for transfers between devices  1.13 us (4%)
  other arithmetic  0.61 us (2%)
    pallas_call x1, Pallas kernels, pool(): pl.pallas_call(functools.partial(pool_kernel, block), out_shape=(jax.Shap...  7.57 us
    ppermute x3, starting transfers between devices, shards(): lax.ppermute(train_packet, 'train', _pairs(shift, train_blocks))  5.3 us
    pallas_call x3, Pallas kernels, sign_block(): pl.pallas_call(functools.partial(sign_kernel, seeds.dtype == jnp.float32,...  4.34 us
    pallas_call x1, Pallas kernels, partial_scores(): pl.pallas_call(functools.partial(score_kernel, train_blocks, test_blocks,...  3.19 us
    ppermute x1, starting transfers between devices, shards(): lax.ppermute(test_packet, 'test', _pairs(shift, test_blocks))  1.64 us
    ppermute x1, waiting for transfers between devices, shards(): received = lax.ppermute(send, 'proj', swap)  1.1 us
    ppermute x4, starting transfers between devices, shards(): far_other = [lax.ppermute(value, 'proj', swap) for value in far]  1.08 us
    mul x1, other arithmetic, shards(): return (keep + received) * (1.0 / (K * math.sqrt(C)))  0.61 us
  transfers between devices with their start and end apart: 10, of which 1 were waited for; matrix products, arithmetic and copies ran while one was open for 0% of the time, Pallas kernels for 17%

profile of v5, /device:TPU:0, one launch (start us, length us, event | category | flops | bytes accessed | tf_op | source)
XLA Modules:
  0.0 25.6 jit_solution(7025372467136712825)
XLA Ops:
  0.0 0.0 copy-start
  0.0 7.6 %pool.1 = (s16[80,256]{1,0:T(8,128)(2,1)S(1)}, s16[32,256]{1,0:T(8,128)(2,1)S(1)}, f32[112,256]{1,0:T(8,128)S(1)}, bf16[4,256,256]{2,1,0:T(8,128)(2,1)S(1)}) custom-call(bf16[64,64,512]{2,1,0:T(8,128)(2,1)} %train_hbm.1, bf16[16,64,512]{2,1,0:T(8,128)(2,1)} %test_hbm.1, bf16[3,512,256]{2,1,0:T(8,128)(2,1)} %weight_hbm.1, f32[1,256]{1,0:T(1,128)} %bitcast.10, ...), custom_call_target="tpu_custom_call" | custom-call | tf_op jit(solution)/shard_map/pool/pallas_call | solution.py:217
  7.6 0.5 %collective-permute-start = (f32[112,256]{1,0:T(8,128)S(1)}, f32[112,256]{1,0:T(8,128)S(1)}, u32[]{:S(2)}, u32[]{:S(2)}) collective-permute-start(f32[112,256]{1,0:T(8,128)S(1)} %get-tuple-element.17.refs_0_), channel_id=1, source_target_pairs={{0,1},{1,0},{2,3},{3,2},{4,5},{5,4},{6,7},{7,6},{8,9},{9,8},{10,11... | collective-permute-start | bytes 344072 | tf_op jit(solution)/shard_map/ppermute | solution.py:423
  8.1 4.7 %collective-permute-start.3 = (s16[80,256]{1,0:T(8,128)(2,1)S(1)}, s16[80,256]{1,0:T(8,128)(2,1)S(1)}, u32[]{:S(2)}, u32[]{:S(2)}) collective-permute-start(s16[80,256]{1,0:T(8,128)(2,1)S(1)} %get-tuple-element.18), channel_id=1, source_target_pairs={{0,12},{4,8},{8,4},{12,0},{1,13},{5,9},{9,5},{13,1},{2,14},{6,10},... | collective-permute-start | bytes 122888 | tf_op jit(solution)/shard_map/ppermute | solution.py:421
  12.8 0.0 collective-permute-start.2
  12.8 0.6 %collective-permute-start.1 = (s16[80,256]{1,0:T(8,128)(2,1)S(1)}, s16[80,256]{1,0:T(8,128)(2,1)S(1)}, u32[]{:S(2)}, u32[]{:S(2)}) collective-permute-start(s16[80,256]{1,0:T(8,128)(2,1)S(1)} %get-tuple-element.18), channel_id=1, source_target_pairs={{0,4},{4,0},{8,12},{12,8},{1,5},{5,1},{9,13},{13,9},{2,6},{6,2},{1... | collective-permute-start | bytes 122888 | tf_op jit(solution)/shard_map/ppermute | solution.py:421
  13.4 0.0 copy-start.1
  13.4 1.6 %collective-permute-start.4 = (s16[32,256]{1,0:T(8,128)(2,1)S(1)}, s16[32,256]{1,0:T(8,128)(2,1)S(1)}, u32[]{:S(2)}, u32[]{:S(2)}) collective-permute-start(s16[32,256]{1,0:T(8,128)(2,1)S(1)} %get-tuple-element.19), channel_id=1, source_target_pairs={{0,2},{2,0},{1,3},{3,1},{4,6},{6,4},{5,7},{7,5},{8,10},{10,8},{9,1... | collective-permute-start | bytes 49160 | tf_op jit(solution)/shard_map/ppermute | solution.py:422
  15.1 0.0 copy-done
  15.1 2.0 %signs.3.refs_11_ = bf16[4,1792,256]{2,1,0:T(8,128)(2,1)S(1)} custom-call(s32[16,128]{1,0:T(8,128)S(1)} %bitcast.7), custom_call_target="tpu_custom_call" | custom-call | flops 14680064 | bytes 3670016 | tf_op jit(solution)/shard_map/signs/pallas_call | solution.py:266
  17.0 0.0 collective-permute-done.seed_ref.refs_1_
  17.0 1.2 %signs.4.refs_12_ = bf16[4,1024,256]{2,1,0:T(8,128)(2,1)S(1)} custom-call(f32[112,256]{1,0:T(8,128)S(1)} %collective-permute-done.seed_ref.refs_1_), custom_call_target="tpu_custom_call" | custom-call | flops 8388608 | bytes 2097152 | tf_op jit(solution)/shard_map/signs/pallas_call | solution.py:266
  18.2 0.0 collective-permute-done.4.refs_8_
  18.2 0.0 collective-permute-done.3.refs_6_
  18.3 0.0 collective-permute-done.2.refs_4_
  18.3 0.0 collective-permute-done.1.refs_2_
  18.3 0.1 collective-permute-start.5
  18.4 0.5 %collective-permute-start.6 = (s16[80,256]{1,0:T(8,128)(2,1)S(1)}, s16[80,256]{1,0:T(8,128)(2,1)S(1)}, u32[]{:S(2)}, u32[]{:S(2)}) collective-permute-start(s16[80,256]{1,0:T(8,128)(2,1)S(1)} %collective-permute-done.2.refs_4_), channel_id=1, source_target_pairs={{0,1},{1,0},{2,3},{3,2},{4,5},{5,4},{6,7},{7,6},{8,9},{9,8},{10,11... | collective-permute-start | bytes 122888 | tf_op jit(solution)/shard_map/ppermute | solution.py:429
  18.9 0.1 collective-permute-start.7
  18.9 0.4 %collective-permute-start.8 = (s16[32,256]{1,0:T(8,128)(2,1)S(1)}, s16[32,256]{1,0:T(8,128)(2,1)S(1)}, u32[]{:S(2)}, u32[]{:S(2)}) collective-permute-start(s16[32,256]{1,0:T(8,128)(2,1)S(1)} %collective-permute-done.4.refs_8_), channel_id=1, source_target_pairs={{0,1},{1,0},{2,3},{3,2},{4,5},{5,4},{6,7},{7,6},{8,9},{9,8},{10,11... | collective-permute-start | bytes 49160 | tf_op jit(solution)/shard_map/ppermute | solution.py:429
  19.4 1.2 %signs.5.refs_13_ = bf16[4,1024,256]{2,1,0:T(8,128)(2,1)S(1)} custom-call(f32[112,256]{1,0:T(8,128)S(1)} %collective-permute-done.seed_ref.refs_1_), custom_call_target="tpu_custom_call" | custom-call | flops 8388608 | bytes 2097152 | tf_op jit(solution)/shard_map/signs/pallas_call | solution.py:266
  20.6 0.0 collective-permute-done.8.refs_9_
  20.6 0.0 collective-permute-done.5.refs_3_
  20.6 0.0 collective-permute-done.6.refs_5_
  20.6 0.0 collective-permute-done.7.refs_7_
  20.6 0.0 copy-done.1
  20.6 3.2 %partial_scores.1 = (f32[32,128]{1,0:T(8,128)S(1)}, f32[32,128]{1,0:T(8,128)S(1)}) custom-call(f32[112,256]{1,0:T(8,128)S(1)} %get-tuple-element.17.refs_0_, f32[112,256]{1,0:T(8,128)S(1)} %collective-permute-done.seed_ref.refs_1_, s16[80,256]{1,0:T(8,128)(2,1)S(1)} %collective-permute-done.1.refs_2_, s16[80,256]{1,0:T(8,128)(2,1)S(1)} %collective-permute-done.5.refs_3_, ...), custom_call_target="tpu_custom_call" | custom-call | flops 2415919104 | bytes 8388608 | tf_op jit(solution)/shard_map/partial_scores/pallas_call | solution.py:373
  23.8 0.1 collective-permute-start.9
  23.9 1.1 %collective-permute-done.9 = f32[32,128]{1,0:T(8,128)S(1)} collective-permute-done((f32[32,128]{1,0:T(8,128)S(1)}, f32[32,128]{1,0:T(8,128)S(1)}, u32[]{:S(2)}, u32[]{:S(2)}) %collective-permute-start.9) | collective-permute-done | bytes 16416 | tf_op jit(solution)/shard_map/ppermute | solution.py:443
  25.0 0.6 %add_multiply_fusion = f32[32,128]{1,0:T(8,128)} fusion(f32[32,128]{1,0:T(8,128)S(1)} %get-tuple-element.27, f32[32,128]{1,0:T(8,128)S(1)} %collective-permute-done.9), kind=kLoop, calls=%fused_computation | loop fusion | flops 8192 | bytes 49152 | tf_op jit(solution)/shard_map/mul | solution.py:444
Async XLA Ops:
  0.0 15.1 %copy-start = (s32[2048]{0:T(1024)S(1)}, s32[2048]{0:T(1024)}, u32[]{:S(2)}) copy-start(s32[2048]{0:T(1024)} %param.16) | copy-start | bytes 24580
  7.6 9.4 %collective-permute-start = (f32[112,256]{1,0:T(8,128)S(1)}, f32[112,256]{1,0:T(8,128)S(1)}, u32[]{:S(2)}, u32[]{:S(2)}) collective-permute-start(f32[112,256]{1,0:T(8,128)S(1)} %get-tuple-element.17.refs_0_), channel_id=1, source_target_pairs={{0,1},{1,0},{2,3},{3,2},{4,5},{5,4},{6,7},{7,6},{8,9},{9,8},{10,11... | collective-permute-start | bytes 344072 | tf_op jit(solution)/shard_map/ppermute | solution.py:423
  8.1 10.1 %collective-permute-start.3 = (s16[80,256]{1,0:T(8,128)(2,1)S(1)}, s16[80,256]{1,0:T(8,128)(2,1)S(1)}, u32[]{:S(2)}, u32[]{:S(2)}) collective-permute-start(s16[80,256]{1,0:T(8,128)(2,1)S(1)} %get-tuple-element.18), channel_id=1, source_target_pairs={{0,12},{4,8},{8,4},{12,0},{1,13},{5,9},{9,5},{13,1},{2,14},{6,10},... | collective-permute-start | bytes 122888 | tf_op jit(solution)/shard_map/ppermute | solution.py:421
  12.8 5.5 %collective-permute-start.2 = (s16[80,256]{1,0:T(8,128)(2,1)S(1)}, s16[80,256]{1,0:T(8,128)(2,1)S(1)}, u32[]{:S(2)}, u32[]{:S(2)}) collective-permute-start(s16[80,256]{1,0:T(8,128)(2,1)S(1)} %get-tuple-element.18), channel_id=1, source_target_pairs={{0,8},{4,12},{8,0},{12,4},{1,9},{5,13},{9,1},{13,5},{2,10},{6,14},... | collective-permute-start | bytes 122888 | tf_op jit(solution)/shard_map/ppermute | solution.py:421
  12.8 5.5 %collective-permute-start.1 = (s16[80,256]{1,0:T(8,128)(2,1)S(1)}, s16[80,256]{1,0:T(8,128)(2,1)S(1)}, u32[]{:S(2)}, u32[]{:S(2)}) collective-permute-start(s16[80,256]{1,0:T(8,128)(2,1)S(1)} %get-tuple-element.18), channel_id=1, source_target_pairs={{0,4},{4,0},{8,12},{12,8},{1,5},{5,1},{9,13},{13,9},{2,6},{6,2},{1... | collective-permute-start | bytes 122888 | tf_op jit(solution)/shard_map/ppermute | solution.py:421
  13.4 7.2 %copy-start.1 = (f32[2048]{0:T(1024)S(1)}, f32[2048]{0:T(1024)}, u32[]{:S(2)}) copy-start(f32[2048]{0:T(1024)} %param.17) | copy-start | bytes 24580
  13.4 4.8 %collective-permute-start.4 = (s16[32,256]{1,0:T(8,128)(2,1)S(1)}, s16[32,256]{1,0:T(8,128)(2,1)S(1)}, u32[]{:S(2)}, u32[]{:S(2)}) collective-permute-start(s16[32,256]{1,0:T(8,128)(2,1)S(1)} %get-tuple-element.19), channel_id=1, source_target_pairs={{0,2},{2,0},{1,3},{3,1},{4,6},{6,4},{5,7},{7,5},{8,10},{10,8},{9,1... | collective-permute-start | bytes 49160 | tf_op jit(solution)/shard_map/ppermute | solution.py:422
  18.3 2.3 %collective-permute-start.5 = (s16[80,256]{1,0:T(8,128)(2,1)S(1)}, s16[80,256]{1,0:T(8,128)(2,1)S(1)}, u32[]{:S(2)}, u32[]{:S(2)}) collective-permute-start(s16[80,256]{1,0:T(8,128)(2,1)S(1)} %collective-permute-done.1.refs_2_), channel_id=1, source_target_pairs={{0,1},{1,0},{2,3},{3,2},{4,5},{5,4},{6,7},{7,6},{8,9},{9,8},{10,11... | collective-permute-start | bytes 122888 | tf_op jit(solution)/shard_map/ppermute | solution.py:429
  18.4 2.2 %collective-permute-start.6 = (s16[80,256]{1,0:T(8,128)(2,1)S(1)}, s16[80,256]{1,0:T(8,128)(2,1)S(1)}, u32[]{:S(2)}, u32[]{:S(2)}) collective-permute-start(s16[80,256]{1,0:T(8,128)(2,1)S(1)} %collective-permute-done.2.refs_4_), channel_id=1, source_target_pairs={{0,1},{1,0},{2,3},{3,2},{4,5},{5,4},{6,7},{7,6},{8,9},{9,8},{10,11... | collective-permute-start | bytes 122888 | tf_op jit(solution)/shard_map/ppermute | solution.py:429
  18.9 1.7 %collective-permute-start.7 = (s16[80,256]{1,0:T(8,128)(2,1)S(1)}, s16[80,256]{1,0:T(8,128)(2,1)S(1)}, u32[]{:S(2)}, u32[]{:S(2)}) collective-permute-start(s16[80,256]{1,0:T(8,128)(2,1)S(1)} %collective-permute-done.3.refs_6_), channel_id=1, source_target_pairs={{0,1},{1,0},{2,3},{3,2},{4,5},{5,4},{6,7},{7,6},{8,9},{9,8},{10,11... | collective-permute-start | bytes 122888 | tf_op jit(solution)/shard_map/ppermute | solution.py:429
  18.9 1.6 %collective-permute-start.8 = (s16[32,256]{1,0:T(8,128)(2,1)S(1)}, s16[32,256]{1,0:T(8,128)(2,1)S(1)}, u32[]{:S(2)}, u32[]{:S(2)}) collective-permute-start(s16[32,256]{1,0:T(8,128)(2,1)S(1)} %collective-permute-done.4.refs_8_), channel_id=1, source_target_pairs={{0,1},{1,0},{2,3},{3,2},{4,5},{5,4},{6,7},{7,6},{8,9},{9,8},{10,11... | collective-permute-start | bytes 49160 | tf_op jit(solution)/shard_map/ppermute | solution.py:429
  23.8 1.2 %collective-permute-start.9 = (f32[32,128]{1,0:T(8,128)S(1)}, f32[32,128]{1,0:T(8,128)S(1)}, u32[]{:S(2)}, u32[]{:S(2)}) collective-permute-start(f32[32,128]{1,0:T(8,128)S(1)} %get-tuple-element.28), channel_id=1, source_target_pairs={{0,1},{1,0},{2,3},{3,2},{4,5},{5,4},{6,7},{7,6},{8,9},{9,8},{10,11... | collective-permute-start | bytes 49160 | tf_op jit(solution)/shard_map/ppermute | solution.py:443

commit v6 on v5

--- a/solution.py
+++ b/solution.py
@@ -18,7 +18,6 @@
 MIX_LAST = MIX_LAST - (1 << 32) if MIX_LAST >= 1 << 31 else MIX_LAST
 MIB = 2**20
 AHEAD = 3
-EARLY_CLASSES = tuple(range(1))
 
 VMEM = pl.BlockSpec(memory_space=pltpu.VMEM)
 HBM = pl.BlockSpec(memory_space=pltpu.HBM)
@@ -53,14 +52,14 @@
     return jnp.exp(exponent * math.log(2.0))
 
 
-def encode_packet(packet, pooled, logits, labels):
+def encode_packet(packet, at, pooled, logits, labels):
     count = pooled.shape[0]
     largest = jnp.maximum(jnp.max(jnp.abs(pooled), axis=1, keepdims=True), 1e-30)
     exponent = jnp.floor(jnp.log(largest) * (1.0 / math.log(2.0)))
     factor = jnp.ceil(largest * power_of_two(-exponent) * 8192.0)
     step = factor * (power_of_two(exponent) * (1.0 / (8192.0 * 32767.0)))
     steps = jnp.clip(jnp.round(pooled * (1.0 / step)), -32767.0, 32767.0)
-    packet[pl.ds(0, count), :] = steps.astype(jnp.int32).astype(jnp.int16)
+    packet[pl.ds(at, count), :] = steps.astype(jnp.int32).astype(jnp.int16)
     lane = lax.broadcasted_iota(jnp.int32, (count, 128), 1)
     turned = jnp.where(lane == 1, factor, jnp.where(lane == 2, exponent, 0.0)).T[:NCLS]
     logit_exponent = jnp.ceil(
@@ -79,19 +78,22 @@
         ],
         axis=0,
     )
-    packet[pl.ds(count, 2 * NCLS), :] = extra.astype(jnp.int32).astype(jnp.int16)
+    packet[pl.ds(at + count, 2 * NCLS), :] = extra.astype(jnp.int32).astype(jnp.int16)
 
 
 def decode_packet(packet):
     count = packet.shape[0] - 2 * NCLS
-    steps = packet[pl.ds(0, count), :].astype(jnp.int32).astype(jnp.float32)
-    extra = packet[pl.ds(count, 2 * NCLS), :].astype(jnp.int32).astype(jnp.float32)
+    extra = packet[count:]
     facts = extra[:NCLS, 128:]
     step = facts[1:2] * (power_of_two(facts[2:3]) * (1.0 / (8192.0 * 32767.0)))
     logits = (extra[:NCLS, :128] + extra[NCLS:, :128] * (1.0 / 16384.0)) * (
         power_of_two(facts[3:4]) * (1.0 / 8192.0)
     )
-    return steps, step, logits, facts[0:1]
+    return packet[:count], step, logits, facts[0:1]
+
+
+def as_float(values):
+    return values.astype(jnp.int32).astype(jnp.float32)
 
 
 def pool_kernel(
@@ -104,10 +106,7 @@
     train_label_ref,
     test_label_ref,
     seed_ref,
-    train_packet,
-    test_packet,
-    own_packet,
-    sign_ref,
+    packet,
     rows,
     weight,
     pooled,
@@ -116,8 +115,6 @@
     train_label,
     test_label,
     seeds,
-    turned,
-    column_ref,
     row_sem,
     weight_sem,
     small_sem,
@@ -155,7 +152,6 @@
         fetch(b).start()
     for copy in small:
         copy.wait()
-    write_signs(EARLY_CLASSES, seeds[...], sign_ref, turned, column_ref)
     weight_copy.wait()
     gain = gain_row[...]
     own_start = pl.multiple_of(proj_index * half, half)
@@ -186,10 +182,7 @@
 
     lax.fori_loop(0, blocks, one_block, 0)
     at = 0
-    for packet, label_ref, start, count in (
-        (train_packet, train_label, 0, train_count),
-        (test_packet, test_label, train_count, test_count),
-    ):
+    for label_ref, start, count in ((train_label, 0, train_count), (test_label, train_count, test_count)):
         own = pooled[pl.ds(start, count), :]
         logits = lax.dot_general(
             cls_rows[...],
@@ -199,16 +192,13 @@
             preferred_element_type=jnp.float32,
         )
         labels = jnp.broadcast_to(label_ref[...].astype(jnp.float32), (NCLS, count))
-        own_packet[pl.ds(at, count), :] = own
-        own_packet[pl.ds(at + count, NCLS), pl.ds(0, count)] = logits
-        own_packet[pl.ds(at + count, NCLS), pl.ds(128, count)] = labels
-        encode_packet(packet, own, logits, labels)
-        at += count + NCLS
-    own_packet[pl.ds(at, seeds.shape[0]), pl.ds(0, 128)] = (seeds[...] >> 15).astype(jnp.float32)
-    own_packet[pl.ds(at, seeds.shape[0]), pl.ds(128, 128)] = (seeds[...] & 32767).astype(jnp.float32)
-
-
-def pool(train_windows, test_windows, weight, gain, cls_t, train_labels, test_labels, seeds, count):
+        encode_packet(packet, at, own, logits, labels)
+        at += count + 2 * NCLS
+    packet[pl.ds(at, seeds.shape[0]), pl.ds(0, 128)] = (seeds[...] >> 15).astype(jnp.int16)
+    packet[pl.ds(at, seeds.shape[0]), pl.ds(128, 128)] = (seeds[...] & 32767).astype(jnp.int16)
+
+
+def pool(train_windows, test_windows, weight, gain, cls_t, train_labels, test_labels, seeds):
     block = 16
     train_count, length, width = train_windows.shape
     test_count = test_windows.shape[0]
@@ -216,14 +206,9 @@
     total = train_count + test_count
     return pl.pallas_call(
         functools.partial(pool_kernel, block),
-        out_shape=(
-            jax.ShapeDtypeStruct((train_count + 2 * NCLS, half), jnp.int16),
-            jax.ShapeDtypeStruct((test_count + 2 * NCLS, half), jnp.int16),
-            jax.ShapeDtypeStruct((total + 2 * NCLS + seeds.shape[0], half), jnp.float32),
-            jax.ShapeDtypeStruct((count // 256, seeds.size // NCLS * len(EARLY_CLASSES), 256), jnp.bfloat16),
-        ),
+        out_shape=jax.ShapeDtypeStruct((total + 4 * NCLS + seeds.shape[0], half), jnp.int16),
         in_specs=[HBM] * 8,
-        out_specs=(VMEM, VMEM, VMEM, VMEM),
+        out_specs=VMEM,
         scratch_shapes=[
             pltpu.VMEM((total, length, width), jnp.bfloat16),
             pltpu.VMEM(weight.shape, jnp.bfloat16),
@@ -233,8 +218,6 @@
             pltpu.VMEM(train_labels.shape, jnp.int32),
             pltpu.VMEM(test_labels.shape, jnp.int32),
             pltpu.VMEM(seeds.shape, jnp.int32),
-            pltpu.VMEM((128, 128), jnp.int32),
-            pltpu.VMEM((128 // NCLS, count), jnp.int32),
             pltpu.SemaphoreType.DMA((total // block,)),
             pltpu.SemaphoreType.DMA,
             pltpu.SemaphoreType.DMA((5,)),
@@ -249,6 +232,37 @@
     )
 
 
+def transfer_steps(train_blocks, test_blocks):
+    shifts = [("train", d) for d in reversed(range(1, train_blocks))]
+    shifts += [("test", d) for d in range(1, test_blocks)]
+    return [(shifts[i], shifts[i + 1]) for i in range(0, len(shifts), 2)]
+
+
+def pack_kernel(kinds, train_rows, test_rows, mine, theirs, *outs):
+    proj_index = lax.axis_index("proj")
+    for pair, out in zip(kinds, outs):
+        for core, kind in enumerate(pair):
+
+            @pl.when(proj_index == core)
+            def _():
+                start, count = (0, train_rows) if kind == "train" else (train_rows, test_rows)
+                for side, packet in enumerate((mine, theirs)):
+                    out[side, pl.ds(0, count), :] = packet[pl.ds(start, count), :]
+
+
+def pack(kinds, train_rows, test_rows, mine, theirs):
+    width = mine.shape[1]
+    rows = [train_rows if "train" in pair else test_rows for pair in kinds]
+    return pl.pallas_call(
+        functools.partial(pack_kernel, kinds, train_rows, test_rows),
+        out_shape=tuple(jax.ShapeDtypeStruct((2, count, width), jnp.int16) for count in rows),
+        in_specs=[VMEM, VMEM],
+        out_specs=(VMEM,) * len(kinds),
+        compiler_params=pltpu.CompilerParams(vmem_limit_bytes=8 * MIB),
+        name="pack",
+    )(mine, theirs)
+
+
 def sign_kernel(packed, classes, seed_ref, sign_ref, turned, column_ref):
     if packed:
         chunks = sign_ref.shape[1] // ((128 // NCLS) * len(classes))
@@ -264,7 +278,7 @@
     rows = channels * len(classes)
     parts = count // 256
     return pl.pallas_call(
-        functools.partial(sign_kernel, seeds.dtype == jnp.float32, classes),
+        functools.partial(sign_kernel, seeds.dtype == jnp.int16, classes),
         out_shape=jax.ShapeDtypeStruct((parts, rows, 256), jnp.bfloat16),
         in_specs=[VMEM],
         out_specs=VMEM,
@@ -278,44 +292,58 @@
 
 
 def score_kernel(train_blocks, test_blocks, train_count, test_count, *refs):
-    far = train_blocks + test_blocks - 2
-    packets = refs[: 2 * far + 2]
-    signs = refs[2 * far + 2 : -5]
+    steps = transfer_steps(train_blocks, test_blocks)
+    packets = refs[: 2 * len(steps) + 2]
+    signs = refs[2 * len(steps) + 2 : -5]
     precond_ref, keep_ref, send_ref, train_feat, test_feat = refs[-5:]
     proj_index = lax.axis_index("proj")
     parts, _, part_width = signs[0].shape
     train_rows = train_blocks * train_count
+    blocks = {"train": [], "test": []}
+    for kind, first, count in (
+        ("train", 0, train_count),
+        ("test", train_count + 2 * NCLS, test_count),
+    ):
+        rows = pl.ds(first, count + 2 * NCLS)
+        blocks[kind].append((0, [as_float(packet[rows, :]) for packet in packets[:2]]))
+    for i, pair in enumerate(steps):
+        direct, swapped = packets[2 * i + 2], packets[2 * i + 3]
+        for core, (kind, shift) in enumerate(pair):
+            rows = pl.ds(0, (train_count if kind == "train" else test_count) + 2 * NCLS)
+            blocks[kind].append(
+                (
+                    shift,
+                    [
+                        jnp.where(
+                            proj_index == core,
+                            as_float(direct[side, rows, :]),
+                            as_float(swapped[1 - side, rows, :]),
+                        )
+                        for side in range(2)
+                    ],
+                )
+            )
     gradients = []
     row_weights = []
-    for i in range(train_blocks + test_blocks):
+    for i, (_, pair) in enumerate(blocks["train"] + blocks["test"]):
         count = train_count if i < train_blocks else test_count
-        if i == 0 or i == train_blocks:
-            first = 0 if i == 0 else train_count + NCLS
-            values, logits, steps = [], 0.0, []
-            for packet in packets[:2]:
-                values.append(packet[pl.ds(first, count), :])
-                logits += packet[pl.ds(first + count, NCLS), pl.ds(0, 128)]
-            label = packets[0][pl.ds(first + count, 1), pl.ds(128, 128)]
-        else:
-            at = 2 * i if i < train_blocks else 2 * (i - 1)
-            decoded = [decode_packet(packet) for packet in packets[at : at + 2]]
-            values = [value for value, _, _, _ in decoded]
-            steps = [step for _, step, _, _ in decoded]
-            logits = decoded[0][2] + decoded[1][2]
-            label = decoded[0][3]
+        decoded = [decode_packet(packet) for packet in pair]
+        values = [value for value, _, _, _ in decoded]
+        sizes = [step for _, step, _, _ in decoded]
+        logits = decoded[0][2] + decoded[1][2]
+        label = decoded[0][3]
         chance = 1.0 / (1.0 + jnp.exp(-logits))
         classes = lax.broadcasted_iota(jnp.int32, (NCLS, 128), 0).astype(jnp.float32)
         target = jnp.where(label == classes, 1.0, 0.0)
         retain = 1.0 - jnp.sum(chance * target, axis=0, keepdims=True)
-        rest = [retain, *steps]
+        rest = [retain, *sizes]
         rest += [jnp.zeros((NCLS - len(rest), 128), jnp.float32)]
         turned = jnp.concatenate([chance - target, *rest], axis=0).T[:count]
         if i < train_blocks:
             row_weights.append(turned[:, NCLS : NCLS + 1])
         pieces = []
         for value_index, value in enumerate(values):
-            if steps:
-                value = value * turned[:, NCLS + 1 + value_index : NCLS + 2 + value_index]
+            value = value * turned[:, NCLS + 1 + value_index : NCLS + 2 + value_index]
             for k in range(NCLS):
                 pieces.append((value * turned[:, k : k + 1]).astype(jnp.bfloat16))
         gradients.append(jnp.concatenate(pieces, axis=1))
@@ -330,7 +358,7 @@
         columns = pl.ds(n * part_width, part_width)
         for i in range(train_blocks):
             part = projected[i * train_count : (i + 1) * train_count]
-            train_feat[_source(train_index, i, train_blocks), :, columns] = (
+            train_feat[train_index ^ blocks["train"][i][0], :, columns] = (
                 part * row_weights[i]
             ).astype(jnp.bfloat16)
         precond = precond_ref[
@@ -338,7 +366,7 @@
         ]
         for i in range(test_blocks):
             start = train_rows + i * test_count
-            test_feat[_source(test_index, i, test_blocks), :, columns] = (
+            test_feat[test_index ^ blocks["test"][i][0], :, columns] = (
                 projected[start : start + test_count] * precond
             ).astype(jnp.bfloat16)
     half_blocks = train_blocks // 2
@@ -350,18 +378,6 @@
         target[...] = lax.dot_general(
             test, train, (((1,), (1,)), ((), ())), preferred_element_type=jnp.float32
         )
-
-
-def _source(index, shift, count):
-    if count & (count - 1) == 0:
-        return index ^ shift
-    return lax.rem(index + count - shift, count)
-
-
-def _pairs(shift, count):
-    if count & (count - 1) == 0:
-        return [(i, i ^ shift) for i in range(count)]
-    return [(i, (i + shift) % count) for i in range(count)]
 
 
 def partial_scores(packets, signs, precond, train_blocks, test_blocks, train_count, test_count):
@@ -407,7 +423,7 @@
     count = K // lax.axis_size("proj")
     swap = [(0, 1), (1, 0)]
     seeds = sign_seeds.reshape(-1, 128)
-    train_packet, test_packet, own_packet, early_signs = pool(
+    packet = pool(
         train_windows,
         test_windows,
         dilated_weight,
@@ -416,29 +432,34 @@
         train_labels.reshape(1, -1),
         test_labels.reshape(1, -1),
         seeds,
-        count,
-    )
-    far = [lax.ppermute(train_packet, "train", _pairs(shift, train_blocks)) for shift in range(1, train_blocks)]
-    far += [lax.ppermute(test_packet, "test", _pairs(shift, test_blocks)) for shift in range(1, test_blocks)]
-    other_packet = lax.ppermute(own_packet, "proj", swap)
+    )
     channels = sign_seeds.shape[0] // NCLS
-    classes = tuple(range(NCLS))
-    own_signs = sign_block(seeds, channels, count, classes[len(EARLY_CLASSES) :])
-    first_signs = sign_block(other_packet, channels, count, classes[: NCLS // 2])
-    *far, own_signs, first_signs = lax.optimization_barrier((*far, own_signs, first_signs))
-    far_other = [lax.ppermute(value, "proj", swap) for value in far]
-    last_signs = sign_block(other_packet, channels, count, classes[NCLS // 2 :])
-    packets = [own_packet, other_packet]
-    for value, other in zip(far, far_other):
-        packets += [value, other]
+    halves = (tuple(range(NCLS // 2)), tuple(range(NCLS // 2, NCLS)))
+    steps = transfer_steps(train_blocks, test_blocks)
+    other_packet = lax.ppermute(packet, "proj", swap)
+    signs = [sign_block(seeds, channels, count, halves[0])]
+    other_packet, signs[0] = lax.optimization_barrier((other_packet, signs[0]))
+    kinds = list(dict.fromkeys((a, b) for (a, _), (b, _) in steps))
+    packed = pack(kinds, train_count + 2 * NCLS, test_count + 2 * NCLS, packet, other_packet)
+    far = []
+    for pair in steps:
+        moves = []
+        for source in range(train_blocks * test_blocks * 2):
+            core = source % 2
+            kind, shift = pair[core]
+            scale = 2 * test_blocks if kind == "train" else 2
+            moves.append((source, source ^ (shift * scale)))
+        value = packed[kinds.index((pair[0][0], pair[1][0]))]
+        far.append(lax.ppermute(value, ("train", "test", "proj"), moves))
+    signs.append(sign_block(seeds, channels, count, halves[1]))
+    signs.append(sign_block(other_packet, channels, count, halves[0]))
+    *far, signs[1], signs[2] = lax.optimization_barrier((*far, signs[1], signs[2]))
+    packets = [packet, other_packet]
+    for value in far:
+        packets += [value, lax.ppermute(value, "proj", swap)]
+    signs.append(sign_block(other_packet, channels, count, halves[1]))
     keep, send = partial_scores(
-        packets,
-        [early_signs, own_signs, first_signs, last_signs],
-        precond.reshape(1, -1),
-        train_blocks,
-        test_blocks,
-        train_count,
-        test_count,
+        packets, signs, precond.reshape(1, -1), train_blocks, test_blocks, train_count, test_count
     )
     received = lax.ppermute(send, "proj", swap)
     return (keep + received) * (1.0 / (K * math.sqrt(C)))

time: 25.8 us -> 24.9 us (0.965)
  starting transfers between devices: 8.65 us -> 5.79 us
  waiting for transfers between devices: 1.13 us -> 3.17 us
    ppermute x9 -> x5, starting transfers between devices: 8.55 us -> 5.72 us  [the longest x2 4.67 us: shards(): far.append(lax.ppermute(value, ('train', 'test', 'proj'), moves))]
    ppermute x9 -> x5, waiting for transfers between devices: 0.02 us -> 2.04 us  [the longest x2 2.04 us: shards(): far.append(lax.ppermute(value, ('train', 'test', 'proj'), moves))]
    pallas_call x4 -> x6, Pallas kernels: 11.9 us -> 12 us  [the longest x1 7.19 us: pool(): pl.pallas_call(functools.partial(pool_kernel, block), out_shape=jax.Shape...]
  transfers between devices with their start and end apart: 10 -> 6, of which waited for: 1 -> 3; matrix products, arithmetic and copies ran while one was open for 0% -> 0% of each run, Pallas kernels for 17% -> 19%
where the time goes in v6:
time: 24.9 us; the launch traced here: 24.8 us
  Pallas kernels  15.1 us (61%)
  starting transfers between devices  5.79 us (23%)
  waiting for transfers between devices  3.17 us (13%)
  other arithmetic  0.61 us (2%)
    pallas_call x1, Pallas kernels, pool(): pl.pallas_call(functools.partial(pool_kernel, block), out_shape=jax.Shape...  7.19 us
    pallas_call x4, Pallas kernels, sign_block(): pl.pallas_call(functools.partial(sign_kernel, seeds.dtype == jnp.int16, c...  4.75 us
    ppermute x2, starting transfers between devices, shards(): far.append(lax.ppermute(value, ('train', 'test', 'proj'), moves))  4.67 us
    pallas_call x1, Pallas kernels, partial_scores(): pl.pallas_call(functools.partial(score_kernel, train_blocks, test_blocks,...  3.16 us
    ppermute x2, waiting for transfers between devices, shards(): far.append(lax.ppermute(value, ('train', 'test', 'proj'), moves))  2.04 us
    ppermute x1, waiting for transfers between devices, shards(): received = lax.ppermute(send, 'proj', swap)  1.13 us
    mul x1, other arithmetic, shards(): return (keep + received) * (1.0 / (K * math.sqrt(C)))  0.61 us
    ppermute x1, starting transfers between devices, shards(): other_packet = lax.ppermute(packet, 'proj', swap)  0.54 us
  transfers between devices with their start and end apart: 6, of which 3 were waited for; matrix products, arithmetic and copies ran while one was open for 0% of the time, Pallas kernels for 19%

profile of v6, /device:TPU:0, one launch (start us, length us, event | category | flops | bytes accessed | tf_op | source)
XLA Modules:
  0.0 24.8 jit_solution(7539835042516553098)
XLA Ops:
  0.0 0.0 copy-start
  0.0 7.2 %pool.1.mine.refs_0_ = s16[128,256]{1,0:T(8,128)(2,1)S(1)} custom-call(bf16[64,64,512]{2,1,0:T(8,128)(2,1)} %train_hbm.1, bf16[16,64,512]{2,1,0:T(8,128)(2,1)} %test_hbm.1, bf16[3,512,256]{2,1,0:T(8,128)(2,1)} %weight_hbm.1, f32[1,256]{1,0:T(1,128)} %bitcast.11, f32[8,256]{1,0:T(8,128)} %bitcast.10, s32[1,64]{1,0:T(1,128)} %bitcast.12, s32[1,16]{1,0:T(1,128)} %bitcast.13, ...), custom_call_target="tpu_custom_call" | custom-call | tf_op jit(solution)/shard_map/pool/pallas_call | solution.py:207
  7.2 0.5 %collective-permute-start = (s16[128,256]{1,0:T(8,128)(2,1)S(1)}, s16[128,256]{1,0:T(8,128)(2,1)S(1)}, u32[]{:S(2)}, u32[]{:S(2)}) collective-permute-start(s16[128,256]{1,0:T(8,128)(2,1)S(1)} %pool.1.mine.refs_0_), channel_id=1, source_target_pairs={{0,1},{1,0},{2,3},{3,2},{4,5},{5,4},{6,7},{7,6},{8,9},{9,8},{10,11... | collective-permute-start | bytes 196616 | tf_op jit(solution)/shard_map/ppermute | solution.py:439
  7.7 0.0 copy-done
  7.7 1.2 %signs.4.refs_6_ = bf16[4,1024,256]{2,1,0:T(8,128)(2,1)S(1)} custom-call(s32[16,128]{1,0:T(8,128)S(1)} %bitcast.7), custom_call_target="tpu_custom_call" | custom-call | flops 8388608 | bytes 2097152 | tf_op jit(solution)/shard_map/signs/pallas_call | solution.py:280
  8.9 0.0 collective-permute-done.theirs.seed_ref.refs_1_
  9.0 4.7 %collective-permute-start.1 = (s16[2,80,256]{2,1,0:T(8,128)(2,1)S(1)}, s16[2,80,256]{2,1,0:T(8,128)(2,1)S(1)}, u32[]{:S(2)}, u32[]{:S(2)}) collective-permute-start(s16[2,80,256]{2,1,0:T(8,128)(2,1)S(1)} %get-tuple-element.16), channel_id=1, source_target_pairs={{0,12},{1,9},{2,14},{3,11},{4,8},{5,13},{6,10},{7,15},{8,4},{9,1},... | collective-permute-start | bytes 245768 | tf_op jit(solution)/shard_map/ppermute | solution.py:453
  13.7 0.0 collective-permute-start.2
  13.7 1.2 %signs.5.refs_7_ = bf16[4,1024,256]{2,1,0:T(8,128)(2,1)S(1)} custom-call(s32[16,128]{1,0:T(8,128)S(1)} %bitcast.8), custom_call_target="tpu_custom_call" | custom-call | flops 8388608 | bytes 2097152 | tf_op jit(solution)/shard_map/signs/pallas_call | solution.py:280
  14.8 0.0 copy-start.1
  14.9 1.2 %signs.6.refs_8_ = bf16[4,1024,256]{2,1,0:T(8,128)(2,1)S(1)} custom-call(s16[128,256]{1,0:T(8,128)(2,1)S(1)} %collective-permute-done.theirs.seed_ref.refs_1_), custom_call_target="tpu_custom_call" | custom-call | flops 8388608 | bytes 2097152 | tf_op jit(solution)/shard_map/signs/pallas_call | solution.py:280
  16.1 0.8 %collective-permute-done.1.refs_2_ = s16[2,80,256]{2,1,0:T(8,128)(2,1)S(1)} collective-permute-done((s16[2,80,256]{2,1,0:T(8,128)(2,1)S(1)}, s16[2,80,256]{2,1,0:T(8,128)(2,1)S(1)}, u32[]{:S(2)}, u32[]{:S(2)}) %collective-permute-start.1) | collective-permute-done | bytes 81952 | tf_op jit(solution)/shard_map/ppermute | solution.py:453
  16.9 1.2 %collective-permute-done.2.refs_4_ = s16[2,80,256]{2,1,0:T(8,128)(2,1)S(1)} collective-permute-done((s16[2,80,256]{2,1,0:T(8,128)(2,1)S(1)}, s16[2,80,256]{2,1,0:T(8,128)(2,1)S(1)}, u32[]{:S(2)}, u32[]{:S(2)}) %collective-permute-start.2) | collective-permute-done | bytes 81952 | tf_op jit(solution)/shard_map/ppermute | solution.py:453
  18.1 0.0 collective-permute-start.3
  18.1 0.5 %collective-permute-start.4 = (s16[2,80,256]{2,1,0:T(8,128)(2,1)S(1)}, s16[2,80,256]{2,1,0:T(8,128)(2,1)S(1)}, u32[]{:S(2)}, u32[]{:S(2)}) collective-permute-start(s16[2,80,256]{2,1,0:T(8,128)(2,1)S(1)} %collective-permute-done.2.refs_4_), channel_id=1, source_target_pairs={{0,1},{1,0},{2,3},{3,2},{4,5},{5,4},{6,7},{7,6},{8,9},{9,8},{10,11... | collective-permute-start | bytes 245768 | tf_op jit(solution)/shard_map/ppermute | solution.py:459
  18.6 1.2 %signs.7.refs_9_ = bf16[4,1024,256]{2,1,0:T(8,128)(2,1)S(1)} custom-call(s16[128,256]{1,0:T(8,128)(2,1)S(1)} %collective-permute-done.theirs.seed_ref.refs_1_), custom_call_target="tpu_custom_call" | custom-call | flops 8388608 | bytes 2097152 | tf_op jit(solution)/shard_map/signs/pallas_call | solution.py:280
  19.8 0.0 collective-permute-done.3.refs_3_
  19.8 0.0 collective-permute-done.4.refs_5_
  19.8 0.0 copy-done.1
  19.8 3.2 %partial_scores.1 = (f32[32,128]{1,0:T(8,128)S(1)}, f32[32,128]{1,0:T(8,128)S(1)}) custom-call(s16[128,256]{1,0:T(8,128)(2,1)S(1)} %pool.1.mine.refs_0_, s16[128,256]{1,0:T(8,128)(2,1)S(1)} %collective-permute-done.theirs.seed_ref.refs_1_, s16[2,80,256]{2,1,0:T(8,128)(2,1)S(1)} %collective-permute-done.1.refs_2_, ...), custom_call_target="tpu_custom_call" | custom-call | flops 2415919104 | bytes 8388608 | tf_op jit(solution)/shard_map/partial_scores/pallas_call | solution.py:389
  23.0 0.1 collective-permute-start.5
  23.1 1.1 %collective-permute-done.5 = f32[32,128]{1,0:T(8,128)S(1)} collective-permute-done((f32[32,128]{1,0:T(8,128)S(1)}, f32[32,128]{1,0:T(8,128)S(1)}, u32[]{:S(2)}, u32[]{:S(2)}) %collective-permute-start.5) | collective-permute-done | bytes 16416 | tf_op jit(solution)/shard_map/ppermute | solution.py:464
  24.2 0.6 %add_multiply_fusion = f32[32,128]{1,0:T(8,128)} fusion(f32[32,128]{1,0:T(8,128)S(1)} %get-tuple-element.23, f32[32,128]{1,0:T(8,128)S(1)} %collective-permute-done.5), kind=kLoop, calls=%fused_computation | loop fusion | flops 8192 | bytes 49152 | tf_op jit(solution)/shard_map/mul | solution.py:465
  (1 shorter events, 0.0 us)
Async XLA Ops:
  0.0 7.7 %copy-start = (s32[2048]{0:T(1024)S(1)}, s32[2048]{0:T(1024)}, u32[]{:S(2)}) copy-start(s32[2048]{0:T(1024)} %param.16) | copy-start | bytes 24580
  7.2 1.7 %collective-permute-start = (s16[128,256]{1,0:T(8,128)(2,1)S(1)}, s16[128,256]{1,0:T(8,128)(2,1)S(1)}, u32[]{:S(2)}, u32[]{:S(2)}) collective-permute-start(s16[128,256]{1,0:T(8,128)(2,1)S(1)} %pool.1.mine.refs_0_), channel_id=1, source_target_pairs={{0,1},{1,0},{2,3},{3,2},{4,5},{5,4},{6,7},{7,6},{8,9},{9,8},{10,11... | collective-permute-start | bytes 196616 | tf_op jit(solution)/shard_map/ppermute | solution.py:439
  9.0 7.9 %collective-permute-start.1 = (s16[2,80,256]{2,1,0:T(8,128)(2,1)S(1)}, s16[2,80,256]{2,1,0:T(8,128)(2,1)S(1)}, u32[]{:S(2)}, u32[]{:S(2)}) collective-permute-start(s16[2,80,256]{2,1,0:T(8,128)(2,1)S(1)} %get-tuple-element.16), channel_id=1, source_target_pairs={{0,12},{1,9},{2,14},{3,11},{4,8},{5,13},{6,10},{7,15},{8,4},{9,1},... | collective-permute-start | bytes 245768 | tf_op jit(solution)/shard_map/ppermute | solution.py:453
  13.7 4.4 %collective-permute-start.2 = (s16[2,80,256]{2,1,0:T(8,128)(2,1)S(1)}, s16[2,80,256]{2,1,0:T(8,128)(2,1)S(1)}, u32[]{:S(2)}, u32[]{:S(2)}) collective-permute-start(s16[2,80,256]{2,1,0:T(8,128)(2,1)S(1)} %get-tuple-element.17), channel_id=1, source_target_pairs={{0,4},{1,3},{2,6},{3,1},{4,0},{5,7},{6,2},{7,5},{8,12},{9,11},{10,... | collective-permute-start | bytes 245768 | tf_op jit(solution)/shard_map/ppermute | solution.py:453
  14.8 5.0 %copy-start.1 = (f32[2048]{0:T(1024)S(1)}, f32[2048]{0:T(1024)}, u32[]{:S(2)}) copy-start(f32[2048]{0:T(1024)} %param.17) | copy-start | bytes 24580
  18.1 1.7 %collective-permute-start.3 = (s16[2,80,256]{2,1,0:T(8,128)(2,1)S(1)}, s16[2,80,256]{2,1,0:T(8,128)(2,1)S(1)}, u32[]{:S(2)}, u32[]{:S(2)}) collective-permute-start(s16[2,80,256]{2,1,0:T(8,128)(2,1)S(1)} %collective-permute-done.1.refs_2_), channel_id=1, source_target_pairs={{0,1},{1,0},{2,3},{3,2},{4,5},{5,4},{6,7},{7,6},{8,9},{9,8},{10,11... | collective-permute-start | bytes 245768 | tf_op jit(solution)/shard_map/ppermute | solution.py:459
  18.1 1.7 %collective-permute-start.4 = (s16[2,80,256]{2,1,0:T(8,128)(2,1)S(1)}, s16[2,80,256]{2,1,0:T(8,128)(2,1)S(1)}, u32[]{:S(2)}, u32[]{:S(2)}) collective-permute-start(s16[2,80,256]{2,1,0:T(8,128)(2,1)S(1)} %collective-permute-done.2.refs_4_), channel_id=1, source_target_pairs={{0,1},{1,0},{2,3},{3,2},{4,5},{5,4},{6,7},{7,6},{8,9},{9,8},{10,11... | collective-permute-start | bytes 245768 | tf_op jit(solution)/shard_map/ppermute | solution.py:459
  23.0 1.2 %collective-permute-start.5 = (f32[32,128]{1,0:T(8,128)S(1)}, f32[32,128]{1,0:T(8,128)S(1)}, u32[]{:S(2)}, u32[]{:S(2)}) collective-permute-start(f32[32,128]{1,0:T(8,128)S(1)} %get-tuple-element.24), channel_id=1, source_target_pairs={{0,1},{1,0},{2,3},{3,2},{4,5},{5,4},{6,7},{7,6},{8,9},{9,8},{10,11... | collective-permute-start | bytes 49160 | tf_op jit(solution)/shard_map/ppermute | solution.py:464

commit v7 on v6

--- a/solution.py
+++ b/solution.py
@@ -235,7 +235,7 @@
 def transfer_steps(train_blocks, test_blocks):
     shifts = [("train", d) for d in reversed(range(1, train_blocks))]
     shifts += [("test", d) for d in range(1, test_blocks)]
-    return [(shifts[i], shifts[i + 1]) for i in range(0, len(shifts), 2)]
+    return [(shifts[i + 1], shifts[i]) for i in range(0, len(shifts), 2)]
 
 
 def pack_kernel(kinds, train_rows, test_rows, mine, theirs, *outs):
@@ -261,6 +261,27 @@
         compiler_params=pltpu.CompilerParams(vmem_limit_bytes=8 * MIB),
         name="pack",
     )(mine, theirs)
+
+
+def join_kernel(*refs):
+    *values, out = refs
+    at = 0
+    for value in values:
+        for side in range(value.shape[0]):
+            out[pl.ds(at, value.shape[1]), :] = value[side]
+            at += value.shape[1]
+
+
+def join(values):
+    rows = sum(value.shape[0] * value.shape[1] for value in values)
+    return pl.pallas_call(
+        join_kernel,
+        out_shape=jax.ShapeDtypeStruct((rows, values[0].shape[2]), values[0].dtype),
+        in_specs=[VMEM] * len(values),
+        out_specs=VMEM,
+        compiler_params=pltpu.CompilerParams(vmem_limit_bytes=8 * MIB),
+        name="join",
+    )(*values)
 
 
 def sign_kernel(packed, classes, seed_ref, sign_ref, turned, column_ref):
@@ -293,8 +314,8 @@
 
 def score_kernel(train_blocks, test_blocks, train_count, test_count, *refs):
     steps = transfer_steps(train_blocks, test_blocks)
-    packets = refs[: 2 * len(steps) + 2]
-    signs = refs[2 * len(steps) + 2 : -5]
+    packets = refs[: len(steps) + 3]
+    signs = refs[len(steps) + 3 : -5]
     precond_ref, keep_ref, send_ref, train_feat, test_feat = refs[-5:]
     proj_index = lax.axis_index("proj")
     parts, _, part_width = signs[0].shape
@@ -306,23 +327,26 @@
     ):
         rows = pl.ds(first, count + 2 * NCLS)
         blocks[kind].append((0, [as_float(packet[rows, :]) for packet in packets[:2]]))
+    swapped = packets[-1]
+    base = 0
     for i, pair in enumerate(steps):
-        direct, swapped = packets[2 * i + 2], packets[2 * i + 3]
+        direct = packets[i + 2]
         for core, (kind, shift) in enumerate(pair):
-            rows = pl.ds(0, (train_count if kind == "train" else test_count) + 2 * NCLS)
+            size = (train_count if kind == "train" else test_count) + 2 * NCLS
             blocks[kind].append(
                 (
                     shift,
                     [
                         jnp.where(
                             proj_index == core,
-                            as_float(direct[side, rows, :]),
-                            as_float(swapped[1 - side, rows, :]),
+                            as_float(direct[side, pl.ds(0, size), :]),
+                            as_float(swapped[pl.ds(base + (1 - side) * direct.shape[1], size), :]),
                         )
                         for side in range(2)
                     ],
                 )
             )
+        base += 2 * direct.shape[1]
     gradients = []
     row_weights = []
     for i, (_, pair) in enumerate(blocks["train"] + blocks["test"]):
@@ -454,9 +478,7 @@
     signs.append(sign_block(seeds, channels, count, halves[1]))
     signs.append(sign_block(other_packet, channels, count, halves[0]))
     *far, signs[1], signs[2] = lax.optimization_barrier((*far, signs[1], signs[2]))
-    packets = [packet, other_packet]
-    for value in far:
-        packets += [value, lax.ppermute(value, "proj", swap)]
+    packets = [packet, other_packet, *far, lax.ppermute(join(far), "proj", swap)]
     signs.append(sign_block(other_packet, channels, count, halves[1]))
     keep, send = partial_scores(
         packets, signs, precond.reshape(1, -1), train_blocks, test_blocks, train_count, test_count

time: 24.9 us -> 24.3 us (0.976)
  waiting for transfers between devices: 3.17 us -> 2.26 us
  starting transfers between devices: 5.79 us -> 6.11 us
    ppermute x2, waiting for transfers between devices: 2.04 us -> 1.22 us  [shards(): far.append(lax.ppermute(value, ('train', 'test', 'proj'), moves))]
    ppermute x2, starting transfers between devices: 4.67 us -> 5.15 us  [shards(): far.append(lax.ppermute(value, ('train', 'test', 'proj'), moves))]
    ppermute x2 -> x1, starting transfers between devices: 0.51 us -> 0.08 us  [shards(): lax.ppermute(join(far), 'proj', swap)]
    ppermute x1, starting transfers between devices: 0.08 us -> 0.35 us  [shards(): received = lax.ppermute(send, 'proj', swap)]
    ppermute x1, waiting for transfers between devices: 1.13 us -> 0.85 us  [shards(): received = lax.ppermute(send, 'proj', swap)]
  transfers between devices with their start and end apart: 6 -> 5, of which waited for: 3 -> 3; matrix products, arithmetic and copies ran while one was open for 0% -> 0% of each run, Pallas kernels for 19% -> 20%
where the time goes in v7:
time: 24.3 us; the launch traced here: 24.2 us
  Pallas kernels  15.1 us (62%)
  starting transfers between devices  6.11 us (25%)
  waiting for transfers between devices  2.26 us (9%)
  other arithmetic  0.61 us (3%)
    pallas_call x1, Pallas kernels, pool(): pl.pallas_call(functools.partial(pool_kernel, block), out_shape=jax.Shape...  7.19 us
    ppermute x2, starting transfers between devices, shards(): far.append(lax.ppermute(value, ('train', 'test', 'proj'), moves))  5.15 us
    pallas_call x4, Pallas kernels, sign_block(): pl.pallas_call(functools.partial(sign_kernel, seeds.dtype == jnp.int16, c...  4.75 us
    pallas_call x1, Pallas kernels, partial_scores(): pl.pallas_call(functools.partial(score_kernel, train_blocks, test_blocks,...  3.15 us
    ppermute x2, waiting for transfers between devices, shards(): far.append(lax.ppermute(value, ('train', 'test', 'proj'), moves))  1.22 us
    ppermute x1, waiting for transfers between devices, shards(): received = lax.ppermute(send, 'proj', swap)  0.85 us
    mul x1, other arithmetic, shards(): return (keep + received) * (1.0 / (K * math.sqrt(C)))  0.61 us
    ppermute x1, starting transfers between devices, shards(): other_packet = lax.ppermute(packet, 'proj', swap)  0.54 us
  transfers between devices with their start and end apart: 5, of which 3 were waited for; matrix products, arithmetic and copies ran while one was open for 0% of the time, Pallas kernels for 20%

profile of v7, /device:TPU:0, one launch (start us, length us, event | category | flops | bytes accessed | tf_op | source)
XLA Modules:
  0.0 24.2 jit_solution(3909640544644216539)
XLA Ops:
  0.0 0.0 copy-start
  0.0 7.2 %pool.1.mine.refs_0_ = s16[128,256]{1,0:T(8,128)(2,1)S(1)} custom-call(bf16[64,64,512]{2,1,0:T(8,128)(2,1)} %train_hbm.1, bf16[16,64,512]{2,1,0:T(8,128)(2,1)} %test_hbm.1, bf16[3,512,256]{2,1,0:T(8,128)(2,1)} %weight_hbm.1, f32[1,256]{1,0:T(1,128)} %bitcast.11, f32[8,256]{1,0:T(8,128)} %bitcast.10, s32[1,64]{1,0:T(1,128)} %bitcast.12, s32[1,16]{1,0:T(1,128)} %bitcast.13, ...), custom_call_target="tpu_custom_call" | custom-call | tf_op jit(solution)/shard_map/pool/pallas_call | solution.py:207
  7.2 0.5 %collective-permute-start = (s16[128,256]{1,0:T(8,128)(2,1)S(1)}, s16[128,256]{1,0:T(8,128)(2,1)S(1)}, u32[]{:S(2)}, u32[]{:S(2)}) collective-permute-start(s16[128,256]{1,0:T(8,128)(2,1)S(1)} %pool.1.mine.refs_0_), channel_id=1, source_target_pairs={{0,1},{1,0},{2,3},{3,2},{4,5},{5,4},{6,7},{7,6},{8,9},{9,8},{10,11... | collective-permute-start | bytes 196616 | tf_op jit(solution)/shard_map/ppermute | solution.py:463
  7.7 0.0 copy-done
  7.7 1.2 %signs.4.refs_5_ = bf16[4,1024,256]{2,1,0:T(8,128)(2,1)S(1)} custom-call(s32[16,128]{1,0:T(8,128)S(1)} %bitcast.7), custom_call_target="tpu_custom_call" | custom-call | flops 8388608 | bytes 2097152 | tf_op jit(solution)/shard_map/signs/pallas_call | solution.py:301
  8.9 0.0 collective-permute-done.theirs.seed_ref.refs_1_
  9.0 3.7 %collective-permute-start.1 = (s16[2,80,256]{2,1,0:T(8,128)(2,1)S(1)}, s16[2,80,256]{2,1,0:T(8,128)(2,1)S(1)}, u32[]{:S(2)}, u32[]{:S(2)}) collective-permute-start(s16[2,80,256]{2,1,0:T(8,128)(2,1)S(1)} %get-tuple-element.16), channel_id=1, source_target_pairs={{0,8},{1,13},{2,10},{3,15},{4,12},{5,9},{6,14},{7,11},{8,0},{9,5},... | collective-permute-start | bytes 245768 | tf_op jit(solution)/shard_map/ppermute | solution.py:477
  12.6 1.5 %collective-permute-start.2 = (s16[2,80,256]{2,1,0:T(8,128)(2,1)S(1)}, s16[2,80,256]{2,1,0:T(8,128)(2,1)S(1)}, u32[]{:S(2)}, u32[]{:S(2)}) collective-permute-start(s16[2,80,256]{2,1,0:T(8,128)(2,1)S(1)} %get-tuple-element.17), channel_id=1, source_target_pairs={{0,2},{1,5},{2,0},{3,7},{4,6},{5,1},{6,4},{7,3},{8,10},{9,13},{10,... | collective-permute-start | bytes 245768 | tf_op jit(solution)/shard_map/ppermute | solution.py:477
  14.1 1.2 %signs.5.refs_6_ = bf16[4,1024,256]{2,1,0:T(8,128)(2,1)S(1)} custom-call(s32[16,128]{1,0:T(8,128)S(1)} %bitcast.8), custom_call_target="tpu_custom_call" | custom-call | flops 8388608 | bytes 2097152 | tf_op jit(solution)/shard_map/signs/pallas_call | solution.py:301
  15.3 0.0 copy-start.1
  15.3 1.2 %signs.6.refs_7_ = bf16[4,1024,256]{2,1,0:T(8,128)(2,1)S(1)} custom-call(s16[128,256]{1,0:T(8,128)(2,1)S(1)} %collective-permute-done.theirs.seed_ref.refs_1_), custom_call_target="tpu_custom_call" | custom-call | flops 8388608 | bytes 2097152 | tf_op jit(solution)/shard_map/signs/pallas_call | solution.py:301
  16.5 1.2 %collective-permute-done.1.refs_0_.refs_2_ = s16[2,80,256]{2,1,0:T(8,128)(2,1)S(1)} collective-permute-done((s16[2,80,256]{2,1,0:T(8,128)(2,1)S(1)}, s16[2,80,256]{2,1,0:T(8,128)(2,1)S(1)}, u32[]{:S(2)}, u32[]{:S(2)}) %collective-permute-start.1) | collective-permute-done | bytes 81952 | tf_op jit(solution)/shard_map/ppermute | solution.py:477
  17.7 0.0 collective-permute-done.2.refs_1_.refs_3_
  17.8 0.1 collective-permute-start.3
  17.8 1.2 %signs.7.refs_8_ = bf16[4,1024,256]{2,1,0:T(8,128)(2,1)S(1)} custom-call(s16[128,256]{1,0:T(8,128)(2,1)S(1)} %collective-permute-done.theirs.seed_ref.refs_1_), custom_call_target="tpu_custom_call" | custom-call | flops 8388608 | bytes 2097152 | tf_op jit(solution)/shard_map/signs/pallas_call | solution.py:301
  19.0 0.2 collective-permute-done.3.refs_4_
  19.2 0.0 copy-done.1
  19.2 3.2 %partial_scores.1 = (f32[32,128]{1,0:T(8,128)S(1)}, f32[32,128]{1,0:T(8,128)S(1)}) custom-call(s16[128,256]{1,0:T(8,128)(2,1)S(1)} %pool.1.mine.refs_0_, s16[128,256]{1,0:T(8,128)(2,1)S(1)} %collective-permute-done.theirs.seed_ref.refs_1_, s16[2,80,256]{2,1,0:T(8,128)(2,1)S(1)} %collective-permute-done.1.refs_0_.refs_2_, ...), custom_call_target="tpu_custom_call" | custom-call | flops 2415919104 | bytes 8388608 | tf_op jit(solution)/shard_map/partial_scores/pallas_call | solution.py:413
  22.4 0.4 %collective-permute-start.4 = (f32[32,128]{1,0:T(8,128)S(1)}, f32[32,128]{1,0:T(8,128)S(1)}, u32[]{:S(2)}, u32[]{:S(2)}) collective-permute-start(f32[32,128]{1,0:T(8,128)S(1)} %get-tuple-element.24), channel_id=1, source_target_pairs={{0,1},{1,0},{2,3},{3,2},{4,5},{5,4},{6,7},{7,6},{8,9},{9,8},{10,11... | collective-permute-start | bytes 49160 | tf_op jit(solution)/shard_map/ppermute | solution.py:486
  22.7 0.9 %collective-permute-done.4 = f32[32,128]{1,0:T(8,128)S(1)} collective-permute-done((f32[32,128]{1,0:T(8,128)S(1)}, f32[32,128]{1,0:T(8,128)S(1)}, u32[]{:S(2)}, u32[]{:S(2)}) %collective-permute-start.4) | collective-permute-done | bytes 16416 | tf_op jit(solution)/shard_map/ppermute | solution.py:486
  23.6 0.6 %add_multiply_fusion = f32[32,128]{1,0:T(8,128)} fusion(f32[32,128]{1,0:T(8,128)S(1)} %get-tuple-element.23, f32[32,128]{1,0:T(8,128)S(1)} %collective-permute-done.4), kind=kLoop, calls=%fused_computation | loop fusion | flops 8192 | bytes 49152 | tf_op jit(solution)/shard_map/mul | solution.py:487
  (2 shorter events, 0.0 us)
Async XLA Ops:
  0.0 7.7 %copy-start = (s32[2048]{0:T(1024)S(1)}, s32[2048]{0:T(1024)}, u32[]{:S(2)}) copy-start(s32[2048]{0:T(1024)} %param.16) | copy-start | bytes 24580
  7.2 1.7 %collective-permute-start = (s16[128,256]{1,0:T(8,128)(2,1)S(1)}, s16[128,256]{1,0:T(8,128)(2,1)S(1)}, u32[]{:S(2)}, u32[]{:S(2)}) collective-permute-start(s16[128,256]{1,0:T(8,128)(2,1)S(1)} %pool.1.mine.refs_0_), channel_id=1, source_target_pairs={{0,1},{1,0},{2,3},{3,2},{4,5},{5,4},{6,7},{7,6},{8,9},{9,8},{10,11... | collective-permute-start | bytes 196616 | tf_op jit(solution)/shard_map/ppermute | solution.py:463
  9.0 8.8 %collective-permute-start.1 = (s16[2,80,256]{2,1,0:T(8,128)(2,1)S(1)}, s16[2,80,256]{2,1,0:T(8,128)(2,1)S(1)}, u32[]{:S(2)}, u32[]{:S(2)}) collective-permute-start(s16[2,80,256]{2,1,0:T(8,128)(2,1)S(1)} %get-tuple-element.16), channel_id=1, source_target_pairs={{0,8},{1,13},{2,10},{3,15},{4,12},{5,9},{6,14},{7,11},{8,0},{9,5},... | collective-permute-start | bytes 245768 | tf_op jit(solution)/shard_map/ppermute | solution.py:477
  12.6 5.1 %collective-permute-start.2 = (s16[2,80,256]{2,1,0:T(8,128)(2,1)S(1)}, s16[2,80,256]{2,1,0:T(8,128)(2,1)S(1)}, u32[]{:S(2)}, u32[]{:S(2)}) collective-permute-start(s16[2,80,256]{2,1,0:T(8,128)(2,1)S(1)} %get-tuple-element.17), channel_id=1, source_target_pairs={{0,2},{1,5},{2,0},{3,7},{4,6},{5,1},{6,4},{7,3},{8,10},{9,13},{10,... | collective-permute-start | bytes 245768 | tf_op jit(solution)/shard_map/ppermute | solution.py:477
  15.3 3.9 %copy-start.1 = (f32[2048]{0:T(1024)S(1)}, f32[2048]{0:T(1024)}, u32[]{:S(2)}) copy-start(f32[2048]{0:T(1024)} %param.17) | copy-start | bytes 24580
  17.8 1.5 %collective-permute-start.3 = (s16[320,256]{1,0:T(8,128)(2,1)S(1)}, s16[320,256]{1,0:T(8,128)(2,1)S(1)}, u32[]{:S(2)}, u32[]{:S(2)}) collective-permute-start(s16[320,256]{1,0:T(8,128)(2,1)S(1)} %join.1), channel_id=1, source_target_pairs={{0,1},{1,0},{2,3},{3,2},{4,5},{5,4},{6,7},{7,6},{8,9},{9,8},{10,11... | collective-permute-start | bytes 491528 | tf_op jit(solution)/shard_map/ppermute | solution.py:481
  22.4 1.2 %collective-permute-start.4 = (f32[32,128]{1,0:T(8,128)S(1)}, f32[32,128]{1,0:T(8,128)S(1)}, u32[]{:S(2)}, u32[]{:S(2)}) collective-permute-start(f32[32,128]{1,0:T(8,128)S(1)} %get-tuple-element.24), channel_id=1, source_target_pairs={{0,1},{1,0},{2,3},{3,2},{4,5},{5,4},{6,7},{7,6},{8,9},{9,8},{10,11... | collective-permute-start | bytes 49160 | tf_op jit(solution)/shard_map/ppermute | solution.py:486

commit v8 on v7

--- a/solution.py
+++ b/solution.py
@@ -17,7 +17,8 @@
 MIX_LAST = (1274126177 << 15) & 0xFFFFFFFF
 MIX_LAST = MIX_LAST - (1 << 32) if MIX_LAST >= 1 << 31 else MIX_LAST
 MIB = 2**20
-AHEAD = 3
+AHEAD = 2
+PART = 64
 
 VMEM = pl.BlockSpec(memory_space=pltpu.VMEM)
 HBM = pl.BlockSpec(memory_space=pltpu.HBM)
@@ -70,23 +71,19 @@
     low = jnp.round((scaled - high) * 16384.0)
     row = lax.broadcasted_iota(jnp.int32, (NCLS, count), 0)
     facts = jnp.where(row == 0, labels, jnp.where(row == 3, logit_exponent, turned))
-    blank = jnp.zeros((NCLS, 128 - count), jnp.float32)
-    extra = jnp.concatenate(
-        [
-            jnp.concatenate([high, blank, facts, blank], axis=1),
-            jnp.concatenate([low, blank, jnp.zeros((NCLS, 128), jnp.float32)], axis=1),
-        ],
-        axis=0,
-    )
-    packet[pl.ds(at + count, 2 * NCLS), :] = extra.astype(jnp.int32).astype(jnp.int16)
+    blank = jnp.zeros((NCLS, PART - count), jnp.float32)
+    pieces = [value for part in (high, low, facts) for value in ((part, blank) if count < PART else (part,))]
+    pieces.append(jnp.zeros((NCLS, pooled.shape[1] - 3 * PART), jnp.float32))
+    return jnp.concatenate(pieces, axis=1).astype(jnp.int32)
 
 
 def decode_packet(packet):
-    count = packet.shape[0] - 2 * NCLS
+    count = packet.shape[0] - NCLS
     extra = packet[count:]
-    facts = extra[:NCLS, 128:]
+    facts = extra[:, 128:]
     step = facts[1:2] * (power_of_two(facts[2:3]) * (1.0 / (8192.0 * 32767.0)))
-    logits = (extra[:NCLS, :128] + extra[NCLS:, :128] * (1.0 / 16384.0)) * (
+    high = extra[:, :128]
+    logits = (high + pltpu.roll(high, PART, 1) * (1.0 / 16384.0)) * (
         power_of_two(facts[3:4]) * (1.0 / 8192.0)
     )
     return packet[:count], step, logits, facts[0:1]
@@ -181,7 +178,7 @@
         return carry
 
     lax.fori_loop(0, blocks, one_block, 0)
-    at = 0
+    extra = []
     for label_ref, start, count in ((train_label, 0, train_count), (test_label, train_count, test_count)):
         own = pooled[pl.ds(start, count), :]
         logits = lax.dot_general(
@@ -192,8 +189,10 @@
             preferred_element_type=jnp.float32,
         )
         labels = jnp.broadcast_to(label_ref[...].astype(jnp.float32), (NCLS, count))
-        encode_packet(packet, at, own, logits, labels)
-        at += count + 2 * NCLS
+        extra.append(encode_packet(packet, start, own, logits, labels))
+    at = train_count + test_count
+    packet[pl.ds(at, 2 * NCLS), :] = jnp.concatenate(extra, axis=0).astype(jnp.int16)
+    at += 2 * NCLS
     packet[pl.ds(at, seeds.shape[0]), pl.ds(0, 128)] = (seeds[...] >> 15).astype(jnp.int16)
     packet[pl.ds(at, seeds.shape[0]), pl.ds(128, 128)] = (seeds[...] & 32767).astype(jnp.int16)
 
@@ -206,7 +205,7 @@
     total = train_count + test_count
     return pl.pallas_call(
         functools.partial(pool_kernel, block),
-        out_shape=jax.ShapeDtypeStruct((total + 4 * NCLS + seeds.shape[0], half), jnp.int16),
+        out_shape=jax.ShapeDtypeStruct((total + 2 * NCLS + seeds.shape[0], half), jnp.int16),
         in_specs=[HBM] * 8,
         out_specs=VMEM,
         scratch_shapes=[
@@ -238,23 +237,25 @@
     return [(shifts[i + 1], shifts[i]) for i in range(0, len(shifts), 2)]
 
 
-def pack_kernel(kinds, train_rows, test_rows, mine, theirs, *outs):
+def pack_kernel(kinds, train_count, test_count, mine, theirs, *outs):
     proj_index = lax.axis_index("proj")
     for pair, out in zip(kinds, outs):
         for core, kind in enumerate(pair):
 
             @pl.when(proj_index == core)
             def _():
-                start, count = (0, train_rows) if kind == "train" else (train_rows, test_rows)
+                start, count = (0, train_count) if kind == "train" else (train_count, test_count)
+                extra = train_count + test_count + (0 if kind == "train" else NCLS)
                 for side, packet in enumerate((mine, theirs)):
                     out[side, pl.ds(0, count), :] = packet[pl.ds(start, count), :]
-
-
-def pack(kinds, train_rows, test_rows, mine, theirs):
+                    out[side, pl.ds(count, NCLS), :] = packet[pl.ds(extra, NCLS), :]
+
+
+def pack(kinds, train_count, test_count, mine, theirs):
     width = mine.shape[1]
-    rows = [train_rows if "train" in pair else test_rows for pair in kinds]
+    rows = [(train_count if "train" in pair else test_count) + NCLS for pair in kinds]
     return pl.pallas_call(
-        functools.partial(pack_kernel, kinds, train_rows, test_rows),
+        functools.partial(pack_kernel, kinds, train_count, test_count),
         out_shape=tuple(jax.ShapeDtypeStruct((2, count, width), jnp.int16) for count in rows),
         in_specs=[VMEM, VMEM],
         out_specs=(VMEM,) * len(kinds),
@@ -321,18 +322,21 @@
     parts, _, part_width = signs[0].shape
     train_rows = train_blocks * train_count
     blocks = {"train": [], "test": []}
-    for kind, first, count in (
-        ("train", 0, train_count),
-        ("test", train_count + 2 * NCLS, test_count),
+    for kind, first, count, extra in (
+        ("train", 0, train_count, train_count + test_count),
+        ("test", train_count, test_count, train_count + test_count + NCLS),
     ):
-        rows = pl.ds(first, count + 2 * NCLS)
-        blocks[kind].append((0, [as_float(packet[rows, :]) for packet in packets[:2]]))
+        own = [
+            as_float(jnp.concatenate([packet[pl.ds(first, count), :], packet[pl.ds(extra, NCLS), :]], axis=0))
+            for packet in packets[:2]
+        ]
+        blocks[kind].append((0, own))
     swapped = packets[-1]
     base = 0
     for i, pair in enumerate(steps):
         direct = packets[i + 2]
         for core, (kind, shift) in enumerate(pair):
-            size = (train_count if kind == "train" else test_count) + 2 * NCLS
+            size = (train_count if kind == "train" else test_count) + NCLS
             blocks[kind].append(
                 (
                     shift,
@@ -464,7 +468,7 @@
     signs = [sign_block(seeds, channels, count, halves[0])]
     other_packet, signs[0] = lax.optimization_barrier((other_packet, signs[0]))
     kinds = list(dict.fromkeys((a, b) for (a, _), (b, _) in steps))
-    packed = pack(kinds, train_count + 2 * NCLS, test_count + 2 * NCLS, packet, other_packet)
+    packed = pack(kinds, train_count, test_count, packet, other_packet)
     far = []
     for pair in steps:
         moves = []

time: 24.3 us -> 23.8 us (0.979)
  waiting for transfers between devices: 2.26 us -> 1.88 us
    ppermute x2, waiting for transfers between devices: 1.22 us -> 0.88 us  [shards(): far.append(lax.ppermute(value, ('train', 'test', 'proj'), moves))]
where the time goes in v8:
time: 23.8 us; the launch traced here: 23.7 us
  Pallas kernels  15 us (63%)
  starting transfers between devices  6.13 us (26%)
  waiting for transfers between devices  1.88 us (8%)
  other arithmetic  0.61 us (3%)
    pallas_call x1, Pallas kernels, pool(): pl.pallas_call(functools.partial(pool_kernel, block), out_shape=jax.Shape...  6.97 us
    ppermute x2, starting transfers between devices, shards(): far.append(lax.ppermute(value, ('train', 'test', 'proj'), moves))  5.14 us
    pallas_call x4, Pallas kernels, sign_block(): pl.pallas_call(functools.partial(sign_kernel, seeds.dtype == jnp.int16, c...  4.75 us
    pallas_call x1, Pallas kernels, partial_scores(): pl.pallas_call(functools.partial(score_kernel, train_blocks, test_blocks,...  3.22 us
    ppermute x2, waiting for transfers between devices, shards(): far.append(lax.ppermute(value, ('train', 'test', 'proj'), moves))  0.88 us
    ppermute x1, waiting for transfers between devices, shards(): received = lax.ppermute(send, 'proj', swap)  0.84 us
    mul x1, other arithmetic, shards(): return (keep + received) * (1.0 / (K * math.sqrt(C)))  0.61 us
    ppermute x1, starting transfers between devices, shards(): other_packet = lax.ppermute(packet, 'proj', swap)  0.54 us
  transfers between devices with their start and end apart: 5, of which 3 were waited for; matrix products, arithmetic and copies ran while one was open for 0% of the time, Pallas kernels for 20%

profile of v8, /device:TPU:0, one launch (start us, length us, event | category | flops | bytes accessed | tf_op | source)
XLA Modules:
  0.0 23.7 jit_solution(2828171069078432041)
XLA Ops:
  0.0 0.0 copy-start
  0.0 7.0 %pool.1.mine.refs_0_ = s16[112,256]{1,0:T(8,128)(2,1)S(1)} custom-call(bf16[64,64,512]{2,1,0:T(8,128)(2,1)} %train_hbm.1, bf16[16,64,512]{2,1,0:T(8,128)(2,1)} %test_hbm.1, bf16[3,512,256]{2,1,0:T(8,128)(2,1)} %weight_hbm.1, f32[1,256]{1,0:T(1,128)} %bitcast.11, f32[8,256]{1,0:T(8,128)} %bitcast.10, s32[1,64]{1,0:T(1,128)} %bitcast.12, s32[1,16]{1,0:T(1,128)} %bitcast.13, ...), custom_call_target="tpu_custom_call" | custom-call | tf_op jit(solution)/shard_map/pool/pallas_call | solution.py:206
  7.0 0.5 %collective-permute-start = (s16[112,256]{1,0:T(8,128)(2,1)S(1)}, s16[112,256]{1,0:T(8,128)(2,1)S(1)}, u32[]{:S(2)}, u32[]{:S(2)}) collective-permute-start(s16[112,256]{1,0:T(8,128)(2,1)S(1)} %pool.1.mine.refs_0_), channel_id=1, source_target_pairs={{0,1},{1,0},{2,3},{3,2},{4,5},{5,4},{6,7},{7,6},{8,9},{9,8},{10,11... | collective-permute-start | bytes 172040 | tf_op jit(solution)/shard_map/ppermute | solution.py:467
  7.5 0.0 copy-done
  7.5 1.2 %signs.4.refs_5_ = bf16[4,1024,256]{2,1,0:T(8,128)(2,1)S(1)} custom-call(s32[16,128]{1,0:T(8,128)S(1)} %bitcast.7), custom_call_target="tpu_custom_call" | custom-call | flops 8388608 | bytes 2097152 | tf_op jit(solution)/shard_map/signs/pallas_call | solution.py:302
  8.7 0.0 collective-permute-done.theirs.seed_ref.refs_1_
  8.8 3.7 %collective-permute-start.1 = (s16[2,72,256]{2,1,0:T(8,128)(2,1)S(1)}, s16[2,72,256]{2,1,0:T(8,128)(2,1)S(1)}, u32[]{:S(2)}, u32[]{:S(2)}) collective-permute-start(s16[2,72,256]{2,1,0:T(8,128)(2,1)S(1)} %get-tuple-element.16), channel_id=1, source_target_pairs={{0,8},{1,13},{2,10},{3,15},{4,12},{5,9},{6,14},{7,11},{8,0},{9,5},... | collective-permute-start | bytes 221192 | tf_op jit(solution)/shard_map/ppermute | solution.py:481
  12.4 1.5 %collective-permute-start.2 = (s16[2,72,256]{2,1,0:T(8,128)(2,1)S(1)}, s16[2,72,256]{2,1,0:T(8,128)(2,1)S(1)}, u32[]{:S(2)}, u32[]{:S(2)}) collective-permute-start(s16[2,72,256]{2,1,0:T(8,128)(2,1)S(1)} %get-tuple-element.17), channel_id=1, source_target_pairs={{0,2},{1,5},{2,0},{3,7},{4,6},{5,1},{6,4},{7,3},{8,10},{9,13},{10,... | collective-permute-start | bytes 221192 | tf_op jit(solution)/shard_map/ppermute | solution.py:481
  13.9 1.2 %signs.5.refs_6_ = bf16[4,1024,256]{2,1,0:T(8,128)(2,1)S(1)} custom-call(s32[16,128]{1,0:T(8,128)S(1)} %bitcast.8), custom_call_target="tpu_custom_call" | custom-call | flops 8388608 | bytes 2097152 | tf_op jit(solution)/shard_map/signs/pallas_call | solution.py:302
  15.1 0.0 copy-start.1
  15.1 1.2 %signs.6.refs_7_ = bf16[4,1024,256]{2,1,0:T(8,128)(2,1)S(1)} custom-call(s16[112,256]{1,0:T(8,128)(2,1)S(1)} %collective-permute-done.theirs.seed_ref.refs_1_), custom_call_target="tpu_custom_call" | custom-call | flops 8388608 | bytes 2097152 | tf_op jit(solution)/shard_map/signs/pallas_call | solution.py:302
  16.3 0.9 %collective-permute-done.1.refs_0_.refs_2_ = s16[2,72,256]{2,1,0:T(8,128)(2,1)S(1)} collective-permute-done((s16[2,72,256]{2,1,0:T(8,128)(2,1)S(1)}, s16[2,72,256]{2,1,0:T(8,128)(2,1)S(1)}, u32[]{:S(2)}, u32[]{:S(2)}) %collective-permute-start.1) | collective-permute-done | bytes 73760 | tf_op jit(solution)/shard_map/ppermute | solution.py:481
  17.2 0.0 collective-permute-done.2.refs_1_.refs_3_
  17.2 0.1 collective-permute-start.3
  17.3 1.2 %signs.7.refs_8_ = bf16[4,1024,256]{2,1,0:T(8,128)(2,1)S(1)} custom-call(s16[112,256]{1,0:T(8,128)(2,1)S(1)} %collective-permute-done.theirs.seed_ref.refs_1_), custom_call_target="tpu_custom_call" | custom-call | flops 8388608 | bytes 2097152 | tf_op jit(solution)/shard_map/signs/pallas_call | solution.py:302
  18.5 0.2 collective-permute-done.3.refs_4_
  18.6 0.0 copy-done.1
  18.6 3.2 %partial_scores.1 = (f32[32,128]{1,0:T(8,128)S(1)}, f32[32,128]{1,0:T(8,128)S(1)}) custom-call(s16[112,256]{1,0:T(8,128)(2,1)S(1)} %pool.1.mine.refs_0_, s16[112,256]{1,0:T(8,128)(2,1)S(1)} %collective-permute-done.theirs.seed_ref.refs_1_, s16[2,72,256]{2,1,0:T(8,128)(2,1)S(1)} %collective-permute-done.1.refs_0_.refs_2_, ...), custom_call_target="tpu_custom_call" | custom-call | flops 2415919104 | bytes 8388608 | tf_op jit(solution)/shard_map/partial_scores/pallas_call | solution.py:417
  21.8 0.4 %collective-permute-start.4 = (f32[32,128]{1,0:T(8,128)S(1)}, f32[32,128]{1,0:T(8,128)S(1)}, u32[]{:S(2)}, u32[]{:S(2)}) collective-permute-start(f32[32,128]{1,0:T(8,128)S(1)} %get-tuple-element.24), channel_id=1, source_target_pairs={{0,1},{1,0},{2,3},{3,2},{4,5},{5,4},{6,7},{7,6},{8,9},{9,8},{10,11... | collective-permute-start | bytes 49160 | tf_op jit(solution)/shard_map/ppermute | solution.py:490
  22.2 0.8 %collective-permute-done.4 = f32[32,128]{1,0:T(8,128)S(1)} collective-permute-done((f32[32,128]{1,0:T(8,128)S(1)}, f32[32,128]{1,0:T(8,128)S(1)}, u32[]{:S(2)}, u32[]{:S(2)}) %collective-permute-start.4) | collective-permute-done | bytes 16416 | tf_op jit(solution)/shard_map/ppermute | solution.py:490
  23.1 0.6 %add_multiply_fusion = f32[32,128]{1,0:T(8,128)} fusion(f32[32,128]{1,0:T(8,128)S(1)} %get-tuple-element.23, f32[32,128]{1,0:T(8,128)S(1)} %collective-permute-done.4), kind=kLoop, calls=%fused_computation | loop fusion | flops 8192 | bytes 49152 | tf_op jit(solution)/shard_map/mul | solution.py:491
  (2 shorter events, 0.0 us)
Async XLA Ops:
  0.0 7.5 %copy-start = (s32[2048]{0:T(1024)S(1)}, s32[2048]{0:T(1024)}, u32[]{:S(2)}) copy-start(s32[2048]{0:T(1024)} %param.16) | copy-start | bytes 24580
  7.0 1.7 %collective-permute-start = (s16[112,256]{1,0:T(8,128)(2,1)S(1)}, s16[112,256]{1,0:T(8,128)(2,1)S(1)}, u32[]{:S(2)}, u32[]{:S(2)}) collective-permute-start(s16[112,256]{1,0:T(8,128)(2,1)S(1)} %pool.1.mine.refs_0_), channel_id=1, source_target_pairs={{0,1},{1,0},{2,3},{3,2},{4,5},{5,4},{6,7},{7,6},{8,9},{9,8},{10,11... | collective-permute-start | bytes 172040 | tf_op jit(solution)/shard_map/ppermute | solution.py:467
  8.8 8.4 %collective-permute-start.1 = (s16[2,72,256]{2,1,0:T(8,128)(2,1)S(1)}, s16[2,72,256]{2,1,0:T(8,128)(2,1)S(1)}, u32[]{:S(2)}, u32[]{:S(2)}) collective-permute-start(s16[2,72,256]{2,1,0:T(8,128)(2,1)S(1)} %get-tuple-element.16), channel_id=1, source_target_pairs={{0,8},{1,13},{2,10},{3,15},{4,12},{5,9},{6,14},{7,11},{8,0},{9,5},... | collective-permute-start | bytes 221192 | tf_op jit(solution)/shard_map/ppermute | solution.py:481
  12.4 4.8 %collective-permute-start.2 = (s16[2,72,256]{2,1,0:T(8,128)(2,1)S(1)}, s16[2,72,256]{2,1,0:T(8,128)(2,1)S(1)}, u32[]{:S(2)}, u32[]{:S(2)}) collective-permute-start(s16[2,72,256]{2,1,0:T(8,128)(2,1)S(1)} %get-tuple-element.17), channel_id=1, source_target_pairs={{0,2},{1,5},{2,0},{3,7},{4,6},{5,1},{6,4},{7,3},{8,10},{9,13},{10,... | collective-permute-start | bytes 221192 | tf_op jit(solution)/shard_map/ppermute | solution.py:481
  15.1 3.5 %copy-start.1 = (f32[2048]{0:T(1024)S(1)}, f32[2048]{0:T(1024)}, u32[]{:S(2)}) copy-start(f32[2048]{0:T(1024)} %param.17) | copy-start | bytes 24580
  17.2 1.4 %collective-permute-start.3 = (s16[288,256]{1,0:T(8,128)(2,1)S(1)}, s16[288,256]{1,0:T(8,128)(2,1)S(1)}, u32[]{:S(2)}, u32[]{:S(2)}) collective-permute-start(s16[288,256]{1,0:T(8,128)(2,1)S(1)} %join.1), channel_id=1, source_target_pairs={{0,1},{1,0},{2,3},{3,2},{4,5},{5,4},{6,7},{7,6},{8,9},{9,8},{10,11... | collective-permute-start | bytes 442376 | tf_op jit(solution)/shard_map/ppermute | solution.py:485
  21.8 1.2 %collective-permute-start.4 = (f32[32,128]{1,0:T(8,128)S(1)}, f32[32,128]{1,0:T(8,128)S(1)}, u32[]{:S(2)}, u32[]{:S(2)}) collective-permute-start(f32[32,128]{1,0:T(8,128)S(1)} %get-tuple-element.24), channel_id=1, source_target_pairs={{0,1},{1,0},{2,3},{3,2},{4,5},{5,4},{6,7},{7,6},{8,9},{9,8},{10,11... | collective-permute-start | bytes 49160 | tf_op jit(solution)/shard_map/ppermute | solution.py:490

commit v9 on v8

--- a/solution.py
+++ b/solution.py
@@ -465,7 +465,7 @@
     halves = (tuple(range(NCLS // 2)), tuple(range(NCLS // 2, NCLS)))
     steps = transfer_steps(train_blocks, test_blocks)
     other_packet = lax.ppermute(packet, "proj", swap)
-    signs = [sign_block(seeds, channels, count, halves[0])]
+    signs = [sign_block(seeds, channels, count, tuple(range(3)))]
     other_packet, signs[0] = lax.optimization_barrier((other_packet, signs[0]))
     kinds = list(dict.fromkeys((a, b) for (a, _), (b, _) in steps))
     packed = pack(kinds, train_count, test_count, packet, other_packet)
@@ -479,7 +479,7 @@
             moves.append((source, source ^ (shift * scale)))
         value = packed[kinds.index((pair[0][0], pair[1][0]))]
         far.append(lax.ppermute(value, ("train", "test", "proj"), moves))
-    signs.append(sign_block(seeds, channels, count, halves[1]))
+    signs.append(sign_block(seeds, channels, count, tuple(range(3, NCLS))))
     signs.append(sign_block(other_packet, channels, count, halves[0]))
     *far, signs[1], signs[2] = lax.optimization_barrier((*far, signs[1], signs[2]))
     packets = [packet, other_packet, *far, lax.ppermute(join(far), "proj", swap)]

time: 23.8 us -> 23.4 us (0.983)
  waiting for transfers between devices: 1.88 us -> 1.12 us
  starting transfers between devices: 6.13 us -> 6.5 us
    ppermute x2, waiting for transfers between devices: 0.88 us -> 0.24 us  [shards(): far.append(lax.ppermute(value, ('train', 'test', 'proj'), moves))]
    ppermute x2, starting transfers between devices: 5.14 us -> 5.4 us  [shards(): far.append(lax.ppermute(value, ('train', 'test', 'proj'), moves))]
  transfers between devices with their start and end apart: 5 -> 5, of which waited for: 3 -> 2; matrix products, arithmetic and copies ran while one was open for 0% -> 0% of each run, Pallas kernels for 20% -> 20%
where the time goes in v9:
time: 23.4 us; the launch traced here: 23.3 us
  Pallas kernels  15 us (64%)
  starting transfers between devices  6.5 us (28%)
  waiting for transfers between devices  1.12 us (5%)
  other arithmetic  0.61 us (3%)
    pallas_call x1, Pallas kernels, pool(): pl.pallas_call(functools.partial(pool_kernel, block), out_shape=jax.Shape...  6.97 us
    ppermute x2, starting transfers between devices, shards(): far.append(lax.ppermute(value, ('train', 'test', 'proj'), moves))  5.4 us
    pallas_call x4, Pallas kernels, sign_block(): pl.pallas_call(functools.partial(sign_kernel, seeds.dtype == jnp.int16, c...  4.75 us
    pallas_call x1, Pallas kernels, partial_scores(): pl.pallas_call(functools.partial(score_kernel, train_blocks, test_blocks,...  3.22 us
    ppermute x1, waiting for transfers between devices, shards(): received = lax.ppermute(send, 'proj', swap)  0.84 us
    mul x1, other arithmetic, shards(): return (keep + received) * (1.0 / (K * math.sqrt(C)))  0.61 us
    ppermute x1, starting transfers between devices, shards(): other_packet = lax.ppermute(packet, 'proj', swap)  0.54 us
  transfers between devices with their start and end apart: 5, of which 2 were waited for; matrix products, arithmetic and copies ran while one was open for 0% of the time, Pallas kernels for 20%

profile of v9, /device:TPU:0, one launch (start us, length us, event | category | flops | bytes accessed | tf_op | source)
XLA Modules:
  0.0 23.3 jit_solution(15369345738931613912)
XLA Ops:
  0.0 0.0 copy-start
  0.0 7.0 %pool.1.mine.refs_0_ = s16[112,256]{1,0:T(8,128)(2,1)S(1)} custom-call(bf16[64,64,512]{2,1,0:T(8,128)(2,1)} %train_hbm.1, bf16[16,64,512]{2,1,0:T(8,128)(2,1)} %test_hbm.1, bf16[3,512,256]{2,1,0:T(8,128)(2,1)} %weight_hbm.1, f32[1,256]{1,0:T(1,128)} %bitcast.11, f32[8,256]{1,0:T(8,128)} %bitcast.10, s32[1,64]{1,0:T(1,128)} %bitcast.12, s32[1,16]{1,0:T(1,128)} %bitcast.13, ...), custom_call_target="tpu_custom_call" | custom-call | tf_op jit(solution)/shard_map/pool/pallas_call | solution.py:206
  7.0 0.5 %collective-permute-start = (s16[112,256]{1,0:T(8,128)(2,1)S(1)}, s16[112,256]{1,0:T(8,128)(2,1)S(1)}, u32[]{:S(2)}, u32[]{:S(2)}) collective-permute-start(s16[112,256]{1,0:T(8,128)(2,1)S(1)} %pool.1.mine.refs_0_), channel_id=1, source_target_pairs={{0,1},{1,0},{2,3},{3,2},{4,5},{5,4},{6,7},{7,6},{8,9},{9,8},{10,11... | collective-permute-start | bytes 172040 | tf_op jit(solution)/shard_map/ppermute | solution.py:467
  7.5 0.0 copy-done
  7.5 0.9 %signs.4.refs_5_ = bf16[4,768,256]{2,1,0:T(8,128)(2,1)S(1)} custom-call(s32[16,128]{1,0:T(8,128)S(1)} %bitcast.7), custom_call_target="tpu_custom_call" | custom-call | flops 6291456 | bytes 1572864 | tf_op jit(solution)/shard_map/signs/pallas_call | solution.py:302
  8.5 0.0 collective-permute-done.theirs.seed_ref.refs_1_
  8.5 3.9 %collective-permute-start.1 = (s16[2,72,256]{2,1,0:T(8,128)(2,1)S(1)}, s16[2,72,256]{2,1,0:T(8,128)(2,1)S(1)}, u32[]{:S(2)}, u32[]{:S(2)}) collective-permute-start(s16[2,72,256]{2,1,0:T(8,128)(2,1)S(1)} %get-tuple-element.16), channel_id=1, source_target_pairs={{0,8},{1,13},{2,10},{3,15},{4,12},{5,9},{6,14},{7,11},{8,0},{9,5},... | collective-permute-start | bytes 221192 | tf_op jit(solution)/shard_map/ppermute | solution.py:481
  12.4 1.5 %collective-permute-start.2 = (s16[2,72,256]{2,1,0:T(8,128)(2,1)S(1)}, s16[2,72,256]{2,1,0:T(8,128)(2,1)S(1)}, u32[]{:S(2)}, u32[]{:S(2)}) collective-permute-start(s16[2,72,256]{2,1,0:T(8,128)(2,1)S(1)} %get-tuple-element.17), channel_id=1, source_target_pairs={{0,2},{1,5},{2,0},{3,7},{4,6},{5,1},{6,4},{7,3},{8,10},{9,13},{10,... | collective-permute-start | bytes 221192 | tf_op jit(solution)/shard_map/ppermute | solution.py:481
  13.9 1.4 %signs.5.refs_6_ = bf16[4,1280,256]{2,1,0:T(8,128)(2,1)S(1)} custom-call(s32[16,128]{1,0:T(8,128)S(1)} %bitcast.8), custom_call_target="tpu_custom_call" | custom-call | flops 10485760 | bytes 2621440 | tf_op jit(solution)/shard_map/signs/pallas_call | solution.py:302
  15.3 0.0 copy-start.1
  15.4 1.2 %signs.6.refs_7_ = bf16[4,1024,256]{2,1,0:T(8,128)(2,1)S(1)} custom-call(s16[112,256]{1,0:T(8,128)(2,1)S(1)} %collective-permute-done.theirs.seed_ref.refs_1_), custom_call_target="tpu_custom_call" | custom-call | flops 8388608 | bytes 2097152 | tf_op jit(solution)/shard_map/signs/pallas_call | solution.py:302
  16.6 0.2 %collective-permute-done.1.refs_0_.refs_2_ = s16[2,72,256]{2,1,0:T(8,128)(2,1)S(1)} collective-permute-done((s16[2,72,256]{2,1,0:T(8,128)(2,1)S(1)}, s16[2,72,256]{2,1,0:T(8,128)(2,1)S(1)}, u32[]{:S(2)}, u32[]{:S(2)}) %collective-permute-start.1) | collective-permute-done | bytes 73760 | tf_op jit(solution)/shard_map/ppermute | solution.py:481
  16.8 0.0 collective-permute-done.2.refs_1_.refs_3_
  16.8 0.2 collective-permute-start.3
  17.0 1.2 %signs.7.refs_8_ = bf16[4,1024,256]{2,1,0:T(8,128)(2,1)S(1)} custom-call(s16[112,256]{1,0:T(8,128)(2,1)S(1)} %collective-permute-done.theirs.seed_ref.refs_1_), custom_call_target="tpu_custom_call" | custom-call | flops 8388608 | bytes 2097152 | tf_op jit(solution)/shard_map/signs/pallas_call | solution.py:302
  18.2 0.0 collective-permute-done.3.refs_4_
  18.2 0.0 copy-done.1
  18.3 3.2 %partial_scores.1 = (f32[32,128]{1,0:T(8,128)S(1)}, f32[32,128]{1,0:T(8,128)S(1)}) custom-call(s16[112,256]{1,0:T(8,128)(2,1)S(1)} %pool.1.mine.refs_0_, s16[112,256]{1,0:T(8,128)(2,1)S(1)} %collective-permute-done.theirs.seed_ref.refs_1_, s16[2,72,256]{2,1,0:T(8,128)(2,1)S(1)} %collective-permute-done.1.refs_0_.refs_2_, ...), custom_call_target="tpu_custom_call" | custom-call | flops 2415919104 | bytes 8388608 | tf_op jit(solution)/shard_map/partial_scores/pallas_call | solution.py:417
  21.5 0.4 %collective-permute-start.4 = (f32[32,128]{1,0:T(8,128)S(1)}, f32[32,128]{1,0:T(8,128)S(1)}, u32[]{:S(2)}, u32[]{:S(2)}) collective-permute-start(f32[32,128]{1,0:T(8,128)S(1)} %get-tuple-element.24), channel_id=1, source_target_pairs={{0,1},{1,0},{2,3},{3,2},{4,5},{5,4},{6,7},{7,6},{8,9},{9,8},{10,11... | collective-permute-start | bytes 49160 | tf_op jit(solution)/shard_map/ppermute | solution.py:490
  21.8 0.8 %collective-permute-done.4 = f32[32,128]{1,0:T(8,128)S(1)} collective-permute-done((f32[32,128]{1,0:T(8,128)S(1)}, f32[32,128]{1,0:T(8,128)S(1)}, u32[]{:S(2)}, u32[]{:S(2)}) %collective-permute-start.4) | collective-permute-done | bytes 16416 | tf_op jit(solution)/shard_map/ppermute | solution.py:490
  22.7 0.6 %add_multiply_fusion = f32[32,128]{1,0:T(8,128)} fusion(f32[32,128]{1,0:T(8,128)S(1)} %get-tuple-element.23, f32[32,128]{1,0:T(8,128)S(1)} %collective-permute-done.4), kind=kLoop, calls=%fused_computation | loop fusion | flops 8192 | bytes 49152 | tf_op jit(solution)/shard_map/mul | solution.py:491
  (2 shorter events, 0.0 us)
Async XLA Ops:
  0.0 7.5 %copy-start = (s32[2048]{0:T(1024)S(1)}, s32[2048]{0:T(1024)}, u32[]{:S(2)}) copy-start(s32[2048]{0:T(1024)} %param.16) | copy-start | bytes 24580
  7.0 1.5 %collective-permute-start = (s16[112,256]{1,0:T(8,128)(2,1)S(1)}, s16[112,256]{1,0:T(8,128)(2,1)S(1)}, u32[]{:S(2)}, u32[]{:S(2)}) collective-permute-start(s16[112,256]{1,0:T(8,128)(2,1)S(1)} %pool.1.mine.refs_0_), channel_id=1, source_target_pairs={{0,1},{1,0},{2,3},{3,2},{4,5},{5,4},{6,7},{7,6},{8,9},{9,8},{10,11... | collective-permute-start | bytes 172040 | tf_op jit(solution)/shard_map/ppermute | solution.py:467
  8.5 8.3 %collective-permute-start.1 = (s16[2,72,256]{2,1,0:T(8,128)(2,1)S(1)}, s16[2,72,256]{2,1,0:T(8,128)(2,1)S(1)}, u32[]{:S(2)}, u32[]{:S(2)}) collective-permute-start(s16[2,72,256]{2,1,0:T(8,128)(2,1)S(1)} %get-tuple-element.16), channel_id=1, source_target_pairs={{0,8},{1,13},{2,10},{3,15},{4,12},{5,9},{6,14},{7,11},{8,0},{9,5},... | collective-permute-start | bytes 221192 | tf_op jit(solution)/shard_map/ppermute | solution.py:481
  12.4 4.4 %collective-permute-start.2 = (s16[2,72,256]{2,1,0:T(8,128)(2,1)S(1)}, s16[2,72,256]{2,1,0:T(8,128)(2,1)S(1)}, u32[]{:S(2)}, u32[]{:S(2)}) collective-permute-start(s16[2,72,256]{2,1,0:T(8,128)(2,1)S(1)} %get-tuple-element.17), channel_id=1, source_target_pairs={{0,2},{1,5},{2,0},{3,7},{4,6},{5,1},{6,4},{7,3},{8,10},{9,13},{10,... | collective-permute-start | bytes 221192 | tf_op jit(solution)/shard_map/ppermute | solution.py:481
  15.3 2.9 %copy-start.1 = (f32[2048]{0:T(1024)S(1)}, f32[2048]{0:T(1024)}, u32[]{:S(2)}) copy-start(f32[2048]{0:T(1024)} %param.17) | copy-start | bytes 24580
  16.8 1.4 %collective-permute-start.3 = (s16[288,256]{1,0:T(8,128)(2,1)S(1)}, s16[288,256]{1,0:T(8,128)(2,1)S(1)}, u32[]{:S(2)}, u32[]{:S(2)}) collective-permute-start(s16[288,256]{1,0:T(8,128)(2,1)S(1)} %join.1), channel_id=1, source_target_pairs={{0,1},{1,0},{2,3},{3,2},{4,5},{5,4},{6,7},{7,6},{8,9},{9,8},{10,11... | collective-permute-start | bytes 442376 | tf_op jit(solution)/shard_map/ppermute | solution.py:485
  21.5 1.2 %collective-permute-start.4 = (f32[32,128]{1,0:T(8,128)S(1)}, f32[32,128]{1,0:T(8,128)S(1)}, u32[]{:S(2)}, u32[]{:S(2)}) collective-permute-start(f32[32,128]{1,0:T(8,128)S(1)} %get-tuple-element.24), channel_id=1, source_target_pairs={{0,1},{1,0},{2,3},{3,2},{4,5},{5,4},{6,7},{7,6},{8,9},{9,8},{10,11... | collective-permute-start | bytes 49160 | tf_op jit(solution)/shard_map/ppermute | solution.py:490
